TPU v7x, 256 devices: a whole 4x4x8 slice. The times are simulated.
256 devices in a mesh: seq: 16 (over z_lo, x), hid: 16 (over z_hi, y, core).
Axes of the slice: x: 4, y: 4, z: 8 (z_hi: 2, z_lo: 4; z = z_hi * 4 + z_lo), core: 2. Of those that a mesh axis runs over, the one named last changes fastest.
Arguments:
- tokens: bfloat16 [65536, 2048], P('seq', 'hid'), may hold values from -6 to 6
- cotangent: bfloat16 [65536, 2048], P('seq', 'hid'), may hold values from -6 to 6
- seq_first: bfloat16 [128, 512, 512], P('seq'), may hold values from -0.25 to 0.25
- seq_second: bfloat16 [512, 128, 128], P('seq'), may hold values from -0.5 to 0.5
- feat_first: bfloat16 [32, 64, 64], P('hid'), may hold values from -0.75 to 0.75
- feature_second_blocks: bfloat16 [64, 32, 32], P('hid'), may hold values from -1 to 1
- gate_scale: float32 [2048], P('hid'), may hold values from 0.5 to 2
- gate_bias: float32 [2048], P('hid'), may hold values from -3 to 3
Outputs:
- result: bfloat16 [65536, 2048], P('seq', 'hid')
- token_grad: bfloat16 [65536, 2048], P('seq', 'hid')
- first_grad: float32 [128, 512, 512], P('seq', 'hid')
- second_grad: float32 [512, 128, 128], P('seq', 'hid')
All inputs are finite; a program needn't handle non-finite values.
Results may differ from a plain program's by a relative error of at most 0.0061.
Values may be sent and summed in bfloat16 or wider, within the bound.
No kernel may reach another device: no remote copies, remote signals or barrier semaphores. Data moves between devices by JAX's collectives and lax.ppermute only.
A program may use at most 128 MiB of HBM per device.

v0:
```python
import jax
import jax.numpy as jnp
from jax import lax
from jax.sharding import PartitionSpec as P


def gelu_slope(value):
    normal_cdf = 0.5 * (1.0 + jax.scipy.special.erf(value * 0.7071067811865476))
    density = jnp.exp(-0.5 * value * value) * 0.3989422804014327
    return normal_cdf + value * density


def to_strided(value):
    return lax.all_to_all(value, "seq", split_axis=1, concat_axis=0, tiled=True)


def from_strided(value):
    return lax.all_to_all(value, "seq", split_axis=0, concat_axis=1, tiled=True)


def feat_regroup(value):
    return lax.all_to_all(value, "hid", split_axis=1, concat_axis=0, tiled=True)


def feat_restore(value):
    return lax.all_to_all(value, "hid", split_axis=0, concat_axis=1, tiled=True)


def grad_sums(first_term, second_term):
    return (
        lax.psum_scatter(first_term, "hid", scatter_dimension=1, tiled=True),
        lax.psum_scatter(second_term, "hid", scatter_dimension=1, tiled=True),
    )


def on_device(
    tokens,
    cotangent,
    seq_first,
    seq_second,
    feat_first,
    feature_second_blocks,
    gate_scale,
    gate_bias,
):
    widened_input = jnp.float32
    half = jnp.bfloat16
    rows, width = tokens.shape
    blocks_here, block = (seq_first.shape[0], seq_first.shape[1])
    groups_here, group = (feat_first.shape[0], feat_first.shape[1])
    x_blocks = tokens.reshape(blocks_here, block, width)
    first = jnp.einsum(
        "qkj,qjc->qkc", seq_first, x_blocks, preferred_element_type=widened_input
    ).astype(half)
    strided = to_strided(first)
    mixed_strided = jnp.einsum(
        "jab,bjc->ajc", seq_second, strided, preferred_element_type=widened_input
    ).astype(half)
    mixed = from_strided(mixed_strided).reshape(rows, width).astype(widened_input)
    x_wide = tokens.astype(widened_input)
    gate = jax.nn.sigmoid(x_wide * gate_scale + gate_bias)
    hidden_state = (x_wide + gate * mixed).astype(half)
    panels = hidden_state.reshape(rows, groups_here, group)
    inner = jnp.einsum(
        "bio,tbo->bit", feat_first, panels, preferred_element_type=widened_input
    ).astype(half)
    cot_panels = cotangent.reshape(rows, groups_here, group).transpose(1, 2, 0)
    inner_moved = feat_regroup(inner)
    activation_values = jax.nn.gelu(inner_moved.astype(widened_input), approximate=False).astype(
        half
    )
    outer_shifted = jnp.einsum(
        "whg,gwv->hwv",
        feature_second_blocks,
        activation_values,
        preferred_element_type=widened_input,
    ).astype(half)
    outer = feat_restore(outer_shifted).transpose(2, 0, 1).reshape(rows, width)
    result = (hidden_state.astype(widened_input) + outer.astype(widened_input)).astype(half)
    cotangent_shifted = feat_regroup(cot_panels)
    activation_gradient = jnp.einsum(
        "hec,ehz->chz",
        feature_second_blocks,
        cotangent_shifted,
        preferred_element_type=widened_input,
    )
    d_inner = (activation_gradient * gelu_slope(inner_moved.astype(widened_input))).astype(half)
    d_back = feat_restore(d_inner)
    d_hidden = cotangent.astype(widened_input) + jnp.einsum(
        "bio,bit->tbo", feat_first, d_back, preferred_element_type=widened_input
    ).reshape(rows, width)
    d_mixed = (d_hidden * gate).astype(half).reshape(blocks_here, block, width)
    d_mixed_moved = to_strided(d_mixed)
    d_first_moved = jnp.einsum(
        "jab,ajc->bjc", seq_second, d_mixed_moved, preferred_element_type=widened_input
    ).astype(half)
    second_term = jnp.einsum(
        "ajc,bjc->jab", d_mixed_moved, strided, preferred_element_type=widened_input
    )
    d_first = from_strided(d_first_moved)
    local_part = d_hidden * (1.0 + gate_scale * gate * (1.0 - gate) * mixed)
    seq_part = jnp.einsum(
        "qkj,qkc->qjc", seq_first, d_first, preferred_element_type=widened_input
    ).reshape(rows, width)
    first_term = jnp.einsum("qkc,qjc->qkj", d_first, x_blocks, preferred_element_type=widened_input)
    first_grad, second_grad = grad_sums(first_term, second_term)
    token_grad = (seq_part + local_part).astype(half)
    return (result, token_grad, first_grad, second_grad)


def solution(mesh):
    return jax.shard_map(
        on_device,
        mesh=mesh,
        in_specs=(
            P("seq", "hid"),
            P("seq", "hid"),
            P("seq", None, None),
            P("seq", None, None),
            P("hid", None, None),
            P("hid", None, None),
            P("hid"),
            P("hid"),
        ),
        out_specs=(P("seq", "hid"), P("seq", "hid"), P("seq", "hid", None), P("seq", "hid", None)),
        check_vma=False,
    )
```

profile of v0, /device:TPU:32, one launch (start us, length us, event | category | flops | bytes accessed | tf_op | source)
XLA Modules:
  0.0 480.9 jit_solution(9485754258786453972)
XLA Ops:
  7.2 3.8 convolution_convert_fusion.4
  11.7 34.3 %all_to_all.120 = bf16[8,512,128]{2,0,1:T(8,128)(2,1)S(1)} all-to-all(bf16[8,512,128]{2,0,1:T(8,128)(2,1)S(1)} %copy.103), channel_id=1, replica_groups=mesh['seq'=16,'hid'=16] {'seq'}, dimensions={1} | all-to-all | bytes 2097152 | tf_op jit(solution)/shard_map/all_to_all | solution.py:14
  49.8 5.1 %all-to-all-start.1 = ((bf16[128,32,128]{2,1,0:T(8,128)(2,1)}), bf16[128,32,128]{2,1,0:T(8,128)(2,1)S(1)}, u32[]{:S(2)}, u32[]{:S(2)}) async-start(bf16[128,32,128]{2,1,0:T(8,128)(2,1)} %copy.107), calls=%async_computation.1 | async-start | bytes 2097152 | tf_op jit(solution)/shard_map/all_to_all | solution.py:18
  56.2 3.3 copy.117
  59.5 20.3 %all-to-all-done.1 = bf16[128,32,128]{2,1,0:T(8,128)(2,1)S(1)} async-done(((bf16[128,32,128]{2,1,0:T(8,128)(2,1)}), bf16[128,32,128]{2,1,0:T(8,128)(2,1)S(1)}, u32[]{:S(2)}, u32[]{:S(2)}) %all-to-all-start.1) | async-done | bytes 1048608 | tf_op jit(solution)/shard_map/all_to_all | solution.py:18
  79.9 8.6 %all-to-all-start.4 = ((bf16[2,64,4096]{2,0,1:T(2,128)(2,1)}), bf16[2,64,4096]{2,0,1:T(2,128)(2,1)}, u32[]{:S(2)}, u32[]{:S(2)}) async-start(bf16[2,64,4096]{2,0,1:T(2,128)(2,1)} %copy.117), calls=%async_computation.4 | async-start | bytes 2097152 | tf_op jit(solution)/shard_map/all_to_all | solution.py:22
  97.6 22.2 %all-to-all-done.4 = bf16[2,64,4096]{2,0,1:T(2,128)(2,1)} async-done(((bf16[2,64,4096]{2,0,1:T(2,128)(2,1)}), bf16[2,64,4096]{2,0,1:T(2,128)(2,1)}, u32[]{:S(2)}, u32[]{:S(2)}) %all-to-all-start.4) | async-done | bytes 1048608 | tf_op jit(solution)/shard_map/all_to_all | solution.py:22
  119.8 4.4 all-to-all-start.2
  124.3 3.3 copy.118
  129.9 14.7 %all-to-all-done.2 = bf16[2,64,4096]{2,0,1:T(2,128)(2,1)} async-done(((bf16[2,64,4096]{2,0,1:T(2,128)(2,1)}), bf16[2,64,4096]{2,0,1:T(2,128)(2,1)}, u32[]{:S(2)}, u32[]{:S(2)}) %all-to-all-start.2) | async-done | bytes 1048608 | tf_op jit(solution)/shard_map/all_to_all | solution.py:22
  144.7 3.4 copy_bitcast_fusion
  148.1 3.7 reshape.50
  151.8 3.0 fusion.1
  155.6 26.4 %all_to_all.121 = bf16[32,4,4096]{2,1,0:T(4,128)(2,1)S(1)} all-to-all(bf16[32,4,4096]{2,1,0:T(4,128)(2,1)S(1)} %copy.120), channel_id=1, replica_groups=mesh['seq'=16,'hid'=16] {'hid'}, dimensions={0} | all-to-all | bytes 2097152 | tf_op jit(solution)/shard_map/all_to_all | solution.py:26
  185.6 3.0 fusion.65
  195.2 45.1 %all_to_all.122 = bf16[8,512,128]{2,0,1:T(8,128)(2,1)S(1)} all-to-all(bf16[8,512,128]{2,0,1:T(8,128)(2,1)S(1)} %copy.124), channel_id=1, replica_groups=mesh['seq'=16,'hid'=16] {'seq'}, dimensions={1} | all-to-all | bytes 2097152 | tf_op jit(solution)/shard_map/all_to_all | solution.py:14
  249.1 30.5 %all_to_all.123 = bf16[128,32,128]{2,1,0:T(8,128)(2,1)S(1)} all-to-all(bf16[128,32,128]{2,1,0:T(8,128)(2,1)} %copy.128), channel_id=1, replica_groups=mesh['seq'=16,'hid'=16] {'seq'}, dimensions={0} | all-to-all | bytes 2097152 | tf_op jit(solution)/shard_map/all_to_all | solution.py:18
  280.7 4.5 fusion.66
  285.2 6.0 %fusion.3 = bf16[32,4,4096]{2,0,1:T(8,128)(2,1)S(1)} fusion(bf16[4,32,32]{2,1,0:T(8,128)(2,1)S(1)} %copy-done.13, f32[32,4,4096]{2,0,1:T(8,128)} %reshape.50), kind=kOutput, calls=%fused_computation.6 | convolution fusion | flops 68157440 | bytes 3153920 | tf_op jit(solution)/shard_map/whg,gwv->hwv/dot_general | solution.py:72
  292.0 37.0 %all_to_all.124 = bf16[32,4,4096]{2,1,0:T(4,128)(2,1)S(1)} all-to-all(bf16[32,4,4096]{2,1,0:T(4,128)(2,1)S(1)} %copy.112), channel_id=1, replica_groups=mesh['seq'=16,'hid'=16] {'hid'}, dimensions={0} | all-to-all | bytes 2097152 | tf_op jit(solution)/shard_map/all_to_all | solution.py:26
  335.6 3.1 add_convert_fusion
  338.7 4.3 convolution_bitcast_fusion.1
  345.9 5.9 %fusion.17 = bf16[4096,128]{1,0:T(8,128)(2,1)} fusion(f32[8,512,128]{2,1,0:T(8,128)} %copy.131, f32[8,16,32,128]{3,2,1,0:T(8,128)S(1)} %copy.108, f32[4096,128]{1,0:T(8,128)} %copy.123, bf16[4096,128]{1,0:T(8,128)(2,1)} %param.9, f32[128]{0:T(128)S(1)} %copy-done.12, f32[128]{0:T(128)S(1)} %copy-done.11, bf16[4096,128]{1,0:T(8,128)(2,1)} %param.8), kind=kLoop, calls=%fused_computation.26 | loop fusion | flops 8388608 | bytes 9438208 | tf_op jit(solution)/shard_map/convert_element_type | solution.py:107
  351.9 122.2 %reduce-scatter.3.cloned.1.call-done = f32[8,32,512]{2,1,0:T(8,128)} async-done(((f32[8,512,512]{2,1,0:T(8,128)}), f32[8,32,512]{2,1,0:T(8,128)}) %reduce-scatter.3.cloned.1.call-update) | async-done | bytes 524304 | tf_op jit(solution)/shard_map/reduce_scatter | solution.py:31
  (61 shorter events, 48.4 us)
Async XLA Ops:
  7.2 40.1 %copy-start = (bf16[32,128,128]{2,1,0:T(8,128)(2,1)S(1)}, bf16[32,128,128]{2,1,0:T(8,128)(2,1)}, u32[]{:S(2)}) copy-start(bf16[32,128,128]{2,1,0:T(8,128)(2,1)} %param.11) | copy-start | bytes 3145732
  46.2 1.0 copy-start.7
  48.1 6.8 %copy-start.6 = (bf16[4096,128]{1,0:T(8,128)(2,1)S(1)}, bf16[4096,128]{1,0:T(8,128)(2,1)}, u32[]{:S(2)}) copy-start(bf16[4096,128]{1,0:T(8,128)(2,1)} %param.9) | copy-start | bytes 3145732
  49.8 30.1 %all-to-all-start.1 = ((bf16[128,32,128]{2,1,0:T(8,128)(2,1)}), bf16[128,32,128]{2,1,0:T(8,128)(2,1)S(1)}, u32[]{:S(2)}, u32[]{:S(2)}) async-start(bf16[128,32,128]{2,1,0:T(8,128)(2,1)} %copy.107), calls=%async_computation.1 | async-start | bytes 2097152 | tf_op jit(solution)/shard_map/all_to_all | solution.py:18
  79.9 39.9 %all-to-all-start.4 = ((bf16[2,64,4096]{2,0,1:T(2,128)(2,1)}), bf16[2,64,4096]{2,0,1:T(2,128)(2,1)}, u32[]{:S(2)}, u32[]{:S(2)}) async-start(bf16[2,64,4096]{2,0,1:T(2,128)(2,1)} %copy.117), calls=%async_computation.4 | async-start | bytes 2097152 | tf_op jit(solution)/shard_map/all_to_all | solution.py:22
  88.7 1.2 copy-start.2
  88.7 1.2 copy-start.11
  88.7 1.2 copy-start.12
  91.6 2.3 copy-start.10
  119.8 24.9 %all-to-all-start.2 = ((bf16[2,64,4096]{2,0,1:T(2,128)(2,1)}), bf16[2,64,4096]{2,0,1:T(2,128)(2,1)}, u32[]{:S(2)}, u32[]{:S(2)}) async-start(bf16[2,64,4096]{2,0,1:T(2,128)(2,1)} %copy.110), calls=%async_computation.2 | async-start | bytes 2097152 | tf_op jit(solution)/shard_map/all_to_all | solution.py:22
  124.1 227.7 %reduce-scatter.5.cloned.1.call-start = ((), (), s32[]{:S(2)}) async-start(), calls=%async_computation.11 | async-start | bytes 2228224 | tf_op jit(solution)/shard_map/reduce_scatter | solution.py:32
  148.1 3.7 copy-start.13
  195.2 46.3 %copy-start.8 = (bf16[16,8,32,128]{3,2,1,0:T(8,128)(2,1)S(1)}, bf16[16,8,32,128]{3,2,1,0:T(8,128)(2,1)}, u32[]{:S(2)}) copy-start(bf16[16,8,32,128]{3,2,1,0:T(8,128)(2,1)} %copy-done.7) | copy-start | bytes 3145732
  240.6 1.0 copy-start.9
  243.7 230.3 %reduce-scatter.3.cloned.1.call-start = ((), (), s32[]{:S(2)}) async-start(), calls=%async_computation.10 | async-start | bytes 8912896 | tf_op jit(solution)/shard_map/reduce_scatter | solution.py:31
  249.1 31.6 %copy-start.3 = (bf16[4096,128]{1,0:T(8,128)(2,1)S(1)}, bf16[4096,128]{1,0:T(8,128)(2,1)}, u32[]{:S(2)}) copy-start(bf16[4096,128]{1,0:T(8,128)(2,1)} %param.8) | copy-start | bytes 3145732
  279.7 1.0 copy-start.4
  335.6 3.1 copy-start.5
  345.9 128.1 %copy-start.1 = (bf16[32,128,128]{2,1,0:T(8,128)(2,1)S(1)}, bf16[32,128,128]{2,1,0:T(8,128)(2,1)}, u32[]{:S(2)}) copy-start(bf16[32,128,128]{2,1,0:T(8,128)(2,1)} %param.11) | copy-start | bytes 3145732
Sparse Core Ops, SparseCore 0:
  243.8 84.1 reduce-scatter.4
  333.2 140.7 reduce-scatter.2
where the time goes:
time: 483 us; the launch traced here: 481 us
  waiting for transfers between devices  179 us (37%)
  blocking collectives  173 us (36%)
  local copies, waits for them, and re-layouts  46.2 us (10%)
  matrix products  32.1 us (7%)
  starting transfers between devices  18.3 us (4%)
  other arithmetic  17.4 us (4%)
  between operations  14.3 us (3%)
    reduce_scatter x1, waiting for transfers between devices, grad_sums(): lax.psum_scatter(first_term, 'hid', scatter_dimension=1, tiled=True)  122 us
    all_to_all x2, blocking collectives, to_strided(): return lax.all_to_all(value, 'seq', split_axis=1, concat_axis=0, tiled=True)  79.4 us
    all_to_all x2, blocking collectives, feat_restore(): return lax.all_to_all(value, 'hid', split_axis=0, concat_axis=1, tiled=True)  63.5 us
    all_to_all x2, waiting for transfers between devices, feat_regroup(): return lax.all_to_all(value, 'hid', split_axis=1, concat_axis=0, tiled=True)  36.9 us
    all_to_all x1, blocking collectives, from_strided(): return lax.all_to_all(value, 'seq', split_axis=0, concat_axis=1, tiled=True)  30.5 us
    all_to_all x1, waiting for transfers between devices, from_strided(): return lax.all_to_all(value, 'seq', split_axis=0, concat_axis=1, tiled=True)  20.3 us
    all_to_all x2, starting transfers between devices, feat_regroup(): return lax.all_to_all(value, 'hid', split_axis=1, concat_axis=0, tiled=True)  12.9 us
  transfers between devices with their start and end apart: 5, of which 4 were waited for; matrix products, arithmetic and copies ran while one was open for 12% of the time, Pallas kernels for 0%

commit v1 on v0

v1 whole, which is shorter than its diff:
```python
import jax
import jax.numpy as jnp
from jax import lax
from jax.sharding import Mesh
from jax.sharding import PartitionSpec as P

CHUNKS = 1
SEQ = ("zl", "x")
HID = ("zh", "y", "c")
PLANE = ("y", "c")
F32 = jnp.float32
BF16 = jnp.bfloat16


def swap(value, axes):
    return lax.all_to_all(value, axes, split_axis=0, concat_axis=0, tiled=True)


def gelu_slope(value):
    normal_cdf = 0.5 * (1.0 + jax.scipy.special.erf(value * 0.7071067811865476))
    density = jnp.exp(-0.5 * value * value) * 0.3989422804014327
    return normal_cdf + value * density


def dot(spec, left, right):
    return jnp.einsum(spec, left, right, preferred_element_type=F32)


def spread_second(blocks):
    group, panels = blocks.shape[0], blocks.shape[1]
    width = group * panels
    rows = blocks.transpose(2, 0, 1).reshape(width, panels)
    col = lax.broadcasted_iota(jnp.int32, (panels, width), 1)
    pick = (col // group == lax.broadcasted_iota(jnp.int32, (panels, width), 0)).astype(BF16)
    full = dot("rb,bn->rn", rows, pick)
    at = lax.broadcasted_iota(jnp.int32, (width, width), 0) % group
    to = lax.broadcasted_iota(jnp.int32, (width, width), 1) % group
    return jnp.where(at == to, full, 0.0).astype(BF16)


def on_device(
    tokens,
    cotangent,
    seq_first,
    seq_second,
    feat_first,
    feature_second_blocks,
    gate_scale,
    gate_bias,
):
    n_seq, n_hid = lax.axis_size(SEQ), lax.axis_size(HID)
    n_plane = lax.axis_size(PLANE)
    zh = lax.axis_index("zh")
    rows, width = tokens.shape
    blocks, block = seq_first.shape[0], seq_first.shape[1]
    offs, nb = seq_second.shape[0], seq_second.shape[1]
    groups, group = feat_first.shape[0], feat_first.shape[1]
    per = offs // CHUNKS

    x_blocks = tokens.reshape(blocks, block, width)
    order = (n_seq, CHUNKS, per, blocks, width)
    x_rows = x_blocks.transpose(1, 0, 2).reshape(order)
    cot_rows = cotangent.reshape(blocks, block, width).transpose(1, 0, 2).reshape(order)
    second = seq_second.reshape(CHUNKS, per, nb, nb)

    eye = jnp.eye(groups, dtype=BF16)
    panel = (feat_first[:, :, None, :] * eye[:, None, :, None]).reshape(width, width)

    first = dot("qkj,qjc->kqc", seq_first, x_blocks).astype(BF16).reshape(order)
    x_plane = swap(x_blocks, PLANE).reshape(n_plane, block, width)
    spread = spread_second(lax.all_gather(feature_second_blocks, HID, axis=0, tiled=True))
    spread = spread.reshape(n_hid, width, n_hid, width)

    results, locals_, firsts, second_grads, first_grads = [], [], [], [], []
    for ch in range(CHUNKS):
        strided = swap(first[:, ch], SEQ).transpose(1, 0, 2, 3).reshape(per, nb, width)
        mixed_j = dot("jab,jbc->jac", second[ch], strided).astype(BF16)
        mixed_j = mixed_j.reshape(per, n_seq, blocks, width).transpose(1, 0, 2, 3)
        mixed = swap(mixed_j, SEQ).astype(F32)
        x_wide = x_rows[:, ch].astype(F32)
        cot = cot_rows[:, ch]
        gate = jax.nn.sigmoid(x_wide * gate_scale + gate_bias)
        hidden = (x_wide + gate * mixed).astype(BF16)
        inner = dot("sjqo,io->sjqi", hidden, panel).astype(BF16)
        by_row = (n_hid, per * blocks * n_seq // n_hid, width)
        cot_moved = swap(cot.reshape(by_row), HID)
        inner_moved = swap(inner.reshape(by_row), HID)
        inner_wide = inner_moved.astype(F32)
        act = jax.nn.gelu(inner_wide, approximate=False).astype(BF16)
        outer = dot("htc,hcdn->dtn", act, spread).astype(BF16)
        d_act = dot("dtn,hcdn->htc", cot_moved, spread)
        d_inner = (d_act * gelu_slope(inner_wide)).astype(BF16)
        d_back = swap(d_inner, HID).reshape(hidden.shape)
        d_hidden = cot.astype(F32) + dot("sjqi,io->sjqo", d_back, panel)
        d_mixed = (d_hidden * gate).astype(BF16)
        locals_.append(d_hidden * (1.0 + gate_scale * gate * (1.0 - gate) * mixed))
        d_mixed_j = swap(d_mixed, SEQ).transpose(1, 0, 2, 3).reshape(per, nb, width)
        d_first_j = dot("jab,jac->jbc", second[ch], d_mixed_j).astype(BF16)
        d_first_j = d_first_j.reshape(per, n_seq, blocks, width).transpose(1, 0, 2, 3)
        firsts.append(swap(d_first_j, SEQ))

        outer = swap(outer, HID).reshape(hidden.shape)
        results.append((hidden.astype(F32) + outer.astype(F32)).astype(BF16))

        part = dot("jac,jbc->jab", d_mixed_j, strided).astype(BF16)
        part = part.reshape(per, n_hid // n_plane, n_plane, nb // n_hid, nb)
        part = swap(part.transpose(2, 1, 0, 3, 4), PLANE)
        part = part.reshape(n_plane, n_hid // n_plane, per, nb // n_hid, nb).astype(F32).sum(0)
        keep = lax.dynamic_index_in_dim(part, zh, 0, keepdims=False)
        send = lax.dynamic_index_in_dim(part, 1 - zh, 0, keepdims=False)
        second_grads.append(keep + lax.ppermute(send, "zh", [(0, 1), (1, 0)]))

        d_first_q = firsts[ch].transpose(2, 0, 1, 3).reshape(blocks, n_seq * per, width)
        d_plane = swap(d_first_q, PLANE).reshape(n_plane, n_seq * per, width)
        prod = dot("skc,sjc->kj", d_plane, x_plane)
        prod = prod.reshape(n_hid // n_plane, n_plane, per, block)
        keep = lax.dynamic_index_in_dim(prod, zh, 0, keepdims=False)
        send = lax.dynamic_index_in_dim(prod, 1 - zh, 0, keepdims=False).astype(BF16)
        prod = keep + lax.ppermute(send, "zh", [(0, 1), (1, 0)]).astype(F32)
        first_grads.append(swap(prod, PLANE))

    def whole(parts):
        stacked = jnp.stack(parts, axis=1)
        return stacked.reshape(block, blocks, width).transpose(1, 0, 2).reshape(rows, width)

    d_first = jnp.stack(firsts, axis=1).reshape(block, blocks, width)
    seq_part = dot("qkj,kqc->qjc", seq_first, d_first).reshape(rows, width)
    token_grad = (seq_part + whole(locals_)).astype(BF16)
    first_grad = jnp.concatenate(first_grads, axis=1)
    second_grad = jnp.concatenate(second_grads, axis=0)
    return whole(results), token_grad, first_grad, second_grad


def solution(mesh):
    fine = Mesh(mesh.devices.reshape(4, 4, 2, 4, 2), ("zl", "x", "zh", "y", "c"))
    return jax.shard_map(
        on_device,
        mesh=fine,
        in_specs=(
            P(SEQ, HID),
            P(SEQ, HID),
            P(SEQ, None, None),
            P(SEQ, None, None),
            P(HID, None, None),
            P(HID, None, None),
            P(HID),
            P(HID),
        ),
        out_specs=(P(SEQ, HID), P(SEQ, HID), P(SEQ, HID, None), P(SEQ, HID, None)),
        check_vma=False,
    )
```

time: 483 us -> 421 us (0.87)
  waiting for transfers between devices: 179 us -> 137 us
  starting transfers between devices: 18.3 us -> 46.5 us
  blocking collectives: 173 us -> 148 us
  between operations: 14.3 us -> 0.93 us
  matrix products: 32.1 us -> 42.2 us
  other arithmetic: 17.4 us -> 7.41 us
  local copies, waits for them, and re-layouts: 46.2 us -> 37.5 us
    reduce_scatter x2 -> x0, waiting for transfers between devices: 122 us -> none  [the longest x1 122 us: grad_sums(): lax.psum_scatter(first_term, 'hid', scatter_dimension=1, tiled=True)]
    all_to_all x3 -> x9, waiting for transfers between devices: 57.2 us -> 125 us  [swap(): return lax.all_to_all(value, axes, split_axis=0, concat_axis=0, tiled=True)]
    all_to_all x5 -> x3, blocking collectives: 173 us -> 108 us  [swap(): return lax.all_to_all(value, axes, split_axis=0, concat_axis=0, tiled=True)]
    all_gather x0 -> x1, blocking collectives: none -> 40.7 us  [on_device(): lax.all_gather(feature_second_blocks, HID, axis=0, tiled=True)]
    all_to_all x3 -> x9, starting transfers between devices: 18 us -> 44 us  [swap(): return lax.all_to_all(value, axes, split_axis=0, concat_axis=0, tiled=True)]
    convert_element_type x12 -> x5, local copies, waits for them, and re-layouts: 21.3 us -> 8.11 us  [the longest x1 2.69 us: on_device(): results.append((hidden.astype(F32) + outer.astype(F32)).astype(BF16))]
    convert_element_type x6 -> x4, other arithmetic: 17.4 us -> 4.54 us  [the longest x1 2.55 us: on_device(): hidden = (x_wide + gate * mixed).astype(BF16)]
    ppermute x0 -> x2, waiting for transfers between devices: none -> 11.9 us  [the longest x1 11.9 us: on_device(): prod = keep + lax.ppermute(send, 'zh', [(0, 1), (1, 0)]).astype(F32)]
  transfers between devices with their start and end apart: 5 -> 11, of which waited for: 4 -> 9; matrix products, arithmetic and copies ran while one was open for 12% -> 15% of each run, Pallas kernels for 0% -> 0%
where the time goes in v1:
time: 421 us; the launch traced here: 420 us
  blocking collectives  148 us (35%)
  waiting for transfers between devices  137 us (33%)
  starting transfers between devices  46.5 us (11%)
  matrix products  42.2 us (10%)
  local copies, waits for them, and re-layouts  37.5 us (9%)
  other arithmetic  7.41 us (2%)
    all_to_all x9, waiting for transfers between devices, swap(): return lax.all_to_all(value, axes, split_axis=0, concat_axis=0, tiled=True)  125 us
    all_to_all x3, blocking collectives, swap(): return lax.all_to_all(value, axes, split_axis=0, concat_axis=0, tiled=True)  108 us
    all_to_all x9, starting transfers between devices, swap(): return lax.all_to_all(value, axes, split_axis=0, concat_axis=0, tiled=True)  44 us
    dot_general x11, matrix products, dot(): return jnp.einsum(spec, left, right, preferred_element_type=F32)  42.2 us
    all_gather x1, blocking collectives, on_device(): lax.all_gather(feature_second_blocks, HID, axis=0, tiled=True)  40.7 us
    unnamed x28, local copies, waits for them, and re-layouts  12.7 us
    ppermute x1, waiting for transfers between devices, on_device(): prod = keep + lax.ppermute(send, 'zh', [(0, 1), (1, 0)]).astype(F32)  11.9 us
  transfers between devices with their start and end apart: 11, of which 9 were waited for; matrix products, arithmetic and copies ran while one was open for 15% of the time, Pallas kernels for 0%

profile of v1, /device:TPU:32, one launch (start us, length us, event | category | flops | bytes accessed | tf_op | source)
XLA Modules:
  0.0 420.0 jit_solution(11952652844444209195)
XLA Ops:
  5.5 34.3 %all_to_all.60 = bf16[16,32,8,128]{3,2,1,0:T(8,128)(2,1)S(1)} all-to-all(bf16[16,32,8,128]{3,2,1,0:T(8,128)(2,1)S(1)} %bitcast.158), channel_id=1, replica_groups=mesh['zl'=4,'x'=4,'zh'=2,'y'=4,'c'=2] {'zl','x'}, dimensions={0} | all-to-all | bytes 2097152 | tf_op jit(solution)/shard_map/all_to_all | solution.py:16
  41.5 5.1 %all-to-all-start.1 = ((bf16[16,32,8,128]{3,2,1,0:T(8,128)(2,1)}), bf16[16,32,8,128]{3,2,1,0:T(8,128)(2,1)}, u32[]{:S(2)}, u32[]{:S(2)}) async-start(bf16[16,32,8,128]{3,2,1,0:T(8,128)(2,1)} %bitcast.143), calls=%async_computation.1 | async-start | bytes 2097152 | tf_op jit(solution)/shard_map/all_to_all | solution.py:16
  49.7 22.0 %all-to-all-done.1 = bf16[16,32,8,128]{3,2,1,0:T(8,128)(2,1)} async-done(((bf16[16,32,8,128]{3,2,1,0:T(8,128)(2,1)}), bf16[16,32,8,128]{3,2,1,0:T(8,128)(2,1)}, u32[]{:S(2)}, u32[]{:S(2)}) %all-to-all-start.1) | async-done | bytes 1048608 | tf_op jit(solution)/shard_map/all_to_all | solution.py:16
  71.7 8.6 %all-to-all-start.4 = ((bf16[16,256,128]{2,1,0:T(8,128)(2,1)}), bf16[16,256,128]{2,1,0:T(8,128)(2,1)}, u32[]{:S(2)}, u32[]{:S(2)}) async-start(bf16[16,256,128]{2,1,0:T(8,128)(2,1)} %bitcast.154), calls=%async_computation.4 | async-start | bytes 2097152 | tf_op jit(solution)/shard_map/all_to_all | solution.py:16
  88.5 23.0 %all-to-all-done.4 = bf16[16,256,128]{2,1,0:T(8,128)(2,1)} async-done(((bf16[16,256,128]{2,1,0:T(8,128)(2,1)}), bf16[16,256,128]{2,1,0:T(8,128)(2,1)}, u32[]{:S(2)}, u32[]{:S(2)}) %all-to-all-start.4) | async-done | bytes 1048608 | tf_op jit(solution)/shard_map/all_to_all | solution.py:16
  111.6 4.3 %all-to-all-start.2 = ((bf16[16,256,128]{1,2,0:T(8,128)(2,1)}), bf16[16,256,128]{1,2,0:T(8,128)(2,1)}, u32[]{:S(2)}, u32[]{:S(2)}) async-start(bf16[16,256,128]{1,2,0:T(8,128)(2,1)} %copy.55), calls=%async_computation.2 | async-start | bytes 2097152 | tf_op jit(solution)/shard_map/all_to_all | solution.py:16
  115.9 40.7 %all_gather.3 = bf16[64,32,32]{2,1,0:T(8,128)(2,1)S(1)} all-gather(bf16[4,32,32]{2,1,0:T(8,128)(2,1)S(1)} %copy-done.10), channel_id=1, replica_groups=mesh['zl'=4,'x'=4,'zh'=2,'y'=4,'c'=2] {'zh','y','c'}, dimensions={0}, use_global_device_ids=true | all-gather | bytes 139264 | tf_op jit(solution)/shard_map/all_gather | solution.py:71
  157.5 5.2 %fusion.5 = bf16[256,8,16,128]{3,1,2,0:T(8,128)(2,1)} fusion(bf16[2048,32]{0,1:T(8,128)(2,1)S(1)} %reshape.92, s32[2048]{0:T(1024)S(1)} %get-tuple-element.7, s32[2048]{0:T(1024)S(1)} %get-tuple-element.8, pred[2048]{0:T(1024)(128)(4,1)S(1)} %get-tuple-element.11, s32[2048]{0:T(1024)S(1)} %get-tuple-element.6, s32[2048]{0:T(1024)S(1)} %get-tuple-element.9, ...), kind=kOutput, calls=%fused_computation.7 | convolution fusion | flops 289538048 | bytes 8556544 | tf_op jit(solution)/shard_map/rb,bn->rn/dot_general | solution.py:26
  162.7 9.8 %copy.82 = bf16[256,8,16,128]{3,2,1,0:T(8,128)(2,1)} copy(bf16[256,8,16,128]{3,1,2,0:T(8,128)(2,1)} %fusion.5) | data formatting | bytes 16777216
  172.5 8.1 %fusion.50 = bf16[16,256,128]{1,2,0:T(8,128)(2,1)S(1)} fusion(bf16[16,256,128]{1,2,0:T(8,128)(2,1)} %all-to-all-done.2, bf16[16,128,16,128]{1,0,3,2:T(8,128)(2,1)} %bitcast.151, bf16[16,256,128]{2,1,0:T(8,128)(2,1)} %all-to-all-done.4), kind=kOutput, calls=%fused_computation.69 | convolution fusion | flops 2153250816 | bytes 11534336 | tf_op jit(solution)/shard_map/dtn,hcdn->htc/dot_general | solution.py:26
  180.7 33.2 %all_to_all.61 = bf16[16,256,128]{1,2,0:T(8,128)(2,1)} all-to-all(bf16[16,256,128]{1,2,0:T(8,128)(2,1)S(1)} %fusion.50), channel_id=1, replica_groups=mesh['zl'=4,'x'=4,'zh'=2,'y'=4,'c'=2] {'zh','y','c'}, dimensions={0} | all-to-all | bytes 2097152 | tf_op jit(solution)/shard_map/all_to_all | solution.py:16
  216.2 4.8 %multiply_convert_fusion = (bf16[16,32,8,128]{3,2,1,0:T(8,128)(2,1)S(1)}, f32[16,32,8,128]{3,2,1,0:T(8,128)}) fusion(f32[128]{0:T(128)S(1)} %copy-done.11, f32[16,32,8,128]{3,2,1,0:T(8,128)} %bitcast.150, f32[128]{0:T(128)S(1)} %copy-done.12, bf16[16,32,8,128]{3,2,1,0:T(8,128)(2,1)} %all-to-all-done.1, bf16[128,128,1,1]{1,0,2,3:T(8,128)(2,1)S(1)} %reshape.106, ...), kind=kOutput, calls=%fused_computation.67 | convolution fusion | flops 142606336 | bytes 8422400 | tf_op jit(solution)/shard_map/sjqi,io->sjqo/dot_general | solution.py:26
  221.0 40.3 %all_to_all.62 = bf16[16,32,8,128]{3,2,1,0:T(8,128)(2,1)S(1)} all-to-all(bf16[16,32,8,128]{3,2,1,0:T(8,128)(2,1)S(1)} %get-tuple-element.4), channel_id=1, replica_groups=mesh['zl'=4,'x'=4,'zh'=2,'y'=4,'c'=2] {'zl','x'}, dimensions={0} | all-to-all | bytes 2097152 | tf_op jit(solution)/shard_map/all_to_all | solution.py:16
  261.3 4.3 %all-to-all-start.9 = ((bf16[8,512,128]{2,1,0:T(8,128)(2,1)}), bf16[8,512,128]{2,1,0:T(8,128)(2,1)}, u32[]{:S(2)}, u32[]{:S(2)}) async-start(bf16[8,512,128]{2,1,0:T(8,128)(2,1)} %bitcast.145), calls=%async_computation.9 | async-start | bytes 2097152 | tf_op jit(solution)/shard_map/all_to_all | solution.py:16
  267.4 14.1 %all-to-all-done.9 = bf16[8,512,128]{2,1,0:T(8,128)(2,1)} async-done(((bf16[8,512,128]{2,1,0:T(8,128)(2,1)}), bf16[8,512,128]{2,1,0:T(8,128)(2,1)}, u32[]{:S(2)}, u32[]{:S(2)}) %all-to-all-start.9) | async-done | bytes 1048608 | tf_op jit(solution)/shard_map/all_to_all | solution.py:16
  281.5 5.1 %all-to-all-start.7 = ((bf16[16,32,8,128]{3,2,1,0:T(8,128)(2,1)}), bf16[16,32,8,128]{3,2,1,0:T(8,128)(2,1)S(1)}, u32[]{:S(2)}, u32[]{:S(2)}) async-start(bf16[16,32,8,128]{3,2,1,0:T(8,128)(2,1)} %bitcast.157), calls=%async_computation.7 | async-start | bytes 2097152 | tf_op jit(solution)/shard_map/all_to_all | solution.py:16
  286.6 11.6 %fusion.59 = bf16[16,256,128]{1,2,0:T(8,128)(2,1)} fusion(bf16[16,128,16,128]{1,0,3,2:T(8,128)(2,1)} %bitcast.152, bf16[16,256,128]{1,2,0:T(8,128)(2,1)} %all-to-all-done.2), kind=kOutput, calls=%fused_computation.79 | convolution fusion | flops 2182610944 | bytes 10485760 | tf_op jit(solution)/shard_map/htc,hcdn->dtn/dot_general | solution.py:26
  298.2 13.8 %all-to-all-done.7 = bf16[16,32,8,128]{3,2,1,0:T(8,128)(2,1)S(1)} async-done(((bf16[16,32,8,128]{3,2,1,0:T(8,128)(2,1)}), bf16[16,32,8,128]{3,2,1,0:T(8,128)(2,1)S(1)}, u32[]{:S(2)}, u32[]{:S(2)}) %all-to-all-start.7) | async-done | bytes 1048608 | tf_op jit(solution)/shard_map/all_to_all | solution.py:16
  312.0 4.3 %all-to-all-start.3 = ((bf16[16,256,128]{1,2,0:T(8,128)(2,1)}), bf16[16,256,128]{1,2,0:T(8,128)(2,1)}, u32[]{:S(2)}, u32[]{:S(2)}) async-start(bf16[16,256,128]{1,2,0:T(8,128)(2,1)} %fusion.59), calls=%async_computation.3 | async-start | bytes 2097152 | tf_op jit(solution)/shard_map/all_to_all | solution.py:16
  317.6 30.1 %all-to-all-done.3 = bf16[16,256,128]{1,2,0:T(8,128)(2,1)} async-done(((bf16[16,256,128]{1,2,0:T(8,128)(2,1)}), bf16[16,256,128]{1,2,0:T(8,128)(2,1)}, u32[]{:S(2)}, u32[]{:S(2)}) %all-to-all-start.3) | async-done | bytes 1048608 | tf_op jit(solution)/shard_map/all_to_all | solution.py:16
  354.0 13.9 %all-to-all-done.8 = bf16[8,512,128]{2,1,0:T(8,128)(2,1)} async-done(((bf16[8,512,128]{2,1,0:T(8,128)(2,1)}), bf16[8,512,128]{2,1,0:T(8,128)(2,1)}, u32[]{:S(2)}, u32[]{:S(2)}) %all-to-all-start.8) | async-done | bytes 1048608 | tf_op jit(solution)/shard_map/all_to_all | solution.py:16
  389.4 11.9 %collective-permute-done = bf16[8,32,512]{2,1,0:T(8,128)(2,1)S(1)} collective-permute-done((bf16[8,32,512]{2,1,0:T(8,128)(2,1)}, bf16[8,32,512]{2,1,0:T(8,128)(2,1)S(1)}, u32[]{:S(2)}, u32[]{:S(2)}) %collective-permute-start) | collective-permute-done | bytes 262176 | tf_op jit(solution)/shard_map/ppermute | solution.py:119
  403.2 4.5 %all-to-all-start.10 = ((f32[8,32,512]{2,1,0:T(8,128)}), f32[8,32,512]{2,1,0:T(8,128)}, u32[]{:S(2)}, u32[]{:S(2)}) async-start(f32[8,32,512]{2,1,0:T(8,128)} %bitcast_add_fusion.2), calls=%async_computation.10 | async-start | bytes 1048576 | tf_op jit(solution)/shard_map/all_to_all | solution.py:16
  413.4 4.7 %all-to-all-done.10 = f32[8,32,512]{2,1,0:T(8,128)} async-done(((f32[8,32,512]{2,1,0:T(8,128)}), f32[8,32,512]{2,1,0:T(8,128)}, u32[]{:S(2)}, u32[]{:S(2)}) %all-to-all-start.10) | async-done | bytes 524320 | tf_op jit(solution)/shard_map/all_to_all | solution.py:16
  (70 shorter events, 61.3 us)
Async XLA Ops:
  0.6 39.2 %copy-start = (bf16[32,128,128]{2,1,0:T(8,128)(2,1)S(1)}, bf16[32,128,128]{2,1,0:T(8,128)(2,1)}, u32[]{:S(2)}) copy-start(bf16[32,128,128]{2,1,0:T(8,128)(2,1)} %param.11) | copy-start | bytes 3145732
  41.5 30.2 %all-to-all-start.1 = ((bf16[16,32,8,128]{3,2,1,0:T(8,128)(2,1)}), bf16[16,32,8,128]{3,2,1,0:T(8,128)(2,1)}, u32[]{:S(2)}, u32[]{:S(2)}) async-start(bf16[16,32,8,128]{3,2,1,0:T(8,128)(2,1)} %bitcast.143), calls=%async_computation.1 | async-start | bytes 2097152 | tf_op jit(solution)/shard_map/all_to_all | solution.py:16
  46.6 33.6 %copy-start.2 = (bf16[4096,128]{1,0:T(8,128)(2,1)S(1)}, bf16[4096,128]{1,0:T(8,128)(2,1)}, u32[]{:S(2)}) copy-start(bf16[4096,128]{1,0:T(8,128)(2,1)} %param.8) | copy-start | bytes 3145732
  71.7 39.9 %all-to-all-start.4 = ((bf16[16,256,128]{2,1,0:T(8,128)(2,1)}), bf16[16,256,128]{2,1,0:T(8,128)(2,1)}, u32[]{:S(2)}, u32[]{:S(2)}) async-start(bf16[16,256,128]{2,1,0:T(8,128)(2,1)} %bitcast.154), calls=%async_computation.4 | async-start | bytes 2097152 | tf_op jit(solution)/shard_map/all_to_all | solution.py:16
  80.4 2.6 copy-start.9
  80.4 2.8 copy-start.11
  80.4 2.8 copy-start.12
  85.8 1.0 copy-start.3
  87.2 28.7 %copy-start.10 = (bf16[4,32,32]{2,1,0:T(8,128)(2,1)S(1)}, bf16[4,32,32]{2,1,0:T(8,128)(2,1)}, u32[]{:S(2)}) copy-start(bf16[4,32,32]{2,1,0:T(8,128)(2,1)} %param.13) | copy-start | bytes 24580
  111.6 61.0 %all-to-all-start.2 = ((bf16[16,256,128]{1,2,0:T(8,128)(2,1)}), bf16[16,256,128]{1,2,0:T(8,128)(2,1)}, u32[]{:S(2)}, u32[]{:S(2)}) async-start(bf16[16,256,128]{1,2,0:T(8,128)(2,1)} %copy.55), calls=%async_computation.2 | async-start | bytes 2097152 | tf_op jit(solution)/shard_map/all_to_all | solution.py:16
  180.7 35.5 %copy-start.7 = (bf16[8,512,128]{2,0,1:T(8,128)(2,1)S(1)}, bf16[8,512,128]{2,0,1:T(8,128)(2,1)}, u32[]{:S(2)}) copy-start(bf16[8,512,128]{2,0,1:T(8,128)(2,1)} %copy.60) | copy-start | bytes 3145732
  261.3 20.2 %all-to-all-start.9 = ((bf16[8,512,128]{2,1,0:T(8,128)(2,1)}), bf16[8,512,128]{2,1,0:T(8,128)(2,1)}, u32[]{:S(2)}, u32[]{:S(2)}) async-start(bf16[8,512,128]{2,1,0:T(8,128)(2,1)} %bitcast.145), calls=%async_computation.9 | async-start | bytes 2097152 | tf_op jit(solution)/shard_map/all_to_all | solution.py:16
  281.5 30.5 %all-to-all-start.7 = ((bf16[16,32,8,128]{3,2,1,0:T(8,128)(2,1)}), bf16[16,32,8,128]{3,2,1,0:T(8,128)(2,1)S(1)}, u32[]{:S(2)}, u32[]{:S(2)}) async-start(bf16[16,32,8,128]{3,2,1,0:T(8,128)(2,1)} %bitcast.157), calls=%async_computation.7 | async-start | bytes 2097152 | tf_op jit(solution)/shard_map/all_to_all | solution.py:16
  312.0 5.5 %copy-start.5 = (bf16[16,32,8,128]{3,2,1,0:T(8,128)(2,1)}, bf16[16,32,8,128]{3,2,1,0:T(8,128)(2,1)S(1)}, u32[]{:S(2)}) copy-start(bf16[16,32,8,128]{3,2,1,0:T(8,128)(2,1)S(1)} %all-to-all-done.7) | copy-start | bytes 3145732
  312.0 35.6 %all-to-all-start.3 = ((bf16[16,256,128]{1,2,0:T(8,128)(2,1)}), bf16[16,256,128]{1,2,0:T(8,128)(2,1)}, u32[]{:S(2)}, u32[]{:S(2)}) async-start(bf16[16,256,128]{1,2,0:T(8,128)(2,1)} %fusion.59), calls=%async_computation.3 | async-start | bytes 2097152 | tf_op jit(solution)/shard_map/all_to_all | solution.py:16
  347.6 20.2 %all-to-all-start.8 = ((bf16[8,512,128]{2,1,0:T(8,128)(2,1)}), bf16[8,512,128]{2,1,0:T(8,128)(2,1)}, u32[]{:S(2)}, u32[]{:S(2)}) async-start(bf16[8,512,128]{2,1,0:T(8,128)(2,1)} %bitcast.156), calls=%async_computation.8 | async-start | bytes 2097152 | tf_op jit(solution)/shard_map/all_to_all | solution.py:16
  367.8 19.4 %all-to-all-start.11 = ((bf16[8,2,32,8,128]{4,3,1,2,0:T(8,128)(2,1)}), bf16[8,2,32,8,128]{4,3,1,2,0:T(8,128)(2,1)S(1)}, u32[]{:S(2)}, u32[]{:S(2)}) async-start(bf16[8,2,32,8,128]{4,3,1,2,0:T(8,128)(2,1)} %bitcast.141), calls=%async_computation.11 | async-start | bytes 2097152 | tf_op jit(solution)/shard_map/all_to_all | solution.py:16
  371.4 2.7 copy-start.4
  382.4 1.4 copy-start.8
  383.2 25.2 %copy-start.6 = (bf16[16,32,8,128]{3,2,1,0:T(8,128)(2,1)S(1)}, bf16[16,32,8,128]{3,2,1,0:T(8,128)(2,1)}, u32[]{:S(2)}) copy-start(bf16[16,32,8,128]{3,2,1,0:T(8,128)(2,1)} %copy-done.5) | copy-start | bytes 3145732
  383.2 18.1 %collective-permute-start = (bf16[8,32,512]{2,1,0:T(8,128)(2,1)}, bf16[8,32,512]{2,1,0:T(8,128)(2,1)S(1)}, u32[]{:S(2)}, u32[]{:S(2)}) collective-permute-start(bf16[8,32,512]{2,1,0:T(8,128)(2,1)} %fusion.105), channel_id=1, source_target_pairs={{0,8},{8,0},{1,9},{9,1},{2,10},{10,2},{3,11},{11,3},{4,12},{12,4},... | collective-permute-start | bytes 786440 | tf_op jit(solution)/shard_map/ppermute | solution.py:119
  387.4 20.3 %collective-permute-start.1 = (f32[32,8,128]{2,1,0:T(8,128)S(1)}, f32[32,8,128]{2,1,0:T(8,128)S(1)}, u32[]{:S(2)}, u32[]{:S(2)}) collective-permute-start(f32[32,8,128]{2,1,0:T(8,128)S(1)} %dynamic-slice_bitcast_fusion), channel_id=1, source_target_pairs={{0,8},{8,0},{1,9},{9,1},{2,10},{10,2},{3,11},{11,3},{4,12},{12,4},... | collective-permute-start | bytes 393224 | tf_op jit(solution)/shard_map/ppermute | solution.py:111
  403.2 14.9 %all-to-all-start.10 = ((f32[8,32,512]{2,1,0:T(8,128)}), f32[8,32,512]{2,1,0:T(8,128)}, u32[]{:S(2)}, u32[]{:S(2)}) async-start(f32[8,32,512]{2,1,0:T(8,128)} %bitcast_add_fusion.2), calls=%async_computation.10 | async-start | bytes 1048576 | tf_op jit(solution)/shard_map/all_to_all | solution.py:16
  408.4 11.6 %copy-start.1 = (bf16[32,128,128]{2,1,0:T(8,128)(2,1)S(1)}, bf16[32,128,128]{2,1,0:T(8,128)(2,1)}, u32[]{:S(2)}) copy-start(bf16[32,128,128]{2,1,0:T(8,128)(2,1)} %param.11) | copy-start | bytes 3145732

commit v2 on v1

v2 whole, which is shorter than its diff:
```python
import jax
import jax.numpy as jnp
from jax import lax
from jax.experimental import pallas as pl
from jax.sharding import Mesh
from jax.sharding import PartitionSpec as P

SEQ = ("zl", "x")
HID = ("zh", "y", "c")
PLANE = ("y", "c")
F32 = jnp.float32
BF16 = jnp.bfloat16


def move(value, axes):
    return lax.all_to_all(value, axes, split_axis=0, concat_axis=0, tiled=True)


def turn(value, axis, dim):
    size, me = lax.axis_size(axis), lax.axis_index(axis)
    got = []
    for r in range(1, size):
        part = lax.dynamic_index_in_dim(value, me ^ r, dim, keepdims=True)
        got.append(lax.ppermute(part, axis, [(s, s ^ r) for s in range(size)]))
    for r in range(1, size):
        value = lax.dynamic_update_slice_in_dim(value, got[r - 1], me ^ r, dim)
    return value


def swap(value, axes):
    shape = value.shape
    value = value.reshape(tuple(lax.axis_size(a) for a in axes) + shape[1:])
    for dim, axis in enumerate(axes):
        value = turn(value, axis, dim)
    return value.reshape(shape)


def dot(spec, left, right):
    return jnp.einsum(spec, left, right, preferred_element_type=F32)


def mix_kernel(inner_ref, cot_ref, rows_ref, outer_ref, d_inner_ref):
    panels, offs, count = inner_ref.shape
    width = panels * offs
    col = lax.broadcasted_iota(jnp.int32, (panels, width), 1)
    row = lax.broadcasted_iota(jnp.int32, (panels, width), 0)
    pick = (col // offs == row).astype(F32).astype(BF16)
    full = jnp.dot(rows_ref[...].reshape(width, panels), pick, preferred_element_type=F32)
    at = lax.broadcasted_iota(jnp.int32, (width, width), 0) % offs
    to = lax.broadcasted_iota(jnp.int32, (width, width), 1) % offs
    spread = jnp.where(at == to, full, 0.0).astype(BF16)
    d_act = jnp.dot(spread, cot_ref[...].reshape(width, count), preferred_element_type=F32)
    inner = inner_ref[...].reshape(width, count).astype(F32)
    cdf = 0.5 * (1.0 + lax.erf(inner * 0.7071067811865476))
    density = jnp.exp(-0.5 * inner * inner) * 0.3989422804014327
    d_inner = (d_act * (cdf + inner * density)).astype(BF16)
    d_inner_ref[...] = d_inner.reshape(panels, offs, count)
    act = (inner * cdf).astype(BF16)
    outer = lax.dot_general(
        spread, act, (((0,), (0,)), ((), ())), preferred_element_type=F32
    ).astype(BF16)
    outer_ref[...] = outer.reshape(panels, offs, count)


def mix_features(inner, cot, blocks):
    panels, group, count = inner.shape
    offs = 16
    rows = blocks.transpose(2, 0, 1)
    data = pl.BlockSpec((panels, offs, count), lambda g: (0, g, 0))
    return pl.pallas_call(
        mix_kernel,
        out_shape=(jax.ShapeDtypeStruct(inner.shape, BF16),) * 2,
        grid=(group // offs,),
        in_specs=[data, data, pl.BlockSpec((panels, offs, panels), lambda g: (0, g, 0))],
        out_specs=(data, data),
        name="mix_features",
    )(inner, cot, rows)


def steps(
    tokens,
    cotangent,
    seq_first,
    seq_second,
    feat_first,
    feature_second_blocks,
    gate_scale,
    gate_bias,
):
    n_seq, n_hid = lax.axis_size(SEQ), lax.axis_size(HID)
    n_plane = lax.axis_size(PLANE)
    halves = n_hid // n_plane
    zh = lax.axis_index("zh")
    rows, width = tokens.shape
    blocks, block = seq_first.shape[0], seq_first.shape[1]
    offs, nb = seq_second.shape[0], seq_second.shape[1]
    groups, group = feat_first.shape[0], feat_first.shape[1]
    panels = feature_second_blocks.shape[1]
    count = rows // n_hid
    wide = (n_hid, count, width)
    tall = (n_hid, width, count)
    flat = (n_seq, offs, blocks, width)
    by_panel = (panels, group, count)

    x_blocks = tokens.reshape(blocks, block, width)
    first = dot("qkj,qjc->kqc", seq_first, x_blocks).astype(BF16).reshape(flat)
    first = move(first, SEQ)

    x_rows = x_blocks.transpose(1, 0, 2).reshape(wide)
    cot_rows = cotangent.reshape(blocks, block, width).transpose(1, 0, 2).reshape(wide)
    small = feature_second_blocks.reshape(1, -1, count)
    small = jnp.broadcast_to(small, (n_hid,) + small.shape[1:])
    sent = jnp.concatenate([cot_rows.transpose(0, 2, 1), small], axis=1)
    eye = jnp.eye(groups, dtype=BF16)
    panel = (feat_first[:, :, None, :] * eye[:, None, :, None]).reshape(width, width)
    panel = jnp.broadcast_to(panel, (n_hid, width, width))
    got = swap(sent, HID)
    x_plane = swap(x_blocks, PLANE)
    cot_moved = got[:, :width].reshape(by_panel)
    second_all = got[:, width:].reshape(group, panels, panels)

    strided = first.transpose(1, 0, 2, 3).reshape(offs, nb, width)
    mixed_j = dot("jab,jbc->jac", seq_second, strided).astype(BF16)
    mixed_j = mixed_j.reshape(offs, n_seq, blocks, width).transpose(1, 0, 2, 3)
    mixed = move(mixed_j, SEQ).reshape(wide)
    mixed = mixed.astype(F32)
    x_wide = x_rows.astype(F32)
    gate = jax.nn.sigmoid(x_wide * gate_scale + gate_bias)
    hidden = (x_wide + gate * mixed).astype(BF16)
    inner = dot("sio,sro->sir", panel, hidden).astype(BF16)
    inner_moved = move(inner, HID).reshape(by_panel)
    outer, d_inner = mix_features(inner_moved, cot_moved, second_all)
    d_back = move(d_inner.reshape(tall), HID)
    outer = swap(outer.reshape(tall), HID).transpose(0, 2, 1)
    d_hidden = cot_rows.astype(F32) + dot("sir,sio->sro", d_back, panel)
    d_mixed = (d_hidden * gate).astype(BF16)
    local = d_hidden * (1.0 + gate_scale * gate * (1.0 - gate) * mixed)
    d_mixed = move(d_mixed.reshape(flat), SEQ)
    d_mixed_j = d_mixed.transpose(1, 0, 2, 3).reshape(offs, nb, width)
    d_first_j = dot("jab,jac->jbc", seq_second, d_mixed_j).astype(BF16)
    d_first_j = d_first_j.reshape(offs, n_seq, blocks, width).transpose(1, 0, 2, 3)
    d_first = move(d_first_j, SEQ).reshape(block, blocks, width)

    part = dot("jac,jbc->jab", d_mixed_j, strided).astype(BF16)
    part = part.reshape(offs, halves, n_plane, nb // n_hid, nb)
    part = swap(part.transpose(2, 1, 0, 3, 4), PLANE)
    part = part.astype(F32).sum(0)
    keep = lax.dynamic_index_in_dim(part, zh, 0, keepdims=False)
    send = lax.dynamic_index_in_dim(part, 1 - zh, 0, keepdims=False)
    second_grad = keep + lax.ppermute(send, "zh", [(0, 1), (1, 0)])

    d_first_q = d_first.transpose(1, 0, 2)
    d_plane = move(d_first_q, PLANE)
    prod = dot("skc,sjc->kj", d_plane, x_plane).astype(BF16)
    prod = move(prod.reshape(n_hid, offs, block), HID)
    prod = prod.reshape(halves, n_plane, offs, block).astype(F32)
    first_grad = prod[0] + prod[1]

    def whole(value):
        return value.reshape(block, blocks, width).transpose(1, 0, 2).reshape(rows, width)

    result = whole((hidden.astype(F32) + outer.astype(F32)).astype(BF16))
    seq_part = dot("qkj,qkc->qjc", seq_first, d_first_q).reshape(rows, width)
    token_grad = (seq_part + whole(local)).astype(BF16)
    return result, token_grad, first_grad, second_grad


def solution(mesh):
    fine = Mesh(mesh.devices.reshape(4, 4, 2, 4, 2), ("zl", "x", "zh", "y", "c"))
    return jax.shard_map(
        steps,
        mesh=fine,
        in_specs=(
            P(SEQ, HID),
            P(SEQ, HID),
            P(SEQ, None, None),
            P(SEQ, None, None),
            P(HID, None, None),
            P(HID, None, None),
            P(HID),
            P(HID),
        ),
        out_specs=(P(SEQ, HID), P(SEQ, HID), P(SEQ, HID, None), P(SEQ, HID, None)),
        check_vma=False,
    )
```

time: 421 us -> 361 us (0.86)
  blocking collectives: 148 us -> 73.4 us
  matrix products: 42.2 us -> 18.5 us
  waiting for transfers between devices: 137 us -> 153 us
  starting transfers between devices: 46.5 us -> 53.5 us
  local copies, waits for them, and re-layouts: 37.5 us -> 43.4 us
  Pallas kernels: 0 us -> 5.26 us
    ppermute x2 -> x19, waiting for transfers between devices: 11.9 us -> 59 us  [the longest x18 59 us: turn(): got.append(lax.ppermute(part, axis, [(s, s ^ r) for s in range(size)]))]
    all_gather x1 -> x0, blocking collectives: 40.7 us -> none  [on_device(): lax.all_gather(feature_second_blocks, HID, axis=0, tiled=True)]
    all_to_all x3 -> x2, blocking collectives: 108 us -> 73.4 us  [move(): return lax.all_to_all(value, axes, split_axis=0, concat_axis=0, tiled=True)]
    all_to_all x9 -> x6, waiting for transfers between devices: 125 us -> 93.6 us  [move(): return lax.all_to_all(value, axes, split_axis=0, concat_axis=0, tiled=True)]
    dot_general x11 -> x8, matrix products: 42.2 us -> 18.5 us  [dot(): return jnp.einsum(spec, left, right, preferred_element_type=F32)]
    ppermute x2 -> x19, starting transfers between devices: 2.53 us -> 20.6 us  [the longest x18 19.8 us: turn(): got.append(lax.ppermute(part, axis, [(s, s ^ r) for s in range(size)]))]
    all_to_all x9 -> x6, starting transfers between devices: 44 us -> 32.9 us  [move(): return lax.all_to_all(value, axes, split_axis=0, concat_axis=0, tiled=True)]
    dynamic_update_slice x0 -> x14, local copies, waits for them, and re-layouts: none -> 9.74 us  [turn(): value = lax.dynamic_update_slice_in_dim(value, got[r - 1], me ^ r, dim)]
  transfers between devices with their start and end apart: 11 -> 25, of which waited for: 9 -> 14; matrix products, arithmetic and copies ran while one was open for 15% -> 15% of each run, Pallas kernels for 0% -> 0%
where the time goes in v2:
time: 361 us; the launch traced here: 359 us
  waiting for transfers between devices  153 us (42%)
  blocking collectives  73.4 us (20%)
  starting transfers between devices  53.5 us (15%)
  local copies, waits for them, and re-layouts  43.4 us (12%)
  matrix products  18.5 us (5%)
  other arithmetic  11.2 us (3%)
  Pallas kernels  5.26 us (1%)
    all_to_all x6, waiting for transfers between devices, move(): return lax.all_to_all(value, axes, split_axis=0, concat_axis=0, tiled=True)  93.6 us
    all_to_all x2, blocking collectives, move(): return lax.all_to_all(value, axes, split_axis=0, concat_axis=0, tiled=True)  73.4 us
    ppermute x18, waiting for transfers between devices, turn(): got.append(lax.ppermute(part, axis, [(s, s ^ r) for s in range(size)]))  59 us
    all_to_all x6, starting transfers between devices, move(): return lax.all_to_all(value, axes, split_axis=0, concat_axis=0, tiled=True)  32.9 us
    ppermute x18, starting transfers between devices, turn(): got.append(lax.ppermute(part, axis, [(s, s ^ r) for s in range(size)]))  19.8 us
    dot_general x8, matrix products, dot(): return jnp.einsum(spec, left, right, preferred_element_type=F32)  18.5 us
    dynamic_update_slice x14, local copies, waits for them, and re-layouts, turn(): value = lax.dynamic_update_slice_in_dim(value, got[r - 1], me ^ r, dim)  9.74 us
    dynamic_slice x14, local copies, waits for them, and re-layouts, turn(): part = lax.dynamic_index_in_dim(value, me ^ r, dim, keepdims=True)  9.17 us
  transfers between devices with their start and end apart: 25, of which 14 were waited for; matrix products, arithmetic and copies ran while one was open for 15% of the time, Pallas kernels for 0%

profile of v2, /device:TPU:32, one launch (start us, length us, event | category | flops | bytes accessed | tf_op | source)
XLA Modules:
  0.0 359.0 jit_solution(846966924265495627)
XLA Ops:
  2.0 4.7 %fusion.6 = bf16[512,8,128]{0,2,1:T(8,128)(2,1)} fusion(bf16[8,512,128]{2,1,0:T(8,128)(2,1)S(1)} %bitcast.111, bf16[8,512,512]{2,1,0:T(8,128)(2,1)} %param.10), kind=kOutput, calls=%fused_computation.20 | convolution fusion | flops 537395200 | bytes 6291456 | tf_op jit(solution)/shard_map/qkj,qjc->kqc/dot_general | solution.py:39
  8.4 34.3 %all_to_all.40 = bf16[16,32,8,128]{3,2,1,0:T(8,128)(2,1)S(1)} all-to-all(bf16[16,32,8,128]{3,2,1,0:T(8,128)(2,1)S(1)} %bitcast.127), channel_id=1, replica_groups=mesh['zl'=4,'x'=4,'zh'=2,'y'=4,'c'=2] {'zl','x'}, dimensions={0} | all-to-all | bytes 2097152 | tf_op jit(solution)/shard_map/all_to_all | solution.py:16
  44.4 5.1 %all-to-all-start.1 = ((bf16[16,32,8,128]{3,2,1,0:T(8,128)(2,1)}), bf16[16,32,8,128]{3,2,1,0:T(8,128)(2,1)}, u32[]{:S(2)}, u32[]{:S(2)}) async-start(bf16[16,32,8,128]{3,2,1,0:T(8,128)(2,1)} %bitcast.110), calls=%async_computation.1 | async-start | bytes 2097152 | tf_op jit(solution)/shard_map/all_to_all | solution.py:16
  56.1 4.5 %collective-permute-start = (bf16[1,4,2,144,256]{4,3,2,1,0:T(8,128)(2,1)}, bf16[1,4,2,144,256]{4,3,2,1,0:T(8,128)(2,1)}, u32[]{:S(2)}, u32[]{:S(2)}) collective-permute-start(bf16[1,4,2,144,256]{4,3,2,1,0:T(8,128)(2,1)} %constant_dynamic-slice_fusion.17), channel_id=1, source_target_pairs={{0,8},{8,0},{1,9},{9,1},{2,10},{10,2},{3,11},{11,3},{4,12},{12,4},... | collective-permute-start | bytes 1769480 | tf_op jit(solution)/shard_map/ppermute | solution.py:24
  62.8 37.1 %all-to-all-done.1 = bf16[16,32,8,128]{3,2,1,0:T(8,128)(2,1)} async-done(((bf16[16,32,8,128]{3,2,1,0:T(8,128)(2,1)}), bf16[16,32,8,128]{3,2,1,0:T(8,128)(2,1)}, u32[]{:S(2)}, u32[]{:S(2)}) %all-to-all-start.1) | async-done | bytes 1048608 | tf_op jit(solution)/shard_map/all_to_all | solution.py:16
  104.8 8.6 %all-to-all-start.2 = ((bf16[16,128,256]{2,1,0:T(8,128)(2,1)}), bf16[16,128,256]{2,1,0:T(8,128)(2,1)}, u32[]{:S(2)}, u32[]{:S(2)}) async-start(bf16[16,128,256]{2,1,0:T(8,128)(2,1)} %convolution_convert_fusion.4), calls=%async_computation.2 | async-start | bytes 2097152 | tf_op jit(solution)/shard_map/all_to_all | solution.py:16
  117.1 11.5 %collective-permute-done.1 = bf16[2,1,2,144,256]{4,3,2,1,0:T(8,128)(2,1)} collective-permute-done((bf16[2,1,2,144,256]{4,3,2,1,0:T(8,128)(2,1)}, bf16[2,1,2,144,256]{4,3,2,1,0:T(8,128)(2,1)}, u32[]{:S(2)}, u32[]{:S(2)}) %collective-permute-start.1) | collective-permute-done | bytes 294944 | tf_op jit(solution)/shard_map/ppermute | solution.py:24
  133.4 13.0 %collective-permute-done.2 = bf16[2,1,2,144,256]{4,3,2,1,0:T(8,128)(2,1)} collective-permute-done((bf16[2,1,2,144,256]{4,3,2,1,0:T(8,128)(2,1)}, bf16[2,1,2,144,256]{4,3,2,1,0:T(8,128)(2,1)}, u32[]{:S(2)}, u32[]{:S(2)}) %collective-permute-start.2) | collective-permute-done | bytes 294944 | tf_op jit(solution)/shard_map/ppermute | solution.py:24
  147.4 4.5 %collective-permute-done.3 = bf16[2,1,2,144,256]{4,3,2,1,0:T(8,128)(2,1)} collective-permute-done((bf16[2,1,2,144,256]{4,3,2,1,0:T(8,128)(2,1)}, bf16[2,1,2,144,256]{4,3,2,1,0:T(8,128)(2,1)}, u32[]{:S(2)}, u32[]{:S(2)}) %collective-permute-start.3) | collective-permute-done | bytes 294944 | tf_op jit(solution)/shard_map/ppermute | solution.py:24
  158.0 5.3 %mix_features.1 = (bf16[32,64,256]{2,1,0:T(8,128)(2,1)}, bf16[32,64,256]{2,1,0:T(8,128)(2,1)}) custom-call(bf16[32,64,256]{2,1,0:T(8,128)(2,1)} %bitcast.12.inner_ref, bf16[32,64,256]{2,1,0:T(8,128)(2,1)} %bitcast.126, bf16[32,64,32]{2,1,0:T(8,128)(2,1)} %bitcast.131), custom_call_target="tpu_custom_call" | custom-call | tf_op jit(solution)/shard_map/mix_features/pallas_call | solution.py:70
  164.9 39.1 %all_to_all.41 = bf16[16,128,256]{1,2,0:T(8,128)(2,1)S(1)} all-to-all(bf16[16,128,256]{1,2,0:T(8,128)(2,1)S(1)} %copy.58), channel_id=1, replica_groups=mesh['zl'=4,'x'=4,'zh'=2,'y'=4,'c'=2] {'zh','y','c'}, dimensions={0} | all-to-all | bytes 2097152 | tf_op jit(solution)/shard_map/all_to_all | solution.py:16
  204.0 4.5 %fusion.10 = (bf16[16,32,8,128]{3,2,1,0:T(8,128)(2,1)}, f32[16,256,128]{2,1,0:T(8,128)}) fusion(f32[128]{0:T(128)S(1)} %copy-done.18, f32[16,256,128]{2,1,0:T(8,128)S(1)} %bitcast.121, f32[128]{0:T(128)S(1)} %copy-done.19, bf16[16,32,8,128]{3,2,1,0:T(8,128)(2,1)} %all-to-all-done.1, bf16[16,128,256]{1,2,0:T(8,128)(2,1)S(1)} %all_to_all.41, ...), kind=kOutput, calls=%fused_computation.25 | convolution fusion | flops 142606336 | bytes 8422400 | tf_op jit(solution)/shard_map/sir,sio->sro/dot_general | solution.py:39
  208.5 5.1 %all-to-all-start.4 = ((bf16[16,32,8,128]{3,2,1,0:T(8,128)(2,1)}), bf16[16,32,8,128]{3,2,1,0:T(8,128)(2,1)S(1)}, u32[]{:S(2)}, u32[]{:S(2)}) async-start(bf16[16,32,8,128]{3,2,1,0:T(8,128)(2,1)} %get-tuple-element.8), calls=%async_computation.4 | async-start | bytes 2097152 | tf_op jit(solution)/shard_map/all_to_all | solution.py:16
  216.2 4.4 %collective-permute-done.10 = bf16[1,2,512,128]{3,2,1,0:T(8,128)(2,1)S(1)} collective-permute-done((bf16[1,2,512,128]{3,2,1,0:T(8,128)(2,1)S(1)}, bf16[1,2,512,128]{3,2,1,0:T(8,128)(2,1)S(1)}, u32[]{:S(2)}, u32[]{:S(2)}) %collective-permute-start.10) | collective-permute-done | bytes 262176 | tf_op jit(solution)/shard_map/ppermute | solution.py:24
  224.4 36.8 %all-to-all-done.4 = bf16[16,32,8,128]{3,2,1,0:T(8,128)(2,1)S(1)} async-done(((bf16[16,32,8,128]{3,2,1,0:T(8,128)(2,1)}), bf16[16,32,8,128]{3,2,1,0:T(8,128)(2,1)S(1)}, u32[]{:S(2)}, u32[]{:S(2)}) %all-to-all-start.4) | async-done | bytes 1048608 | tf_op jit(solution)/shard_map/all_to_all | solution.py:16
  263.0 5.3 %all-to-all-start.5 = ((bf16[16,32,8,128]{3,2,1,0:T(8,128)(2,1)}), bf16[16,32,8,128]{3,2,1,0:T(8,128)(2,1)}, u32[]{:S(2)}, u32[]{:S(2)}) async-start(bf16[16,32,8,128]{3,2,1,0:T(8,128)(2,1)} %bitcast.125), calls=%async_computation.5 | async-start | bytes 2097152 | tf_op jit(solution)/shard_map/all_to_all | solution.py:16
  274.5 6.2 %collective-permute-done.6 = bf16[2,1,2,128,256]{4,3,2,1,0:T(8,128)(2,1)S(1)} collective-permute-done((bf16[2,1,2,128,256]{4,3,2,1,0:T(8,128)(2,1)S(1)}, bf16[2,1,2,128,256]{4,3,2,1,0:T(8,128)(2,1)S(1)}, u32[]{:S(2)}, u32[]{:S(2)}) %collective-permute-start.6) | collective-permute-done | bytes 262176 | tf_op jit(solution)/shard_map/ppermute | solution.py:24
  288.0 4.1 %collective-permute-done.7 = bf16[2,1,2,128,256]{4,3,2,1,0:T(8,128)(2,1)S(1)} collective-permute-done((bf16[2,1,2,128,256]{4,3,2,1,0:T(8,128)(2,1)S(1)}, bf16[2,1,2,128,256]{4,3,2,1,0:T(8,128)(2,1)S(1)}, u32[]{:S(2)}, u32[]{:S(2)}) %collective-permute-start.7) | collective-permute-done | bytes 262176 | tf_op jit(solution)/shard_map/ppermute | solution.py:24
  292.2 10.2 %collective-permute-done.8 = bf16[2,1,2,128,256]{4,3,2,1,0:T(8,128)(2,1)S(1)} collective-permute-done((bf16[2,1,2,128,256]{4,3,2,1,0:T(8,128)(2,1)S(1)}, bf16[2,1,2,128,256]{4,3,2,1,0:T(8,128)(2,1)S(1)}, u32[]{:S(2)}, u32[]{:S(2)}) %collective-permute-start.8) | collective-permute-done | bytes 262176 | tf_op jit(solution)/shard_map/ppermute | solution.py:24
  309.1 4.6 %all-to-all-start.6 = ((bf16[8,512,128]{1,2,0:T(8,128)(2,1)}), bf16[8,512,128]{1,2,0:T(8,128)(2,1)}, u32[]{:S(2)}, u32[]{:S(2)}) async-start(bf16[8,512,128]{1,2,0:T(8,128)(2,1)} %bitcast.36), calls=%async_computation.6 | async-start | bytes 2097152 | tf_op jit(solution)/shard_map/all_to_all | solution.py:16
  319.9 9.6 %all-to-all-done.6 = bf16[8,512,128]{1,2,0:T(8,128)(2,1)} async-done(((bf16[8,512,128]{1,2,0:T(8,128)(2,1)}), bf16[8,512,128]{1,2,0:T(8,128)(2,1)}, u32[]{:S(2)}, u32[]{:S(2)}) %all-to-all-start.6) | async-done | bytes 1048608 | tf_op jit(solution)/shard_map/all_to_all | solution.py:16
  332.3 4.2 %all-to-all-start.7 = ((bf16[16,32,512]{2,1,0:T(8,128)(2,1)}), bf16[16,32,512]{2,1,0:T(8,128)(2,1)}, u32[]{:S(2)}, u32[]{:S(2)}) async-start(bf16[16,32,512]{2,1,0:T(8,128)(2,1)} %bitcast.45), calls=%async_computation.7 | async-start | bytes 1048576 | tf_op jit(solution)/shard_map/all_to_all | solution.py:16
  342.2 3.2 fusion.5
  346.8 10.2 %all-to-all-done.7 = bf16[16,32,512]{2,1,0:T(8,128)(2,1)} async-done(((bf16[16,32,512]{2,1,0:T(8,128)(2,1)}), bf16[16,32,512]{2,1,0:T(8,128)(2,1)}, u32[]{:S(2)}, u32[]{:S(2)}) %all-to-all-start.7) | async-done | bytes 524320 | tf_op jit(solution)/shard_map/all_to_all | solution.py:16
  (136 shorter events, 82.0 us)
Async XLA Ops:
  44.4 55.4 %all-to-all-start.1 = ((bf16[16,32,8,128]{3,2,1,0:T(8,128)(2,1)}), bf16[16,32,8,128]{3,2,1,0:T(8,128)(2,1)}, u32[]{:S(2)}, u32[]{:S(2)}) async-start(bf16[16,32,8,128]{3,2,1,0:T(8,128)(2,1)} %bitcast.110), calls=%async_computation.1 | async-start | bytes 2097152 | tf_op jit(solution)/shard_map/all_to_all | solution.py:16
  56.1 57.2 %collective-permute-start = (bf16[1,4,2,144,256]{4,3,2,1,0:T(8,128)(2,1)}, bf16[1,4,2,144,256]{4,3,2,1,0:T(8,128)(2,1)}, u32[]{:S(2)}, u32[]{:S(2)}) collective-permute-start(bf16[1,4,2,144,256]{4,3,2,1,0:T(8,128)(2,1)} %constant_dynamic-slice_fusion.17), channel_id=1, source_target_pairs={{0,8},{8,0},{1,9},{9,1},{2,10},{10,2},{3,11},{11,3},{4,12},{12,4},... | collective-permute-start | bytes 1769480 | tf_op jit(solution)/shard_map/ppermute | solution.py:24
  104.8 53.2 %all-to-all-start.2 = ((bf16[16,128,256]{2,1,0:T(8,128)(2,1)}), bf16[16,128,256]{2,1,0:T(8,128)(2,1)}, u32[]{:S(2)}, u32[]{:S(2)}) async-start(bf16[16,128,256]{2,1,0:T(8,128)(2,1)} %convolution_convert_fusion.4), calls=%async_computation.2 | async-start | bytes 2097152 | tf_op jit(solution)/shard_map/all_to_all | solution.py:16
  115.2 13.4 %collective-permute-start.1 = (bf16[2,1,2,144,256]{4,3,2,1,0:T(8,128)(2,1)}, bf16[2,1,2,144,256]{4,3,2,1,0:T(8,128)(2,1)}, u32[]{:S(2)}, u32[]{:S(2)}) collective-permute-start(bf16[2,1,2,144,256]{4,3,2,1,0:T(8,128)(2,1)} %constant_dynamic-slice_fusion.16), channel_id=1, source_target_pairs={{0,2},{2,0},{4,6},{6,4},{1,3},{3,1},{5,7},{7,5},{8,10},{10,8},{12,... | collective-permute-start | bytes 884744 | tf_op jit(solution)/shard_map/ppermute | solution.py:24
  130.4 16.0 %collective-permute-start.2 = (bf16[2,1,2,144,256]{4,3,2,1,0:T(8,128)(2,1)}, bf16[2,1,2,144,256]{4,3,2,1,0:T(8,128)(2,1)}, u32[]{:S(2)}, u32[]{:S(2)}) collective-permute-start(bf16[2,1,2,144,256]{4,3,2,1,0:T(8,128)(2,1)} %get-tuple-element.11), channel_id=1, source_target_pairs={{0,4},{2,6},{4,0},{6,2},{1,5},{3,7},{5,1},{7,3},{8,12},{10,14},{12... | collective-permute-start | bytes 884744 | tf_op jit(solution)/shard_map/ppermute | solution.py:24
  133.1 18.8 %collective-permute-start.3 = (bf16[2,1,2,144,256]{4,3,2,1,0:T(8,128)(2,1)}, bf16[2,1,2,144,256]{4,3,2,1,0:T(8,128)(2,1)}, u32[]{:S(2)}, u32[]{:S(2)}) collective-permute-start(bf16[2,1,2,144,256]{4,3,2,1,0:T(8,128)(2,1)} %get-tuple-element.10), channel_id=1, source_target_pairs={{0,6},{2,4},{4,2},{6,0},{1,7},{3,5},{5,3},{7,1},{8,14},{10,12},{12... | collective-permute-start | bytes 884744 | tf_op jit(solution)/shard_map/ppermute | solution.py:24
  208.5 52.7 %all-to-all-start.4 = ((bf16[16,32,8,128]{3,2,1,0:T(8,128)(2,1)}), bf16[16,32,8,128]{3,2,1,0:T(8,128)(2,1)S(1)}, u32[]{:S(2)}, u32[]{:S(2)}) async-start(bf16[16,32,8,128]{3,2,1,0:T(8,128)(2,1)} %get-tuple-element.8), calls=%async_computation.4 | async-start | bytes 2097152 | tf_op jit(solution)/shard_map/all_to_all | solution.py:16
  213.6 7.0 %collective-permute-start.10 = (bf16[1,2,512,128]{3,2,1,0:T(8,128)(2,1)S(1)}, bf16[1,2,512,128]{3,2,1,0:T(8,128)(2,1)S(1)}, u32[]{:S(2)}, u32[]{:S(2)}) collective-permute-start(bf16[1,2,512,128]{3,2,1,0:T(8,128)(2,1)S(1)} %constant_dynamic-slice_fusion.7), channel_id=1, source_target_pairs={{0,2},{2,0},{4,6},{6,4},{1,3},{3,1},{5,7},{7,5},{8,10},{10,8},{12,... | collective-permute-start | bytes 786440 | tf_op jit(solution)/shard_map/ppermute | solution.py:24
  215.6 53.8 %collective-permute-start.5 = (bf16[1,4,2,128,256]{4,3,2,1,0:T(8,128)(2,1)}, bf16[1,4,2,128,256]{4,3,2,1,0:T(8,128)(2,1)}, u32[]{:S(2)}, u32[]{:S(2)}) collective-permute-start(bf16[1,4,2,128,256]{4,3,2,1,0:T(8,128)(2,1)} %constant_dynamic-slice_fusion.12), channel_id=1, source_target_pairs={{0,8},{8,0},{1,9},{9,1},{2,10},{10,2},{3,11},{11,3},{4,12},{12,4},... | collective-permute-start | bytes 1572872 | tf_op jit(solution)/shard_map/ppermute | solution.py:24
  221.4 46.9 %collective-permute-start.11 = (bf16[1,2,512,128]{3,2,1,0:T(8,128)(2,1)}, bf16[1,2,512,128]{3,2,1,0:T(8,128)(2,1)}, u32[]{:S(2)}, u32[]{:S(2)}) collective-permute-start(bf16[1,2,512,128]{3,2,1,0:T(8,128)(2,1)} %get-tuple-element.17), channel_id=1, source_target_pairs={{0,4},{2,6},{4,0},{6,2},{1,5},{3,7},{5,1},{7,3},{8,12},{10,14},{12... | collective-permute-start | bytes 786440 | tf_op jit(solution)/shard_map/ppermute | solution.py:24
  223.2 59.1 %collective-permute-start.12 = (bf16[1,2,512,128]{3,2,1,0:T(8,128)(2,1)S(1)}, bf16[1,2,512,128]{3,2,1,0:T(8,128)(2,1)}, u32[]{:S(2)}, u32[]{:S(2)}) collective-permute-start(bf16[1,2,512,128]{3,2,1,0:T(8,128)(2,1)S(1)} %get-tuple-element.16), channel_id=1, source_target_pairs={{0,6},{2,4},{4,2},{6,0},{1,7},{3,5},{5,3},{7,1},{8,14},{10,12},{12... | collective-permute-start | bytes 786440 | tf_op jit(solution)/shard_map/ppermute | solution.py:24
  263.0 43.7 %all-to-all-start.5 = ((bf16[16,32,8,128]{3,2,1,0:T(8,128)(2,1)}), bf16[16,32,8,128]{3,2,1,0:T(8,128)(2,1)}, u32[]{:S(2)}, u32[]{:S(2)}) async-start(bf16[16,32,8,128]{3,2,1,0:T(8,128)(2,1)} %bitcast.125), calls=%async_computation.5 | async-start | bytes 2097152 | tf_op jit(solution)/shard_map/all_to_all | solution.py:16
  271.5 9.2 %collective-permute-start.6 = (bf16[2,1,2,128,256]{4,3,2,1,0:T(8,128)(2,1)S(1)}, bf16[2,1,2,128,256]{4,3,2,1,0:T(8,128)(2,1)S(1)}, u32[]{:S(2)}, u32[]{:S(2)}) collective-permute-start(bf16[2,1,2,128,256]{4,3,2,1,0:T(8,128)(2,1)S(1)} %constant_dynamic-slice_fusion.11), channel_id=1, source_target_pairs={{0,2},{2,0},{4,6},{6,4},{1,3},{3,1},{5,7},{7,5},{8,10},{10,8},{12,... | collective-permute-start | bytes 786440 | tf_op jit(solution)/shard_map/ppermute | solution.py:24
  272.4 13.9 %collective-permute-start.14 = (bf16[1,2,2,32,8,128]{5,4,1,0,2,3:T(8,128)(2,1)S(1)}, bf16[1,2,2,32,8,128]{5,4,1,0,2,3:T(8,128)(2,1)S(1)}, u32[]{:S(2)}, u32[]{:S(2)}) collective-permute-start(bf16[1,2,2,32,8,128]{5,4,1,0,2,3:T(8,128)(2,1)S(1)} %constant_dynamic-slice_fusion.3), channel_id=1, source_target_pairs={{0,2},{2,0},{4,6},{6,4},{1,3},{3,1},{5,7},{7,5},{8,10},{10,8},{12,... | collective-permute-start | bytes 786440 | tf_op jit(solution)/shard_map/ppermute | solution.py:24
  280.7 11.4 %collective-permute-start.7 = (bf16[2,1,2,128,256]{4,3,2,1,0:T(8,128)(2,1)S(1)}, bf16[2,1,2,128,256]{4,3,2,1,0:T(8,128)(2,1)S(1)}, u32[]{:S(2)}, u32[]{:S(2)}) collective-permute-start(bf16[2,1,2,128,256]{4,3,2,1,0:T(8,128)(2,1)S(1)} %get-tuple-element.20), channel_id=1, source_target_pairs={{0,4},{2,6},{4,0},{6,2},{1,5},{3,7},{5,1},{7,3},{8,12},{10,14},{12... | collective-permute-start | bytes 786440 | tf_op jit(solution)/shard_map/ppermute | solution.py:24
  283.3 19.1 %collective-permute-start.8 = (bf16[2,1,2,128,256]{4,3,2,1,0:T(8,128)(2,1)S(1)}, bf16[2,1,2,128,256]{4,3,2,1,0:T(8,128)(2,1)S(1)}, u32[]{:S(2)}, u32[]{:S(2)}) collective-permute-start(bf16[2,1,2,128,256]{4,3,2,1,0:T(8,128)(2,1)S(1)} %get-tuple-element.19), channel_id=1, source_target_pairs={{0,6},{2,4},{4,2},{6,0},{1,7},{3,5},{5,3},{7,1},{8,14},{10,12},{12... | collective-permute-start | bytes 786440 | tf_op jit(solution)/shard_map/ppermute | solution.py:24
  285.4 28.4 %collective-permute-start.13 = (bf16[4,1,512,128]{3,2,1,0:T(8,128)(2,1)}, bf16[4,1,512,128]{3,2,1,0:T(8,128)(2,1)}, u32[]{:S(2)}, u32[]{:S(2)}) collective-permute-start(bf16[4,1,512,128]{3,2,1,0:T(8,128)(2,1)} %constant_dynamic-slice_fusion.4), channel_id=1, source_target_pairs={{0,1},{1,0},{2,3},{3,2},{4,5},{5,4},{6,7},{7,6},{8,9},{9,8},{10,11... | collective-permute-start | bytes 1572872 | tf_op jit(solution)/shard_map/ppermute | solution.py:24
  286.4 17.0 %collective-permute-start.15 = (bf16[1,2,2,32,8,128]{5,4,1,0,2,3:T(8,128)(2,1)S(1)}, bf16[1,2,2,32,8,128]{5,4,1,0,2,3:T(8,128)(2,1)S(1)}, u32[]{:S(2)}, u32[]{:S(2)}) collective-permute-start(bf16[1,2,2,32,8,128]{5,4,1,0,2,3:T(8,128)(2,1)S(1)} %get-tuple-element.14), channel_id=1, source_target_pairs={{0,4},{2,6},{4,0},{6,2},{1,5},{3,7},{5,1},{7,3},{8,12},{10,14},{12... | collective-permute-start | bytes 786440 | tf_op jit(solution)/shard_map/ppermute | solution.py:24
  292.1 13.6 %collective-permute-start.16 = (bf16[1,2,2,32,8,128]{5,4,1,0,2,3:T(8,128)(2,1)S(1)}, bf16[1,2,2,32,8,128]{5,4,1,0,2,3:T(8,128)(2,1)S(1)}, u32[]{:S(2)}, u32[]{:S(2)}) collective-permute-start(bf16[1,2,2,32,8,128]{5,4,1,0,2,3:T(8,128)(2,1)S(1)} %get-tuple-element.13), channel_id=1, source_target_pairs={{0,6},{2,4},{4,2},{6,0},{1,7},{3,5},{5,3},{7,1},{8,14},{10,12},{12... | collective-permute-start | bytes 786440 | tf_op jit(solution)/shard_map/ppermute | solution.py:24
  303.4 11.5 %collective-permute-start.9 = (bf16[2,4,1,128,256]{4,3,2,1,0:T(8,128)(2,1)}, bf16[2,4,1,128,256]{4,3,2,1,0:T(8,128)(2,1)}, u32[]{:S(2)}, u32[]{:S(2)}) collective-permute-start(bf16[2,4,1,128,256]{4,3,2,1,0:T(8,128)(2,1)} %constant_dynamic-slice_fusion.8), channel_id=1, source_target_pairs={{0,1},{1,0},{2,3},{3,2},{4,5},{5,4},{6,7},{7,6},{8,9},{9,8},{10,11... | collective-permute-start | bytes 1572872 | tf_op jit(solution)/shard_map/ppermute | solution.py:24
  306.7 11.0 %collective-permute-start.17 = (bf16[4,1,2,32,8,128]{5,4,1,0,2,3:T(8,128)(2,1)}, bf16[4,1,2,32,8,128]{5,4,1,0,2,3:T(8,128)(2,1)}, u32[]{:S(2)}, u32[]{:S(2)}) collective-permute-start(bf16[4,1,2,32,8,128]{5,4,1,0,2,3:T(8,128)(2,1)} %constant_dynamic-slice_fusion), channel_id=1, source_target_pairs={{0,1},{1,0},{2,3},{3,2},{4,5},{5,4},{6,7},{7,6},{8,9},{9,8},{10,11... | collective-permute-start | bytes 1572872 | tf_op jit(solution)/shard_map/ppermute | solution.py:24
  309.1 20.3 %all-to-all-start.6 = ((bf16[8,512,128]{1,2,0:T(8,128)(2,1)}), bf16[8,512,128]{1,2,0:T(8,128)(2,1)}, u32[]{:S(2)}, u32[]{:S(2)}) async-start(bf16[8,512,128]{1,2,0:T(8,128)(2,1)} %bitcast.36), calls=%async_computation.6 | async-start | bytes 2097152 | tf_op jit(solution)/shard_map/all_to_all | solution.py:16
  319.1 22.4 %collective-permute-start.18 = (f32[32,8,128]{2,1,0:T(8,128)S(1)}, f32[32,8,128]{2,1,0:T(8,128)S(1)}, u32[]{:S(2)}, u32[]{:S(2)}) collective-permute-start(f32[32,8,128]{2,1,0:T(8,128)S(1)} %dynamic-slice_bitcast_fusion), channel_id=1, source_target_pairs={{0,8},{8,0},{1,9},{9,1},{2,10},{10,2},{3,11},{11,3},{4,12},{12,4},... | collective-permute-start | bytes 393224 | tf_op jit(solution)/shard_map/ppermute | solution.py:150
  332.3 24.6 %all-to-all-start.7 = ((bf16[16,32,512]{2,1,0:T(8,128)(2,1)}), bf16[16,32,512]{2,1,0:T(8,128)(2,1)}, u32[]{:S(2)}, u32[]{:S(2)}) async-start(bf16[16,32,512]{2,1,0:T(8,128)(2,1)} %bitcast.45), calls=%async_computation.7 | async-start | bytes 1048576 | tf_op jit(solution)/shard_map/all_to_all | solution.py:16
  (21 other events, 259.3 us)

commit v3 on v2

--- a/solution.py
+++ b/solution.py
@@ -18,10 +18,13 @@
 
 def turn(value, axis, dim):
     size, me = lax.axis_size(axis), lax.axis_index(axis)
+    parts = [
+        lax.dynamic_index_in_dim(value, me ^ r, dim, keepdims=True) for r in range(1, size)
+    ]
+    value, *parts = lax.optimization_barrier((value, *parts))
     got = []
     for r in range(1, size):
-        part = lax.dynamic_index_in_dim(value, me ^ r, dim, keepdims=True)
-        got.append(lax.ppermute(part, axis, [(s, s ^ r) for s in range(size)]))
+        got.append(lax.ppermute(parts[r - 1], axis, [(s, s ^ r) for s in range(size)]))
     for r in range(1, size):
         value = lax.dynamic_update_slice_in_dim(value, got[r - 1], me ^ r, dim)
     return value
@@ -75,6 +78,60 @@
         out_specs=(data, data),
         name="mix_features",
     )(inner, cot, rows)
+
+
+def gated(x_ref, mixed_ref, scale_ref, bias_ref):
+    x = x_ref[...].astype(F32)
+    mixed = mixed_ref[...].astype(F32)
+    return x, mixed, jax.nn.sigmoid(x * scale_ref[...] + bias_ref[...])
+
+
+def enter_kernel(x_ref, mixed_ref, scale_ref, bias_ref, panel_ref, hidden_ref, inner_ref):
+    x, mixed, gate = gated(x_ref, mixed_ref, scale_ref, bias_ref)
+    hidden_ref[...] = (x + gate * mixed).astype(BF16)
+    for k in range(x_ref.shape[0]):
+        inner = lax.dot_general(
+            panel_ref[...],
+            hidden_ref[k],
+            (((1,), (1,)), ((), ())),
+            preferred_element_type=F32,
+        )
+        inner_ref[k] = inner.astype(BF16)
+
+
+def back_kernel(
+    x_ref, mixed_ref, scale_ref, bias_ref, panel_ref, cot_ref, d_ref, d_mixed_ref, local_ref
+):
+    _, mixed, gate = gated(x_ref, mixed_ref, scale_ref, bias_ref)
+    slope = 1.0 + scale_ref[...] * gate * (1.0 - gate) * mixed
+    for k in range(x_ref.shape[0]):
+        d_hidden = cot_ref[k].astype(F32) + lax.dot_general(
+            d_ref[k],
+            panel_ref[...],
+            (((0,), (0,)), ((), ())),
+            preferred_element_type=F32,
+        )
+        d_mixed_ref[k] = (d_hidden * gate[k]).astype(BF16)
+        local_ref[k] = d_hidden * slope[k]
+
+
+def by_rows(kernel, x, mixed, scale, bias, panel, more, outs):
+    owners, _, width = x.shape
+    here = 4
+
+    def spec(shape):
+        return pl.BlockSpec((here,) + shape[1:], lambda g: (g, 0, 0))
+
+    vector = pl.BlockSpec((1, width), lambda g: (0, 0))
+    return pl.pallas_call(
+        kernel,
+        out_shape=outs,
+        grid=(owners // here,),
+        in_specs=[spec(x.shape), spec(x.shape), vector, vector]
+        + [pl.BlockSpec((width, width), lambda g: (0, 0))]
+        + [spec(m.shape) for m in more],
+        out_specs=tuple(spec(o.shape) for o in outs),
+    )(x, mixed, scale.reshape(1, width), bias.reshape(1, width), panel, *more)
 
 
 def steps(
@@ -113,7 +170,6 @@
     sent = jnp.concatenate([cot_rows.transpose(0, 2, 1), small], axis=1)
     eye = jnp.eye(groups, dtype=BF16)
     panel = (feat_first[:, :, None, :] * eye[:, None, :, None]).reshape(width, width)
-    panel = jnp.broadcast_to(panel, (n_hid, width, width))
     got = swap(sent, HID)
     x_plane = swap(x_blocks, PLANE)
     cot_moved = got[:, :width].reshape(by_panel)
@@ -123,23 +179,35 @@
     mixed_j = dot("jab,jbc->jac", seq_second, strided).astype(BF16)
     mixed_j = mixed_j.reshape(offs, n_seq, blocks, width).transpose(1, 0, 2, 3)
     mixed = move(mixed_j, SEQ).reshape(wide)
-    mixed = mixed.astype(F32)
-    x_wide = x_rows.astype(F32)
-    gate = jax.nn.sigmoid(x_wide * gate_scale + gate_bias)
-    hidden = (x_wide + gate * mixed).astype(BF16)
-    inner = dot("sio,sro->sir", panel, hidden).astype(BF16)
+    hidden, inner = by_rows(
+        enter_kernel,
+        x_rows,
+        mixed,
+        gate_scale,
+        gate_bias,
+        panel,
+        (),
+        (jax.ShapeDtypeStruct(wide, BF16), jax.ShapeDtypeStruct(tall, BF16)),
+    )
     inner_moved = move(inner, HID).reshape(by_panel)
     outer, d_inner = mix_features(inner_moved, cot_moved, second_all)
     d_back = move(d_inner.reshape(tall), HID)
     outer = swap(outer.reshape(tall), HID).transpose(0, 2, 1)
-    d_hidden = cot_rows.astype(F32) + dot("sir,sio->sro", d_back, panel)
-    d_mixed = (d_hidden * gate).astype(BF16)
-    local = d_hidden * (1.0 + gate_scale * gate * (1.0 - gate) * mixed)
+    d_mixed, local = by_rows(
+        back_kernel,
+        x_rows,
+        mixed,
+        gate_scale,
+        gate_bias,
+        panel,
+        (cot_rows, d_back),
+        (jax.ShapeDtypeStruct(wide, BF16), jax.ShapeDtypeStruct(wide, F32)),
+    )
     d_mixed = move(d_mixed.reshape(flat), SEQ)
     d_mixed_j = d_mixed.transpose(1, 0, 2, 3).reshape(offs, nb, width)
     d_first_j = dot("jab,jac->jbc", seq_second, d_mixed_j).astype(BF16)
-    d_first_j = d_first_j.reshape(offs, n_seq, blocks, width).transpose(1, 0, 2, 3)
-    d_first = move(d_first_j, SEQ).reshape(block, blocks, width)
+    d_first_j = d_first_j.reshape(offs, n_seq * blocks, width).transpose(1, 0, 2)
+    d_first = move(d_first_j, SEQ + PLANE).reshape(n_seq, n_plane, offs, width)
 
     part = dot("jac,jbc->jab", d_mixed_j, strided).astype(BF16)
     part = part.reshape(offs, halves, n_plane, nb // n_hid, nb)
@@ -149,19 +217,22 @@
     send = lax.dynamic_index_in_dim(part, 1 - zh, 0, keepdims=False)
     second_grad = keep + lax.ppermute(send, "zh", [(0, 1), (1, 0)])
 
-    d_first_q = d_first.transpose(1, 0, 2)
-    d_plane = move(d_first_q, PLANE)
-    prod = dot("skc,sjc->kj", d_plane, x_plane).astype(BF16)
+    prod = dot("spjc,pkc->sjk", d_first, x_plane).astype(BF16)
     prod = move(prod.reshape(n_hid, offs, block), HID)
     prod = prod.reshape(halves, n_plane, offs, block).astype(F32)
     first_grad = prod[0] + prod[1]
 
+    own = lax.dynamic_index_in_dim(seq_first, lax.axis_index(PLANE), 0, keepdims=False)
+    own = own.reshape(n_seq, offs, block)
+    seq_part = dot("sjk,spjc->pkc", own, d_first).astype(BF16)
+    seq_part = swap(seq_part, PLANE).reshape(rows, width)
+
     def whole(value):
         return value.reshape(block, blocks, width).transpose(1, 0, 2).reshape(rows, width)
 
     result = whole((hidden.astype(F32) + outer.astype(F32)).astype(BF16))
-    seq_part = dot("qkj,qkc->qjc", seq_first, d_first_q).reshape(rows, width)
-    token_grad = (seq_part + whole(local)).astype(BF16)
+    local = whole(local)
+    token_grad = (seq_part.astype(F32) + local).astype(BF16)
     return result, token_grad, first_grad, second_grad
 
 

time: 361 us -> 373 us (1.033)
  waiting for transfers between devices: 153 us -> 136 us
  starting transfers between devices: 53.5 us -> 69.4 us
  local copies, waits for them, and re-layouts: 43.4 us -> 54.3 us
  Pallas kernels: 5.26 us -> 14.7 us
  matrix products: 18.5 us -> 13.5 us
    all_to_all x6 -> x5, waiting for transfers between devices: 93.6 us -> 65.6 us  [move(): return lax.all_to_all(value, axes, split_axis=0, concat_axis=0, tiled=True)]
    ppermute x18 -> x22, waiting for transfers between devices: 59 us -> 70 us  [turn(): lax.ppermute(parts[r - 1], axis, [(s, s ^ r) for s in range(size)])]
    ppermute x18 -> x22, starting transfers between devices: 19.8 us -> 30.1 us  [turn(): lax.ppermute(parts[r - 1], axis, [(s, s ^ r) for s in range(size)])]
    pallas_call x0 -> x2, Pallas kernels: none -> 9.38 us  [by_rows(): pl.pallas_call(kernel, out_shape=outs, grid=(owners // here,), in_specs=[...]
    reshape x5 -> x1, local copies, waits for them, and re-layouts: 9.99 us -> 1.65 us  [steps(): x_blocks = tokens.reshape(blocks, block, width)]
    optimization_barrier x0 -> x2, local copies, waits for them, and re-layouts: none -> 4.98 us  [turn(): value, *parts = lax.optimization_barrier((value, *parts))]
    dot_general x8 -> x6, matrix products: 18.5 us -> 13.5 us  [dot(): return jnp.einsum(spec, left, right, preferred_element_type=F32)]
    dynamic_update_slice x14 -> x22, local copies, waits for them, and re-layouts: 9.74 us -> 12.6 us  [turn(): value = lax.dynamic_update_slice_in_dim(value, got[r - 1], me ^ r, dim)]
  transfers between devices with their start and end apart: 25 -> 28, of which waited for: 14 -> 17; matrix products, arithmetic and copies ran while one was open for 15% -> 16% of each run, Pallas kernels for 0% -> 1%
where the time goes in v3:
time: 373 us; the launch traced here: 370 us
  waiting for transfers between devices  136 us (36%)
  blocking collectives  72.6 us (19%)
  starting transfers between devices  69.4 us (19%)
  local copies, waits for them, and re-layouts  54.3 us (15%)
  Pallas kernels  14.7 us (4%)
  matrix products  13.5 us (4%)
  other arithmetic  8.46 us (2%)
    all_to_all x2, blocking collectives, move(): return lax.all_to_all(value, axes, split_axis=0, concat_axis=0, tiled=True)  72.6 us
    ppermute x22, waiting for transfers between devices, turn(): lax.ppermute(parts[r - 1], axis, [(s, s ^ r) for s in range(size)])  70 us
    all_to_all x5, waiting for transfers between devices, move(): return lax.all_to_all(value, axes, split_axis=0, concat_axis=0, tiled=True)  65.6 us
    all_to_all x5, starting transfers between devices, move(): return lax.all_to_all(value, axes, split_axis=0, concat_axis=0, tiled=True)  34.9 us
    ppermute x22, starting transfers between devices, turn(): lax.ppermute(parts[r - 1], axis, [(s, s ^ r) for s in range(size)])  30.1 us
    dot_general x6, matrix products, dot(): return jnp.einsum(spec, left, right, preferred_element_type=F32)  13.5 us
    dynamic_update_slice x22, local copies, waits for them, and re-layouts, turn(): value = lax.dynamic_update_slice_in_dim(value, got[r - 1], me ^ r, dim)  12.6 us
    pallas_call x2, Pallas kernels, by_rows(): pl.pallas_call(kernel, out_shape=outs, grid=(owners // here,), in_specs=[...  9.38 us
  transfers between devices with their start and end apart: 28, of which 17 were waited for; matrix products, arithmetic and copies ran while one was open for 16% of the time, Pallas kernels for 1%

profile of v3, /device:TPU:32, one launch (start us, length us, event | category | flops | bytes accessed | tf_op | source)
XLA Modules:
  0.0 369.6 jit_solution(14034183949591740871)
XLA Ops:
  2.0 4.7 %fusion.2 = bf16[512,8,128]{0,2,1:T(8,128)(2,1)} fusion(bf16[8,512,128]{2,1,0:T(8,128)(2,1)S(1)} %bitcast.108, bf16[8,512,512]{2,1,0:T(8,128)(2,1)} %param.10), kind=kOutput, calls=%fused_computation.11 | convolution fusion | flops 537395200 | bytes 6291456 | tf_op jit(solution)/shard_map/qkj,qjc->kqc/dot_general | solution.py:42
  8.4 34.3 %all_to_all.35 = bf16[16,32,8,128]{3,2,1,0:T(8,128)(2,1)S(1)} all-to-all(bf16[16,32,8,128]{3,2,1,0:T(8,128)(2,1)S(1)} %bitcast.129), channel_id=1, replica_groups=mesh['zl'=4,'x'=4,'zh'=2,'y'=4,'c'=2] {'zl','x'}, dimensions={0} | all-to-all | bytes 2097152 | tf_op jit(solution)/shard_map/all_to_all | solution.py:16
  44.4 5.1 %all-to-all-start.1 = ((bf16[16,32,8,128]{3,2,1,0:T(8,128)(2,1)}), bf16[16,32,8,128]{3,2,1,0:T(8,128)(2,1)S(1)}, u32[]{:S(2)}, u32[]{:S(2)}) async-start(bf16[16,32,8,128]{3,2,1,0:T(8,128)(2,1)} %bitcast.127), calls=%async_computation.1 | async-start | bytes 2097152 | tf_op jit(solution)/shard_map/all_to_all | solution.py:16
  59.1 4.5 %collective-permute-start = (bf16[1,4,2,144,256]{4,3,2,1,0:T(8,128)(2,1)}, bf16[1,4,2,144,256]{4,3,2,1,0:T(8,128)(2,1)}, u32[]{:S(2)}, u32[]{:S(2)}) collective-permute-start(bf16[1,4,2,144,256]{4,3,2,1,0:T(8,128)(2,1)} %copy.65), channel_id=1, source_target_pairs={{0,8},{8,0},{1,9},{9,1},{2,10},{10,2},{3,11},{11,3},{4,12},{12,4},... | collective-permute-start | bytes 1769480 | tf_op jit(solution)/shard_map/ppermute | solution.py:27
  66.0 33.7 %all-to-all-done.1 = bf16[16,32,8,128]{3,2,1,0:T(8,128)(2,1)S(1)} async-done(((bf16[16,32,8,128]{3,2,1,0:T(8,128)(2,1)}), bf16[16,32,8,128]{3,2,1,0:T(8,128)(2,1)S(1)}, u32[]{:S(2)}, u32[]{:S(2)}) %all-to-all-start.1) | async-done | bytes 1048608 | tf_op jit(solution)/shard_map/all_to_all | solution.py:16
  100.7 4.3 %shard_map.111 = (bf16[16,256,128]{2,1,0:T(8,128)(2,1)}, bf16[16,128,256]{2,1,0:T(8,128)(2,1)}) custom-call(bf16[16,256,128]{2,1,0:T(8,128)(2,1)} %bitcast.123, bf16[16,256,128]{2,1,0:T(8,128)(2,1)} %bitcast.121, f32[1,128]{1,0:T(1,128)} %bitcast.138, f32[1,128]{1,0:T(1,128)} %bitcast.140, bf16[128,128]{1,0:T(8,128)(2,1)} %mul.23.panel_ref), custom_call_target="tpu_custom_call" | custom-call | tf_op jit(solution)/shard_map/pallas_call | solution.py:126
  105.0 8.6 %all-to-all-start.2 = ((bf16[16,128,256]{2,1,0:T(8,128)(2,1)}), bf16[16,128,256]{2,1,0:T(8,128)(2,1)}, u32[]{:S(2)}, u32[]{:S(2)}) async-start(bf16[16,128,256]{2,1,0:T(8,128)(2,1)} %get-tuple-element.45), calls=%async_computation.2 | async-start | bytes 2097152 | tf_op jit(solution)/shard_map/all_to_all | solution.py:16
  123.1 6.2 %collective-permute-done.1 = bf16[2,1,2,144,256]{4,3,2,1,0:T(8,128)(2,1)} collective-permute-done((bf16[2,1,2,144,256]{4,3,2,1,0:T(8,128)(2,1)}, bf16[2,1,2,144,256]{4,3,2,1,0:T(8,128)(2,1)}, u32[]{:S(2)}, u32[]{:S(2)}) %collective-permute-start.1) | collective-permute-done | bytes 294944 | tf_op jit(solution)/shard_map/ppermute | solution.py:27
  130.3 7.9 %collective-permute-done.2 = bf16[2,1,2,144,256]{4,3,2,1,0:T(8,128)(2,1)} collective-permute-done((bf16[2,1,2,144,256]{4,3,2,1,0:T(8,128)(2,1)}, bf16[2,1,2,144,256]{4,3,2,1,0:T(8,128)(2,1)}, u32[]{:S(2)}, u32[]{:S(2)}) %collective-permute-start.2) | collective-permute-done | bytes 294944 | tf_op jit(solution)/shard_map/ppermute | solution.py:27
  149.5 5.3 %mix_features.1 = (bf16[32,64,256]{2,1,0:T(8,128)(2,1)}, bf16[32,64,256]{2,1,0:T(8,128)(2,1)}) custom-call(bf16[32,64,256]{2,1,0:T(8,128)(2,1)} %bitcast.13.inner_ref, bf16[32,64,256]{2,1,0:T(8,128)(2,1)} %bitcast.128, bf16[32,64,32]{2,1,0:T(8,128)(2,1)} %bitcast.131), custom_call_target="tpu_custom_call" | custom-call | tf_op jit(solution)/shard_map/mix_features/pallas_call | solution.py:73
  154.8 38.3 %all_to_all.36.d_ref = bf16[16,128,256]{2,1,0:T(8,128)(2,1)} all-to-all(bf16[16,128,256]{2,1,0:T(8,128)(2,1)} %bitcast.137), channel_id=1, replica_groups=mesh['zl'=4,'x'=4,'zh'=2,'y'=4,'c'=2] {'zh','y','c'}, dimensions={0} | all-to-all | bytes 2097152 | tf_op jit(solution)/shard_map/all_to_all | solution.py:16
  193.1 5.1 %shard_map.112 = (bf16[16,256,128]{2,1,0:T(8,128)(2,1)}, f32[16,256,128]{2,1,0:T(8,128)}) custom-call(bf16[16,256,128]{2,1,0:T(8,128)(2,1)} %bitcast.124, bf16[16,256,128]{2,1,0:T(8,128)(2,1)} %bitcast.122, f32[1,128]{1,0:T(1,128)} %bitcast.139, f32[1,128]{1,0:T(1,128)} %bitcast.141, bf16[128,128]{1,0:T(8,128)(2,1)} %mul.23.panel_ref, ...), custom_call_target="tpu_custom_call" | custom-call | tf_op jit(solution)/shard_map/pallas_call | solution.py:126
  198.2 5.7 %all-to-all-start.4 = ((bf16[16,32,8,128]{3,2,1,0:T(8,128)(2,1)}), bf16[16,32,8,128]{3,2,1,0:T(8,128)(2,1)S(1)}, u32[]{:S(2)}, u32[]{:S(2)}) async-start(bf16[16,32,8,128]{3,2,1,0:T(8,128)(2,1)} %bitcast.135), calls=%async_computation.4 | async-start | bytes 2097152 | tf_op jit(solution)/shard_map/all_to_all | solution.py:16
  213.5 5.1 %collective-permute-done.15 = bf16[1,2,512,128]{3,2,1,0:T(8,128)(2,1)S(1)} collective-permute-done((bf16[1,2,512,128]{3,2,1,0:T(8,128)(2,1)S(1)}, bf16[1,2,512,128]{3,2,1,0:T(8,128)(2,1)S(1)}, u32[]{:S(2)}, u32[]{:S(2)}) %collective-permute-start.15) | collective-permute-done | bytes 262176 | tf_op jit(solution)/shard_map/ppermute | solution.py:27
  222.6 9.0 %collective-permute-done.5 = bf16[1,4,2,128,256]{4,3,2,1,0:T(8,128)(2,1)S(1)} collective-permute-done((bf16[1,4,2,128,256]{4,3,2,1,0:T(8,128)(2,1)S(1)}, bf16[1,4,2,128,256]{4,3,2,1,0:T(8,128)(2,1)S(1)}, u32[]{:S(2)}, u32[]{:S(2)}) %collective-permute-start.5) | collective-permute-done | bytes 524320 | tf_op jit(solution)/shard_map/ppermute | solution.py:27
  234.4 17.9 %all-to-all-done.4 = bf16[16,32,8,128]{3,2,1,0:T(8,128)(2,1)S(1)} async-done(((bf16[16,32,8,128]{3,2,1,0:T(8,128)(2,1)}), bf16[16,32,8,128]{3,2,1,0:T(8,128)(2,1)S(1)}, u32[]{:S(2)}, u32[]{:S(2)}) %all-to-all-start.4) | async-done | bytes 1048608 | tf_op jit(solution)/shard_map/all_to_all | solution.py:16
  256.5 8.1 %all-to-all-start.5 = ((bf16[128,32,128]{2,1,0:T(8,128)(2,1)}), bf16[128,32,128]{2,1,0:T(8,128)(2,1)}, u32[]{:S(2)}, u32[]{:S(2)}) async-start(bf16[128,32,128]{2,1,0:T(8,128)(2,1)} %copy.58), calls=%async_computation.5 | async-start | bytes 2097152 | tf_op jit(solution)/shard_map/all_to_all | solution.py:16
  273.7 9.5 %collective-permute-done.7 = bf16[2,1,2,128,256]{4,3,2,1,0:T(8,128)(2,1)S(1)} collective-permute-done((bf16[2,1,2,128,256]{4,3,2,1,0:T(8,128)(2,1)}, bf16[2,1,2,128,256]{4,3,2,1,0:T(8,128)(2,1)S(1)}, u32[]{:S(2)}, u32[]{:S(2)}) %collective-permute-start.7) | collective-permute-done | bytes 262176 | tf_op jit(solution)/shard_map/ppermute | solution.py:27
  285.6 4.8 %collective-permute-done.8 = bf16[2,1,2,128,256]{4,3,2,1,0:T(8,128)(2,1)S(1)} collective-permute-done((bf16[2,1,2,128,256]{4,3,2,1,0:T(8,128)(2,1)S(1)}, bf16[2,1,2,128,256]{4,3,2,1,0:T(8,128)(2,1)S(1)}, u32[]{:S(2)}, u32[]{:S(2)}) %collective-permute-start.8) | collective-permute-done | bytes 262176 | tf_op jit(solution)/shard_map/ppermute | solution.py:27
  297.1 5.6 %collective-permute-done.20 = bf16[1,2,2,32,8,128]{5,4,1,0,2,3:T(8,128)(2,1)S(1)} collective-permute-done((bf16[1,2,2,32,8,128]{5,4,1,0,2,3:T(8,128)(2,1)S(1)}, bf16[1,2,2,32,8,128]{5,4,1,0,2,3:T(8,128)(2,1)S(1)}, u32[]{:S(2)}, u32[]{:S(2)}) %collective-permute-start.20) | collective-permute-done | bytes 262176 | tf_op jit(solution)/shard_map/ppermute | solution.py:27
  319.0 4.3 %collective-permute-start.22 = (f32[32,8,128]{2,1,0:T(8,128)S(1)}, f32[32,8,128]{2,1,0:T(8,128)S(1)}, u32[]{:S(2)}, u32[]{:S(2)}) collective-permute-start(f32[32,8,128]{2,1,0:T(8,128)S(1)} %dynamic-slice_bitcast_fusion), channel_id=1, source_target_pairs={{0,8},{8,0},{1,9},{9,1},{2,10},{10,2},{3,11},{11,3},{4,12},{12,4},... | collective-permute-start | bytes 393224 | tf_op jit(solution)/shard_map/ppermute | solution.py:218
  323.3 5.3 %collective-permute-done.11 = bf16[1,2,512,128]{2,3,1,0:T(8,128)(2,1)S(1)} collective-permute-done((bf16[1,2,512,128]{2,3,1,0:T(8,128)(2,1)S(1)}, bf16[1,2,512,128]{2,3,1,0:T(8,128)(2,1)S(1)}, u32[]{:S(2)}, u32[]{:S(2)}) %collective-permute-start.11) | collective-permute-done | bytes 262176 | tf_op jit(solution)/shard_map/ppermute | solution.py:27
  339.8 7.5 %all-to-all-start.6 = ((bf16[16,32,512]{2,1,0:T(8,128)(2,1)}), bf16[16,32,512]{2,1,0:T(8,128)(2,1)}, u32[]{:S(2)}, u32[]{:S(2)}) async-start(bf16[16,32,512]{2,1,0:T(8,128)(2,1)} %fusion.5), calls=%async_computation.6 | async-start | bytes 1048576 | tf_op jit(solution)/shard_map/all_to_all | solution.py:16
  353.5 14.1 %all-to-all-done.6 = bf16[16,32,512]{2,1,0:T(8,128)(2,1)} async-done(((bf16[16,32,512]{2,1,0:T(8,128)(2,1)}), bf16[16,32,512]{2,1,0:T(8,128)(2,1)}, u32[]{:S(2)}, u32[]{:S(2)}) %all-to-all-start.6) | async-done | bytes 524320 | tf_op jit(solution)/shard_map/all_to_all | solution.py:16
  (132 shorter events, 113.9 us)
Async XLA Ops:
  44.4 55.3 %all-to-all-start.1 = ((bf16[16,32,8,128]{3,2,1,0:T(8,128)(2,1)}), bf16[16,32,8,128]{3,2,1,0:T(8,128)(2,1)S(1)}, u32[]{:S(2)}, u32[]{:S(2)}) async-start(bf16[16,32,8,128]{3,2,1,0:T(8,128)(2,1)} %bitcast.127), calls=%async_computation.1 | async-start | bytes 2097152 | tf_op jit(solution)/shard_map/all_to_all | solution.py:16
  59.1 57.3 %collective-permute-start = (bf16[1,4,2,144,256]{4,3,2,1,0:T(8,128)(2,1)}, bf16[1,4,2,144,256]{4,3,2,1,0:T(8,128)(2,1)}, u32[]{:S(2)}, u32[]{:S(2)}) collective-permute-start(bf16[1,4,2,144,256]{4,3,2,1,0:T(8,128)(2,1)} %copy.65), channel_id=1, source_target_pairs={{0,8},{8,0},{1,9},{9,1},{2,10},{10,2},{3,11},{11,3},{4,12},{12,4},... | collective-permute-start | bytes 1769480 | tf_op jit(solution)/shard_map/ppermute | solution.py:27
  105.0 44.5 %all-to-all-start.2 = ((bf16[16,128,256]{2,1,0:T(8,128)(2,1)}), bf16[16,128,256]{2,1,0:T(8,128)(2,1)}, u32[]{:S(2)}, u32[]{:S(2)}) async-start(bf16[16,128,256]{2,1,0:T(8,128)(2,1)} %get-tuple-element.45), calls=%async_computation.2 | async-start | bytes 2097152 | tf_op jit(solution)/shard_map/all_to_all | solution.py:16
  118.4 10.9 %collective-permute-start.1 = (bf16[2,1,2,144,256]{4,3,2,1,0:T(8,128)(2,1)}, bf16[2,1,2,144,256]{4,3,2,1,0:T(8,128)(2,1)}, u32[]{:S(2)}, u32[]{:S(2)}) collective-permute-start(bf16[2,1,2,144,256]{4,3,2,1,0:T(8,128)(2,1)} %get-tuple-element.49), channel_id=1, source_target_pairs={{0,2},{2,0},{4,6},{6,4},{1,3},{3,1},{5,7},{7,5},{8,10},{10,8},{12,... | collective-permute-start | bytes 884744 | tf_op jit(solution)/shard_map/ppermute | solution.py:27
  120.3 17.9 %collective-permute-start.2 = (bf16[2,1,2,144,256]{4,3,2,1,0:T(8,128)(2,1)}, bf16[2,1,2,144,256]{4,3,2,1,0:T(8,128)(2,1)}, u32[]{:S(2)}, u32[]{:S(2)}) collective-permute-start(bf16[2,1,2,144,256]{4,3,2,1,0:T(8,128)(2,1)} %get-tuple-element.50), channel_id=1, source_target_pairs={{0,4},{2,6},{4,0},{6,2},{1,5},{3,7},{5,1},{7,3},{8,12},{10,14},{12... | collective-permute-start | bytes 884744 | tf_op jit(solution)/shard_map/ppermute | solution.py:27
  122.9 20.4 %collective-permute-start.3 = (bf16[2,1,2,144,256]{4,3,2,1,0:T(8,128)(2,1)}, bf16[2,1,2,144,256]{4,3,2,1,0:T(8,128)(2,1)}, u32[]{:S(2)}, u32[]{:S(2)}) collective-permute-start(bf16[2,1,2,144,256]{4,3,2,1,0:T(8,128)(2,1)} %get-tuple-element.51), channel_id=1, source_target_pairs={{0,6},{2,4},{4,2},{6,0},{1,7},{3,5},{5,3},{7,1},{8,14},{10,12},{12... | collective-permute-start | bytes 884744 | tf_op jit(solution)/shard_map/ppermute | solution.py:27
  198.2 54.1 %all-to-all-start.4 = ((bf16[16,32,8,128]{3,2,1,0:T(8,128)(2,1)}), bf16[16,32,8,128]{3,2,1,0:T(8,128)(2,1)S(1)}, u32[]{:S(2)}, u32[]{:S(2)}) async-start(bf16[16,32,8,128]{3,2,1,0:T(8,128)(2,1)} %bitcast.135), calls=%async_computation.4 | async-start | bytes 2097152 | tf_op jit(solution)/shard_map/all_to_all | solution.py:16
  205.3 26.3 %collective-permute-start.5 = (bf16[1,4,2,128,256]{4,3,2,1,0:T(8,128)(2,1)S(1)}, bf16[1,4,2,128,256]{4,3,2,1,0:T(8,128)(2,1)S(1)}, u32[]{:S(2)}, u32[]{:S(2)}) collective-permute-start(bf16[1,4,2,128,256]{4,3,2,1,0:T(8,128)(2,1)S(1)} %constant_dynamic-slice_fusion.17), channel_id=1, source_target_pairs={{0,8},{8,0},{1,9},{9,1},{2,10},{10,2},{3,11},{11,3},{4,12},{12,4},... | collective-permute-start | bytes 1572872 | tf_op jit(solution)/shard_map/ppermute | solution.py:27
  206.0 12.6 %collective-permute-start.15 = (bf16[1,2,512,128]{3,2,1,0:T(8,128)(2,1)S(1)}, bf16[1,2,512,128]{3,2,1,0:T(8,128)(2,1)S(1)}, u32[]{:S(2)}, u32[]{:S(2)}) collective-permute-start(bf16[1,2,512,128]{3,2,1,0:T(8,128)(2,1)S(1)} %get-tuple-element.74), channel_id=1, source_target_pairs={{0,4},{2,6},{4,0},{6,2},{1,5},{3,7},{5,1},{7,3},{8,12},{10,14},{12... | collective-permute-start | bytes 786440 | tf_op jit(solution)/shard_map/ppermute | solution.py:27
  208.8 13.8 %collective-permute-start.16 = (bf16[1,2,512,128]{3,2,1,0:T(8,128)(2,1)S(1)}, bf16[1,2,512,128]{3,2,1,0:T(8,128)(2,1)S(1)}, u32[]{:S(2)}, u32[]{:S(2)}) collective-permute-start(bf16[1,2,512,128]{3,2,1,0:T(8,128)(2,1)S(1)} %get-tuple-element.75), channel_id=1, source_target_pairs={{0,6},{2,4},{4,2},{6,0},{1,7},{3,5},{5,3},{7,1},{8,14},{10,12},{12... | collective-permute-start | bytes 786440 | tf_op jit(solution)/shard_map/ppermute | solution.py:27
  234.4 35.2 %collective-permute-start.6 = (bf16[2,1,2,128,256]{4,3,2,1,0:T(8,128)(2,1)}, bf16[2,1,2,128,256]{4,3,2,1,0:T(8,128)(2,1)}, u32[]{:S(2)}, u32[]{:S(2)}) collective-permute-start(bf16[2,1,2,128,256]{4,3,2,1,0:T(8,128)(2,1)} %get-tuple-element.58), channel_id=1, source_target_pairs={{0,2},{2,0},{4,6},{6,4},{1,3},{3,1},{5,7},{7,5},{8,10},{10,8},{12,... | collective-permute-start | bytes 786440 | tf_op jit(solution)/shard_map/ppermute | solution.py:27
  256.5 55.0 %all-to-all-start.5 = ((bf16[128,32,128]{2,1,0:T(8,128)(2,1)}), bf16[128,32,128]{2,1,0:T(8,128)(2,1)}, u32[]{:S(2)}, u32[]{:S(2)}) async-start(bf16[128,32,128]{2,1,0:T(8,128)(2,1)} %copy.58), calls=%async_computation.5 | async-start | bytes 2097152 | tf_op jit(solution)/shard_map/all_to_all | solution.py:16
  265.4 40.3 %collective-permute-start.17 = (bf16[4,1,512,128]{3,2,1,0:T(8,128)(2,1)}, bf16[4,1,512,128]{3,2,1,0:T(8,128)(2,1)}, u32[]{:S(2)}, u32[]{:S(2)}) collective-permute-start(bf16[4,1,512,128]{3,2,1,0:T(8,128)(2,1)} %constant_dynamic-slice_fusion.4), channel_id=1, source_target_pairs={{0,1},{1,0},{2,3},{3,2},{4,5},{5,4},{6,7},{7,6},{8,9},{9,8},{10,11... | collective-permute-start | bytes 1572872 | tf_op jit(solution)/shard_map/ppermute | solution.py:27
  265.5 17.7 %collective-permute-start.7 = (bf16[2,1,2,128,256]{4,3,2,1,0:T(8,128)(2,1)}, bf16[2,1,2,128,256]{4,3,2,1,0:T(8,128)(2,1)S(1)}, u32[]{:S(2)}, u32[]{:S(2)}) collective-permute-start(bf16[2,1,2,128,256]{4,3,2,1,0:T(8,128)(2,1)} %get-tuple-element.59), channel_id=1, source_target_pairs={{0,4},{2,6},{4,0},{6,2},{1,5},{3,7},{5,1},{7,3},{8,12},{10,14},{12... | collective-permute-start | bytes 786440 | tf_op jit(solution)/shard_map/ppermute | solution.py:27
  268.5 21.8 %collective-permute-start.8 = (bf16[2,1,2,128,256]{4,3,2,1,0:T(8,128)(2,1)S(1)}, bf16[2,1,2,128,256]{4,3,2,1,0:T(8,128)(2,1)S(1)}, u32[]{:S(2)}, u32[]{:S(2)}) collective-permute-start(bf16[2,1,2,128,256]{4,3,2,1,0:T(8,128)(2,1)S(1)} %get-tuple-element.60), channel_id=1, source_target_pairs={{0,6},{2,4},{4,2},{6,0},{1,7},{3,5},{5,3},{7,1},{8,14},{10,12},{12... | collective-permute-start | bytes 786440 | tf_op jit(solution)/shard_map/ppermute | solution.py:27
  273.6 22.6 %collective-permute-start.18 = (bf16[1,2,2,32,8,128]{5,4,1,0,2,3:T(8,128)(2,1)S(1)}, bf16[1,2,2,32,8,128]{5,4,1,0,2,3:T(8,128)(2,1)S(1)}, u32[]{:S(2)}, u32[]{:S(2)}) collective-permute-start(bf16[1,2,2,32,8,128]{5,4,1,0,2,3:T(8,128)(2,1)S(1)} %get-tuple-element.79), channel_id=1, source_target_pairs={{0,2},{2,0},{4,6},{6,4},{1,3},{3,1},{5,7},{7,5},{8,10},{10,8},{12,... | collective-permute-start | bytes 786440 | tf_op jit(solution)/shard_map/ppermute | solution.py:27
  283.9 13.2 %collective-permute-start.19 = (bf16[1,2,2,32,8,128]{5,4,1,0,2,3:T(8,128)(2,1)S(1)}, bf16[1,2,2,32,8,128]{5,4,1,0,2,3:T(8,128)(2,1)S(1)}, u32[]{:S(2)}, u32[]{:S(2)}) collective-permute-start(bf16[1,2,2,32,8,128]{5,4,1,0,2,3:T(8,128)(2,1)S(1)} %get-tuple-element.80), channel_id=1, source_target_pairs={{0,4},{2,6},{4,0},{6,2},{1,5},{3,7},{5,1},{7,3},{8,12},{10,14},{12... | collective-permute-start | bytes 786440 | tf_op jit(solution)/shard_map/ppermute | solution.py:27
  291.1 11.6 %collective-permute-start.20 = (bf16[1,2,2,32,8,128]{5,4,1,0,2,3:T(8,128)(2,1)S(1)}, bf16[1,2,2,32,8,128]{5,4,1,0,2,3:T(8,128)(2,1)S(1)}, u32[]{:S(2)}, u32[]{:S(2)}) collective-permute-start(bf16[1,2,2,32,8,128]{5,4,1,0,2,3:T(8,128)(2,1)S(1)} %get-tuple-element.81), channel_id=1, source_target_pairs={{0,6},{2,4},{4,2},{6,0},{1,7},{3,5},{5,3},{7,1},{8,14},{10,12},{12... | collective-permute-start | bytes 786440 | tf_op jit(solution)/shard_map/ppermute | solution.py:27
  296.1 10.7 %collective-permute-start.9 = (bf16[2,4,1,128,256]{4,3,2,1,0:T(8,128)(2,1)S(1)}, bf16[2,4,1,128,256]{4,3,2,1,0:T(8,128)(2,1)S(1)}, u32[]{:S(2)}, u32[]{:S(2)}) collective-permute-start(bf16[2,4,1,128,256]{4,3,2,1,0:T(8,128)(2,1)S(1)} %constant_dynamic-slice_fusion.13), channel_id=1, source_target_pairs={{0,1},{1,0},{2,3},{3,2},{4,5},{5,4},{6,7},{7,6},{8,9},{9,8},{10,11... | collective-permute-start | bytes 1572872 | tf_op jit(solution)/shard_map/ppermute | solution.py:27
  314.5 14.1 %collective-permute-start.11 = (bf16[1,2,512,128]{2,3,1,0:T(8,128)(2,1)S(1)}, bf16[1,2,512,128]{2,3,1,0:T(8,128)(2,1)S(1)}, u32[]{:S(2)}, u32[]{:S(2)}) collective-permute-start(bf16[1,2,512,128]{2,3,1,0:T(8,128)(2,1)S(1)} %get-tuple-element.67), channel_id=1, source_target_pairs={{0,4},{2,6},{4,0},{6,2},{1,5},{3,7},{5,1},{7,3},{8,12},{10,14},{12... | collective-permute-start | bytes 786440 | tf_op jit(solution)/shard_map/ppermute | solution.py:27
  316.4 15.1 %collective-permute-start.12 = (bf16[1,2,512,128]{2,3,1,0:T(8,128)(2,1)S(1)}, bf16[1,2,512,128]{2,3,1,0:T(8,128)(2,1)S(1)}, u32[]{:S(2)}, u32[]{:S(2)}) collective-permute-start(bf16[1,2,512,128]{2,3,1,0:T(8,128)(2,1)S(1)} %get-tuple-element.68), channel_id=1, source_target_pairs={{0,6},{2,4},{4,2},{6,0},{1,7},{3,5},{5,3},{7,1},{8,14},{10,12},{12... | collective-permute-start | bytes 786440 | tf_op jit(solution)/shard_map/ppermute | solution.py:27
  319.0 17.4 %collective-permute-start.22 = (f32[32,8,128]{2,1,0:T(8,128)S(1)}, f32[32,8,128]{2,1,0:T(8,128)S(1)}, u32[]{:S(2)}, u32[]{:S(2)}) collective-permute-start(f32[32,8,128]{2,1,0:T(8,128)S(1)} %dynamic-slice_bitcast_fusion), channel_id=1, source_target_pairs={{0,8},{8,0},{1,9},{9,1},{2,10},{10,2},{3,11},{11,3},{4,12},{12,4},... | collective-permute-start | bytes 393224 | tf_op jit(solution)/shard_map/ppermute | solution.py:218
  332.4 14.9 %collective-permute-start.13 = (bf16[4,1,512,128]{2,3,1,0:T(8,128)(2,1)}, bf16[4,1,512,128]{2,3,1,0:T(8,128)(2,1)}, u32[]{:S(2)}, u32[]{:S(2)}) collective-permute-start(bf16[4,1,512,128]{2,3,1,0:T(8,128)(2,1)} %constant_dynamic-slice_fusion.8), channel_id=1, source_target_pairs={{0,1},{1,0},{2,3},{3,2},{4,5},{5,4},{6,7},{7,6},{8,9},{9,8},{10,11... | collective-permute-start | bytes 1572872 | tf_op jit(solution)/shard_map/ppermute | solution.py:27
  339.8 27.8 %all-to-all-start.6 = ((bf16[16,32,512]{2,1,0:T(8,128)(2,1)}), bf16[16,32,512]{2,1,0:T(8,128)(2,1)}, u32[]{:S(2)}, u32[]{:S(2)}) async-start(bf16[16,32,512]{2,1,0:T(8,128)(2,1)} %fusion.5), calls=%async_computation.6 | async-start | bytes 1048576 | tf_op jit(solution)/shard_map/all_to_all | solution.py:16
  (16 other events, 164.0 us)

commit v4 on v3

--- a/solution.py
+++ b/solution.py
@@ -21,7 +21,8 @@
     parts = [
         lax.dynamic_index_in_dim(value, me ^ r, dim, keepdims=True) for r in range(1, size)
     ]
-    value, *parts = lax.optimization_barrier((value, *parts))
+    if size > 2:
+        parts = lax.optimization_barrier(parts)
     got = []
     for r in range(1, size):
         got.append(lax.ppermute(parts[r - 1], axis, [(s, s ^ r) for s in range(size)]))
@@ -132,6 +133,23 @@
         + [spec(m.shape) for m in more],
         out_specs=tuple(spec(o.shape) for o in outs),
     )(x, mixed, scale.reshape(1, width), bias.reshape(1, width), panel, *more)
+
+
+def finish_kernel(part_ref, local_ref, out_ref):
+    out_ref[...] = (part_ref[...].astype(F32) + local_ref[...]).astype(BF16)
+
+
+def finish(part, local):
+    rows, width = part.shape
+    block = pl.BlockSpec((rows // 4, width), lambda g: (g, 0))
+    return pl.pallas_call(
+        finish_kernel,
+        out_shape=jax.ShapeDtypeStruct(part.shape, BF16),
+        grid=(4,),
+        in_specs=[block, block],
+        out_specs=block,
+        name="finish",
+    )(part, local)
 
 
 def steps(
@@ -232,7 +250,7 @@
 
     result = whole((hidden.astype(F32) + outer.astype(F32)).astype(BF16))
     local = whole(local)
-    token_grad = (seq_part.astype(F32) + local).astype(BF16)
+    token_grad = finish(seq_part, local)
     return result, token_grad, first_grad, second_grad
 
 

time: 373 us -> 355 us (0.952)
  waiting for transfers between devices: 136 us -> 113 us
  blocking collectives: 72.6 us -> 77.1 us
  starting transfers between devices: 69.4 us -> 73.4 us
  Pallas kernels: 14.7 us -> 18.5 us
    all_to_all x5, waiting for transfers between devices: 65.6 us -> 47.7 us  [move(): return lax.all_to_all(value, axes, split_axis=0, concat_axis=0, tiled=True)]
    reshape x0 -> x3, local copies, waits for them, and re-layouts: none -> 5.15 us  [the longest x2 3.43 us: swap(): value = value.reshape(tuple((lax.axis_size(a) for a in axes)) + shape[1:])]
    ppermute x22, waiting for transfers between devices: 70 us -> 65 us  [turn(): lax.ppermute(parts[r - 1], axis, [(s, s ^ r) for s in range(size)])]
    optimization_barrier x2 -> x0, local copies, waits for them, and re-layouts: 4.98 us -> none  [turn(): value, *parts = lax.optimization_barrier((value, *parts))]
    all_to_all x2, blocking collectives: 72.6 us -> 77.1 us  [move(): return lax.all_to_all(value, axes, split_axis=0, concat_axis=0, tiled=True)]
    pallas_call x0 -> x1, Pallas kernels: none -> 3.88 us  [finish(): pl.pallas_call(finish_kernel, out_shape=jax.ShapeDtypeStruct(part.shape,...]
    all_to_all x5, starting transfers between devices: 34.9 us -> 38.8 us  [move(): return lax.all_to_all(value, axes, split_axis=0, concat_axis=0, tiled=True)]
  transfers between devices with their start and end apart: 28 -> 28, of which waited for: 17 -> 14; matrix products, arithmetic and copies ran while one was open for 16% -> 16% of each run, Pallas kernels for 1% -> 2%
where the time goes in v4:
time: 355 us; the launch traced here: 353 us
  waiting for transfers between devices  113 us (32%)
  blocking collectives  77.1 us (22%)
  starting transfers between devices  73.4 us (21%)
  local copies, waits for them, and re-layouts  52 us (15%)
  Pallas kernels  18.5 us (5%)
  matrix products  13.4 us (4%)
  other arithmetic  5.16 us (1%)
    all_to_all x2, blocking collectives, move(): return lax.all_to_all(value, axes, split_axis=0, concat_axis=0, tiled=True)  77.1 us
    ppermute x22, waiting for transfers between devices, turn(): lax.ppermute(parts[r - 1], axis, [(s, s ^ r) for s in range(size)])  65 us
    all_to_all x5, waiting for transfers between devices, move(): return lax.all_to_all(value, axes, split_axis=0, concat_axis=0, tiled=True)  47.7 us
    all_to_all x5, starting transfers between devices, move(): return lax.all_to_all(value, axes, split_axis=0, concat_axis=0, tiled=True)  38.8 us
    ppermute x22, starting transfers between devices, turn(): lax.ppermute(parts[r - 1], axis, [(s, s ^ r) for s in range(size)])  29.2 us
    dynamic_update_slice x22, local copies, waits for them, and re-layouts, turn(): value = lax.dynamic_update_slice_in_dim(value, got[r - 1], me ^ r, dim)  15.5 us
    dot_general x6, matrix products, dot(): return jnp.einsum(spec, left, right, preferred_element_type=F32)  13.4 us
    dynamic_slice x12, local copies, waits for them, and re-layouts, turn(): lax.dynamic_index_in_dim(value, me ^ r, dim, keepdims=True)  9.66 us
  transfers between devices with their start and end apart: 28, of which 14 were waited for; matrix products, arithmetic and copies ran while one was open for 16% of the time, Pallas kernels for 2%

profile of v4, /device:TPU:32, one launch (start us, length us, event | category | flops | bytes accessed | tf_op | source)
XLA Modules:
  0.0 353.3 jit_solution(6914823394539284476)
XLA Ops:
  2.0 4.7 %fusion.1 = bf16[512,8,128]{0,2,1:T(8,128)(2,1)} fusion(bf16[8,512,128]{2,1,0:T(8,128)(2,1)S(1)} %bitcast.104, bf16[8,512,512]{2,1,0:T(8,128)(2,1)} %param.10), kind=kOutput, calls=%fused_computation.9 | convolution fusion | flops 537395200 | bytes 6291456 | tf_op jit(solution)/shard_map/qkj,qjc->kqc/dot_general | solution.py:43
  8.4 34.3 %all_to_all.35 = bf16[16,32,8,128]{3,2,1,0:T(8,128)(2,1)S(1)} all-to-all(bf16[16,32,8,128]{3,2,1,0:T(8,128)(2,1)S(1)} %bitcast.121), channel_id=1, replica_groups=mesh['zl'=4,'x'=4,'zh'=2,'y'=4,'c'=2] {'zl','x'}, dimensions={0} | all-to-all | bytes 2097152 | tf_op jit(solution)/shard_map/all_to_all | solution.py:16
  44.4 5.1 %all-to-all-start.1 = ((bf16[16,32,8,128]{3,2,1,0:T(8,128)(2,1)}), bf16[16,32,8,128]{3,2,1,0:T(8,128)(2,1)}, u32[]{:S(2)}, u32[]{:S(2)}) async-start(bf16[16,32,8,128]{3,2,1,0:T(8,128)(2,1)} %bitcast.103), calls=%async_computation.1 | async-start | bytes 2097152 | tf_op jit(solution)/shard_map/all_to_all | solution.py:16
  56.1 4.5 %collective-permute-start = (bf16[1,4,2,144,256]{4,3,2,1,0:T(8,128)(2,1)}, bf16[1,4,2,144,256]{4,3,2,1,0:T(8,128)(2,1)}, u32[]{:S(2)}, u32[]{:S(2)}) collective-permute-start(bf16[1,4,2,144,256]{4,3,2,1,0:T(8,128)(2,1)} %constant_dynamic-slice_fusion.22), channel_id=1, source_target_pairs={{0,8},{8,0},{1,9},{9,1},{2,10},{10,2},{3,11},{11,3},{4,12},{12,4},... | collective-permute-start | bytes 1769480 | tf_op jit(solution)/shard_map/ppermute | solution.py:28
  63.1 36.7 %all-to-all-done.1 = bf16[16,32,8,128]{3,2,1,0:T(8,128)(2,1)} async-done(((bf16[16,32,8,128]{3,2,1,0:T(8,128)(2,1)}), bf16[16,32,8,128]{3,2,1,0:T(8,128)(2,1)}, u32[]{:S(2)}, u32[]{:S(2)}) %all-to-all-start.1) | async-done | bytes 1048608 | tf_op jit(solution)/shard_map/all_to_all | solution.py:16
  99.8 4.3 %shard_map.111 = (bf16[16,256,128]{2,1,0:T(8,128)(2,1)}, bf16[16,128,256]{2,1,0:T(8,128)(2,1)}) custom-call(bf16[16,256,128]{2,1,0:T(8,128)(2,1)} %bitcast.114, bf16[16,256,128]{2,1,0:T(8,128)(2,1)} %bitcast.10.mixed_ref, f32[1,128]{1,0:T(1,128)} %bitcast.131, f32[1,128]{1,0:T(1,128)} %bitcast.133, bf16[128,128]{1,0:T(8,128)(2,1)} %mul.23.panel_ref), custom_call_target="tpu_custom_call" | custom-call | tf_op jit(solution)/shard_map/pallas_call | solution.py:127
  104.1 8.6 %all-to-all-start.2 = ((bf16[16,128,256]{2,1,0:T(8,128)(2,1)}), bf16[16,128,256]{2,1,0:T(8,128)(2,1)}, u32[]{:S(2)}, u32[]{:S(2)}) async-start(bf16[16,128,256]{2,1,0:T(8,128)(2,1)} %get-tuple-element.26), calls=%async_computation.2 | async-start | bytes 2097152 | tf_op jit(solution)/shard_map/all_to_all | solution.py:16
  119.4 9.0 %collective-permute-done.1 = bf16[2,1,2,144,256]{4,3,2,1,0:T(8,128)(2,1)} collective-permute-done((bf16[2,1,2,144,256]{4,3,2,1,0:T(8,128)(2,1)}, bf16[2,1,2,144,256]{4,3,2,1,0:T(8,128)(2,1)}, u32[]{:S(2)}, u32[]{:S(2)}) %collective-permute-start.1) | collective-permute-done | bytes 294944 | tf_op jit(solution)/shard_map/ppermute | solution.py:28
  129.4 7.6 %collective-permute-done.2 = bf16[2,1,2,144,256]{4,3,2,1,0:T(8,128)(2,1)} collective-permute-done((bf16[2,1,2,144,256]{4,3,2,1,0:T(8,128)(2,1)}, bf16[2,1,2,144,256]{4,3,2,1,0:T(8,128)(2,1)}, u32[]{:S(2)}, u32[]{:S(2)}) %collective-permute-start.2) | collective-permute-done | bytes 294944 | tf_op jit(solution)/shard_map/ppermute | solution.py:28
  144.2 5.3 %mix_features.1 = (bf16[32,64,256]{2,1,0:T(8,128)(2,1)}, bf16[32,64,256]{2,1,0:T(8,128)(2,1)}) custom-call(bf16[32,64,256]{2,1,0:T(8,128)(2,1)} %bitcast.13.inner_ref, bf16[32,64,256]{2,1,0:T(8,128)(2,1)} %bitcast.120, bf16[32,64,32]{2,1,0:T(8,128)(2,1)} %bitcast.124), custom_call_target="tpu_custom_call" | custom-call | tf_op jit(solution)/shard_map/mix_features/pallas_call | solution.py:74
  149.5 42.8 %all_to_all.36.d_ref = bf16[16,128,256]{2,1,0:T(8,128)(2,1)} all-to-all(bf16[16,128,256]{2,1,0:T(8,128)(2,1)} %bitcast.130), channel_id=1, replica_groups=mesh['zl'=4,'x'=4,'zh'=2,'y'=4,'c'=2] {'zh','y','c'}, dimensions={0} | all-to-all | bytes 2097152 | tf_op jit(solution)/shard_map/all_to_all | solution.py:16
  192.2 5.1 %shard_map.112 = (bf16[16,256,128]{2,1,0:T(8,128)(2,1)}, f32[16,256,128]{2,1,0:T(8,128)}) custom-call(bf16[16,256,128]{2,1,0:T(8,128)(2,1)} %bitcast.115, bf16[16,256,128]{2,1,0:T(8,128)(2,1)} %bitcast.10.mixed_ref, f32[1,128]{1,0:T(1,128)} %bitcast.132, f32[1,128]{1,0:T(1,128)} %bitcast.134, bf16[128,128]{1,0:T(8,128)(2,1)} %mul.23.panel_ref, ...), custom_call_target="tpu_custom_call" | custom-call | tf_op jit(solution)/shard_map/pallas_call | solution.py:127
  197.3 5.7 %all-to-all-start.4 = ((bf16[16,32,8,128]{3,2,1,0:T(8,128)(2,1)}), bf16[16,32,8,128]{3,2,1,0:T(8,128)(2,1)S(1)}, u32[]{:S(2)}, u32[]{:S(2)}) async-start(bf16[16,32,8,128]{3,2,1,0:T(8,128)(2,1)} %bitcast.128), calls=%async_computation.4 | async-start | bytes 2097152 | tf_op jit(solution)/shard_map/all_to_all | solution.py:16
  209.8 4.5 %collective-permute-done.14 = bf16[1,2,512,128]{3,2,1,0:T(8,128)(2,1)S(1)} collective-permute-done((bf16[1,2,512,128]{3,2,1,0:T(8,128)(2,1)S(1)}, bf16[1,2,512,128]{3,2,1,0:T(8,128)(2,1)S(1)}, u32[]{:S(2)}, u32[]{:S(2)}) %collective-permute-start.14) | collective-permute-done | bytes 262176 | tf_op jit(solution)/shard_map/ppermute | solution.py:28
  214.3 16.4 %collective-permute-done.5 = bf16[1,4,2,128,256]{4,3,2,1,0:T(8,128)(2,1)S(1)} collective-permute-done((bf16[1,4,2,128,256]{4,3,2,1,0:T(8,128)(2,1)S(1)}, bf16[1,4,2,128,256]{4,3,2,1,0:T(8,128)(2,1)S(1)}, u32[]{:S(2)}, u32[]{:S(2)}) %collective-permute-start.5) | collective-permute-done | bytes 524320 | tf_op jit(solution)/shard_map/ppermute | solution.py:28
  239.1 3.5 collective-permute-done.6
  243.4 8.1 %all-to-all-done.4 = bf16[16,32,8,128]{3,2,1,0:T(8,128)(2,1)S(1)} async-done(((bf16[16,32,8,128]{3,2,1,0:T(8,128)(2,1)}), bf16[16,32,8,128]{3,2,1,0:T(8,128)(2,1)S(1)}, u32[]{:S(2)}, u32[]{:S(2)}) %all-to-all-start.4) | async-done | bytes 1048608 | tf_op jit(solution)/shard_map/all_to_all | solution.py:16
  256.7 15.1 %all-to-all-start.5 = ((bf16[128,32,128]{2,1,0:T(8,128)(2,1)}), bf16[128,32,128]{2,1,0:T(8,128)(2,1)}, u32[]{:S(2)}, u32[]{:S(2)}) async-start(bf16[128,32,128]{2,1,0:T(8,128)(2,1)} %copy.64), calls=%async_computation.5 | async-start | bytes 2097152 | tf_op jit(solution)/shard_map/all_to_all | solution.py:16
  284.1 4.0 %collective-permute-done.18 = bf16[1,2,2,32,8,128]{5,4,1,0,2,3:T(8,128)(2,1)S(1)} collective-permute-done((bf16[1,2,2,32,8,128]{5,4,1,0,2,3:T(8,128)(2,1)S(1)}, bf16[1,2,2,32,8,128]{5,4,1,0,2,3:T(8,128)(2,1)S(1)}, u32[]{:S(2)}, u32[]{:S(2)}) %collective-permute-start.18) | collective-permute-done | bytes 262176 | tf_op jit(solution)/shard_map/ppermute | solution.py:28
  288.1 10.8 %collective-permute-done.19 = bf16[1,2,2,32,8,128]{5,4,1,0,2,3:T(8,128)(2,1)S(1)} collective-permute-done((bf16[1,2,2,32,8,128]{5,4,1,0,2,3:T(8,128)(2,1)S(1)}, bf16[1,2,2,32,8,128]{5,4,1,0,2,3:T(8,128)(2,1)S(1)}, u32[]{:S(2)}, u32[]{:S(2)}) %collective-permute-start.19) | collective-permute-done | bytes 262176 | tf_op jit(solution)/shard_map/ppermute | solution.py:28
  310.1 5.4 %collective-permute-start.22 = (f32[32,8,128]{2,1,0:T(8,128)}, f32[32,8,128]{2,1,0:T(8,128)S(1)}, u32[]{:S(2)}, u32[]{:S(2)}) collective-permute-start(f32[32,8,128]{2,1,0:T(8,128)} %dynamic-slice_bitcast_fusion), channel_id=1, source_target_pairs={{0,8},{8,0},{1,9},{9,1},{2,10},{10,2},{3,11},{11,3},{4,12},{12,4},... | collective-permute-start | bytes 393224 | tf_op jit(solution)/shard_map/ppermute | solution.py:236
  326.6 4.4 %all-to-all-start.6 = ((bf16[16,32,512]{2,1,0:T(8,128)(2,1)}), bf16[16,32,512]{2,1,0:T(8,128)(2,1)}, u32[]{:S(2)}, u32[]{:S(2)}) async-start(bf16[16,32,512]{2,1,0:T(8,128)(2,1)} %fusion.4), calls=%async_computation.6 | async-start | bytes 1048576 | tf_op jit(solution)/shard_map/all_to_all | solution.py:16
  334.3 3.4 collective-permute-done.12
  344.5 3.9 %finish.1 = bf16[4096,128]{1,0:T(8,128)(2,1)} custom-call(bf16[4096,128]{1,0:T(8,128)(2,1)} %bitcast.113, f32[4096,128]{1,0:T(8,128)} %bitcast.118), custom_call_target="tpu_custom_call" | custom-call | tf_op jit(solution)/shard_map/finish/pallas_call | solution.py:145
  (133 shorter events, 99.2 us)
Async XLA Ops:
  44.4 55.4 %all-to-all-start.1 = ((bf16[16,32,8,128]{3,2,1,0:T(8,128)(2,1)}), bf16[16,32,8,128]{3,2,1,0:T(8,128)(2,1)}, u32[]{:S(2)}, u32[]{:S(2)}) async-start(bf16[16,32,8,128]{3,2,1,0:T(8,128)(2,1)} %bitcast.103), calls=%async_computation.1 | async-start | bytes 2097152 | tf_op jit(solution)/shard_map/all_to_all | solution.py:16
  56.1 56.6 %collective-permute-start = (bf16[1,4,2,144,256]{4,3,2,1,0:T(8,128)(2,1)}, bf16[1,4,2,144,256]{4,3,2,1,0:T(8,128)(2,1)}, u32[]{:S(2)}, u32[]{:S(2)}) collective-permute-start(bf16[1,4,2,144,256]{4,3,2,1,0:T(8,128)(2,1)} %constant_dynamic-slice_fusion.22), channel_id=1, source_target_pairs={{0,8},{8,0},{1,9},{9,1},{2,10},{10,2},{3,11},{11,3},{4,12},{12,4},... | collective-permute-start | bytes 1769480 | tf_op jit(solution)/shard_map/ppermute | solution.py:28
  104.1 40.1 %all-to-all-start.2 = ((bf16[16,128,256]{2,1,0:T(8,128)(2,1)}), bf16[16,128,256]{2,1,0:T(8,128)(2,1)}, u32[]{:S(2)}, u32[]{:S(2)}) async-start(bf16[16,128,256]{2,1,0:T(8,128)(2,1)} %get-tuple-element.26), calls=%async_computation.2 | async-start | bytes 2097152 | tf_op jit(solution)/shard_map/all_to_all | solution.py:16
  114.7 13.7 %collective-permute-start.1 = (bf16[2,1,2,144,256]{4,3,2,1,0:T(8,128)(2,1)}, bf16[2,1,2,144,256]{4,3,2,1,0:T(8,128)(2,1)}, u32[]{:S(2)}, u32[]{:S(2)}) collective-permute-start(bf16[2,1,2,144,256]{4,3,2,1,0:T(8,128)(2,1)} %get-tuple-element.27), channel_id=1, source_target_pairs={{0,2},{2,0},{4,6},{6,4},{1,3},{3,1},{5,7},{7,5},{8,10},{10,8},{12,... | collective-permute-start | bytes 884744 | tf_op jit(solution)/shard_map/ppermute | solution.py:28
  116.6 20.5 %collective-permute-start.2 = (bf16[2,1,2,144,256]{4,3,2,1,0:T(8,128)(2,1)}, bf16[2,1,2,144,256]{4,3,2,1,0:T(8,128)(2,1)}, u32[]{:S(2)}, u32[]{:S(2)}) collective-permute-start(bf16[2,1,2,144,256]{4,3,2,1,0:T(8,128)(2,1)} %get-tuple-element.28), channel_id=1, source_target_pairs={{0,4},{2,6},{4,0},{6,2},{1,5},{3,7},{5,1},{7,3},{8,12},{10,14},{12... | collective-permute-start | bytes 884744 | tf_op jit(solution)/shard_map/ppermute | solution.py:28
  119.3 18.8 %collective-permute-start.3 = (bf16[2,1,2,144,256]{4,3,2,1,0:T(8,128)(2,1)}, bf16[2,1,2,144,256]{4,3,2,1,0:T(8,128)(2,1)}, u32[]{:S(2)}, u32[]{:S(2)}) collective-permute-start(bf16[2,1,2,144,256]{4,3,2,1,0:T(8,128)(2,1)} %get-tuple-element.29), channel_id=1, source_target_pairs={{0,6},{2,4},{4,2},{6,0},{1,7},{3,5},{5,3},{7,1},{8,14},{10,12},{12... | collective-permute-start | bytes 884744 | tf_op jit(solution)/shard_map/ppermute | solution.py:28
  197.3 54.1 %all-to-all-start.4 = ((bf16[16,32,8,128]{3,2,1,0:T(8,128)(2,1)}), bf16[16,32,8,128]{3,2,1,0:T(8,128)(2,1)S(1)}, u32[]{:S(2)}, u32[]{:S(2)}) async-start(bf16[16,32,8,128]{3,2,1,0:T(8,128)(2,1)} %bitcast.128), calls=%async_computation.4 | async-start | bytes 2097152 | tf_op jit(solution)/shard_map/all_to_all | solution.py:16
  204.1 26.6 %collective-permute-start.5 = (bf16[1,4,2,128,256]{4,3,2,1,0:T(8,128)(2,1)S(1)}, bf16[1,4,2,128,256]{4,3,2,1,0:T(8,128)(2,1)S(1)}, u32[]{:S(2)}, u32[]{:S(2)}) collective-permute-start(bf16[1,4,2,128,256]{4,3,2,1,0:T(8,128)(2,1)S(1)} %constant_dynamic-slice_fusion.17), channel_id=1, source_target_pairs={{0,8},{8,0},{1,9},{9,1},{2,10},{10,2},{3,11},{11,3},{4,12},{12,4},... | collective-permute-start | bytes 1572872 | tf_op jit(solution)/shard_map/ppermute | solution.py:28
  204.8 9.4 %collective-permute-start.14 = (bf16[1,2,512,128]{3,2,1,0:T(8,128)(2,1)S(1)}, bf16[1,2,512,128]{3,2,1,0:T(8,128)(2,1)S(1)}, u32[]{:S(2)}, u32[]{:S(2)}) collective-permute-start(bf16[1,2,512,128]{3,2,1,0:T(8,128)(2,1)S(1)} %get-tuple-element.40), channel_id=1, source_target_pairs={{0,2},{2,0},{4,6},{6,4},{1,3},{3,1},{5,7},{7,5},{8,10},{10,8},{12,... | collective-permute-start | bytes 786440 | tf_op jit(solution)/shard_map/ppermute | solution.py:28
  205.1 28.4 %collective-permute-start.15 = (bf16[1,2,512,128]{3,2,1,0:T(8,128)(2,1)S(1)}, bf16[1,2,512,128]{3,2,1,0:T(8,128)(2,1)S(1)}, u32[]{:S(2)}, u32[]{:S(2)}) collective-permute-start(bf16[1,2,512,128]{3,2,1,0:T(8,128)(2,1)S(1)} %get-tuple-element.41), channel_id=1, source_target_pairs={{0,4},{2,6},{4,0},{6,2},{1,5},{3,7},{5,1},{7,3},{8,12},{10,14},{12... | collective-permute-start | bytes 786440 | tf_op jit(solution)/shard_map/ppermute | solution.py:28
  208.0 25.5 %collective-permute-start.16 = (bf16[1,2,512,128]{3,2,1,0:T(8,128)(2,1)S(1)}, bf16[1,2,512,128]{3,2,1,0:T(8,128)(2,1)S(1)}, u32[]{:S(2)}, u32[]{:S(2)}) collective-permute-start(bf16[1,2,512,128]{3,2,1,0:T(8,128)(2,1)S(1)} %get-tuple-element.42), channel_id=1, source_target_pairs={{0,6},{2,4},{4,2},{6,0},{1,7},{3,5},{5,3},{7,1},{8,14},{10,12},{12... | collective-permute-start | bytes 786440 | tf_op jit(solution)/shard_map/ppermute | solution.py:28
  234.4 69.0 %collective-permute-start.17 = (bf16[4,1,512,128]{3,2,1,0:T(8,128)(2,1)}, bf16[4,1,512,128]{3,2,1,0:T(8,128)(2,1)}, u32[]{:S(2)}, u32[]{:S(2)}) collective-permute-start(bf16[4,1,512,128]{3,2,1,0:T(8,128)(2,1)} %constant_dynamic-slice_fusion.4), channel_id=1, source_target_pairs={{0,1},{1,0},{2,3},{3,2},{4,5},{5,4},{6,7},{7,6},{8,9},{9,8},{10,11... | collective-permute-start | bytes 1572872 | tf_op jit(solution)/shard_map/ppermute | solution.py:28
  234.4 41.2 %collective-permute-start.7 = (bf16[2,1,2,128,256]{4,3,2,1,0:T(8,128)(2,1)}, bf16[2,1,2,128,256]{4,3,2,1,0:T(8,128)(2,1)}, u32[]{:S(2)}, u32[]{:S(2)}) collective-permute-start(bf16[2,1,2,128,256]{4,3,2,1,0:T(8,128)(2,1)} %get-tuple-element.32), channel_id=1, source_target_pairs={{0,4},{2,6},{4,0},{6,2},{1,5},{3,7},{5,1},{7,3},{8,12},{10,14},{12... | collective-permute-start | bytes 786440 | tf_op jit(solution)/shard_map/ppermute | solution.py:28
  237.3 42.7 %collective-permute-start.8 = (bf16[2,1,2,128,256]{4,3,2,1,0:T(8,128)(2,1)S(1)}, bf16[2,1,2,128,256]{4,3,2,1,0:T(8,128)(2,1)}, u32[]{:S(2)}, u32[]{:S(2)}) collective-permute-start(bf16[2,1,2,128,256]{4,3,2,1,0:T(8,128)(2,1)S(1)} %get-tuple-element.33), channel_id=1, source_target_pairs={{0,6},{2,4},{4,2},{6,0},{1,7},{3,5},{5,3},{7,1},{8,14},{10,12},{12... | collective-permute-start | bytes 786440 | tf_op jit(solution)/shard_map/ppermute | solution.py:28
  256.7 58.9 %all-to-all-start.5 = ((bf16[128,32,128]{2,1,0:T(8,128)(2,1)}), bf16[128,32,128]{2,1,0:T(8,128)(2,1)}, u32[]{:S(2)}, u32[]{:S(2)}) async-start(bf16[128,32,128]{2,1,0:T(8,128)(2,1)} %copy.64), calls=%async_computation.5 | async-start | bytes 2097152 | tf_op jit(solution)/shard_map/all_to_all | solution.py:16
  274.0 14.0 %collective-permute-start.18 = (bf16[1,2,2,32,8,128]{5,4,1,0,2,3:T(8,128)(2,1)S(1)}, bf16[1,2,2,32,8,128]{5,4,1,0,2,3:T(8,128)(2,1)S(1)}, u32[]{:S(2)}, u32[]{:S(2)}) collective-permute-start(bf16[1,2,2,32,8,128]{5,4,1,0,2,3:T(8,128)(2,1)S(1)} %get-tuple-element.43), channel_id=1, source_target_pairs={{0,2},{2,0},{4,6},{6,4},{1,3},{3,1},{5,7},{7,5},{8,10},{10,8},{12,... | collective-permute-start | bytes 786440 | tf_op jit(solution)/shard_map/ppermute | solution.py:28
  277.3 21.6 %collective-permute-start.19 = (bf16[1,2,2,32,8,128]{5,4,1,0,2,3:T(8,128)(2,1)S(1)}, bf16[1,2,2,32,8,128]{5,4,1,0,2,3:T(8,128)(2,1)S(1)}, u32[]{:S(2)}, u32[]{:S(2)}) collective-permute-start(bf16[1,2,2,32,8,128]{5,4,1,0,2,3:T(8,128)(2,1)S(1)} %get-tuple-element.44), channel_id=1, source_target_pairs={{0,4},{2,6},{4,0},{6,2},{1,5},{3,7},{5,1},{7,3},{8,12},{10,14},{12... | collective-permute-start | bytes 786440 | tf_op jit(solution)/shard_map/ppermute | solution.py:28
  281.7 19.8 %collective-permute-start.20 = (bf16[1,2,2,32,8,128]{5,4,1,0,2,3:T(8,128)(2,1)S(1)}, bf16[1,2,2,32,8,128]{5,4,1,0,2,3:T(8,128)(2,1)S(1)}, u32[]{:S(2)}, u32[]{:S(2)}) collective-permute-start(bf16[1,2,2,32,8,128]{5,4,1,0,2,3:T(8,128)(2,1)S(1)} %get-tuple-element.45), channel_id=1, source_target_pairs={{0,6},{2,4},{4,2},{6,0},{1,7},{3,5},{5,3},{7,1},{8,14},{10,12},{12... | collective-permute-start | bytes 786440 | tf_op jit(solution)/shard_map/ppermute | solution.py:28
  284.1 20.6 %collective-permute-start.9 = (bf16[2,4,1,128,256]{4,3,2,1,0:T(8,128)(2,1)}, bf16[2,4,1,128,256]{4,3,2,1,0:T(8,128)(2,1)S(1)}, u32[]{:S(2)}, u32[]{:S(2)}) collective-permute-start(bf16[2,4,1,128,256]{4,3,2,1,0:T(8,128)(2,1)} %constant_dynamic-slice_fusion.13), channel_id=1, source_target_pairs={{0,1},{1,0},{2,3},{3,2},{4,5},{5,4},{6,7},{7,6},{8,9},{9,8},{10,11... | collective-permute-start | bytes 1572872 | tf_op jit(solution)/shard_map/ppermute | solution.py:28
  310.1 32.7 %collective-permute-start.22 = (f32[32,8,128]{2,1,0:T(8,128)}, f32[32,8,128]{2,1,0:T(8,128)S(1)}, u32[]{:S(2)}, u32[]{:S(2)}) collective-permute-start(f32[32,8,128]{2,1,0:T(8,128)} %dynamic-slice_bitcast_fusion), channel_id=1, source_target_pairs={{0,8},{8,0},{1,9},{9,1},{2,10},{10,2},{3,11},{11,3},{4,12},{12,4},... | collective-permute-start | bytes 393224 | tf_op jit(solution)/shard_map/ppermute | solution.py:236
  319.1 11.8 %collective-permute-start.10 = (bf16[1,2,512,128]{3,2,1,0:T(8,128)(2,1)}, bf16[1,2,512,128]{3,2,1,0:T(8,128)(2,1)}, u32[]{:S(2)}, u32[]{:S(2)}) collective-permute-start(bf16[1,2,512,128]{3,2,1,0:T(8,128)(2,1)} %get-tuple-element.36), channel_id=1, source_target_pairs={{0,2},{2,0},{4,6},{6,4},{1,3},{3,1},{5,7},{7,5},{8,10},{10,8},{12,... | collective-permute-start | bytes 786440 | tf_op jit(solution)/shard_map/ppermute | solution.py:28
  319.1 14.2 %collective-permute-start.11 = (bf16[1,2,512,128]{3,2,1,0:T(8,128)(2,1)}, bf16[1,2,512,128]{3,2,1,0:T(8,128)(2,1)}, u32[]{:S(2)}, u32[]{:S(2)}) collective-permute-start(bf16[1,2,512,128]{3,2,1,0:T(8,128)(2,1)} %get-tuple-element.37), channel_id=1, source_target_pairs={{0,4},{2,6},{4,0},{6,2},{1,5},{3,7},{5,1},{7,3},{8,12},{10,14},{12... | collective-permute-start | bytes 786440 | tf_op jit(solution)/shard_map/ppermute | solution.py:28
  320.8 16.8 %collective-permute-start.12 = (bf16[1,2,512,128]{3,2,1,0:T(8,128)(2,1)}, bf16[1,2,512,128]{3,2,1,0:T(8,128)(2,1)}, u32[]{:S(2)}, u32[]{:S(2)}) collective-permute-start(bf16[1,2,512,128]{3,2,1,0:T(8,128)(2,1)} %get-tuple-element.38), channel_id=1, source_target_pairs={{0,6},{2,4},{4,2},{6,0},{1,7},{3,5},{5,3},{7,1},{8,14},{10,12},{12... | collective-permute-start | bytes 786440 | tf_op jit(solution)/shard_map/ppermute | solution.py:28
  326.6 24.7 %all-to-all-start.6 = ((bf16[16,32,512]{2,1,0:T(8,128)(2,1)}), bf16[16,32,512]{2,1,0:T(8,128)(2,1)}, u32[]{:S(2)}, u32[]{:S(2)}) async-start(bf16[16,32,512]{2,1,0:T(8,128)(2,1)} %fusion.4), calls=%async_computation.6 | async-start | bytes 1048576 | tf_op jit(solution)/shard_map/all_to_all | solution.py:16
  (17 other events, 138.2 us)

commit v5 on v4

--- a/solution.py
+++ b/solution.py
@@ -2,6 +2,7 @@
 import jax.numpy as jnp
 from jax import lax
 from jax.experimental import pallas as pl
+from jax.experimental.pallas import tpu as pltpu
 from jax.sharding import Mesh
 from jax.sharding import PartitionSpec as P
 
@@ -16,7 +17,7 @@
     return lax.all_to_all(value, axes, split_axis=0, concat_axis=0, tiled=True)
 
 
-def turn(value, axis, dim):
+def trade(value, axis, dim):
     size, me = lax.axis_size(axis), lax.axis_index(axis)
     parts = [
         lax.dynamic_index_in_dim(value, me ^ r, dim, keepdims=True) for r in range(1, size)
@@ -26,6 +27,30 @@
     got = []
     for r in range(1, size):
         got.append(lax.ppermute(parts[r - 1], axis, [(s, s ^ r) for s in range(size)]))
+    return got
+
+
+def fold(value, axis, dim):
+    got = trade(value, axis, dim)
+    total = lax.dynamic_index_in_dim(value, lax.axis_index(axis), dim).astype(F32)
+    for part in got:
+        total = total + part.astype(F32)
+    return total.squeeze(dim)
+
+
+def gather(value, axis):
+    size, me = lax.axis_size(axis), lax.axis_index(axis)
+    whole = jnp.zeros((size,) + value.shape, value.dtype)
+    whole = lax.dynamic_update_index_in_dim(whole, value, me, 0)
+    for r in range(1, size):
+        other = lax.ppermute(value, axis, [(s, s ^ r) for s in range(size)])
+        whole = lax.dynamic_update_index_in_dim(whole, other, me ^ r, 0)
+    return whole
+
+
+def turn(value, axis, dim):
+    size, me = lax.axis_size(axis), lax.axis_index(axis)
+    got = trade(value, axis, dim)
     for r in range(1, size):
         value = lax.dynamic_update_slice_in_dim(value, got[r - 1], me ^ r, dim)
     return value
@@ -135,6 +160,56 @@
     )(x, mixed, scale.reshape(1, width), bias.reshape(1, width), panel, *more)
 
 
+def close_kernel(d_ref, own_ref, x_ref, prod_ref, part_ref, total):
+    step, (owners, here, offs, width) = pl.program_id(0), d_ref.shape
+    height = owners * offs
+    d_wide = jnp.concatenate([d_ref[:, k].reshape(height, width) for k in range(here)], axis=1)
+    x_wide = jnp.concatenate([x_ref[k] for k in range(here)], axis=1)
+    more = lax.dot_general(
+        d_wide, x_wide, (((1,), (1,)), ((), ())), preferred_element_type=F32
+    )
+    part = lax.dot_general(
+        own_ref[...], d_wide, (((0,), (0,)), ((), ())), preferred_element_type=F32
+    ).astype(BF16)
+    for k in range(here):
+        part_ref[k] = part[:, k * width : (k + 1) * width]
+
+    @pl.when(step == 0)
+    def _():
+        total[...] = more
+
+    @pl.when(step > 0)
+    def _():
+        total[...] += more
+
+    @pl.when(step == pl.num_programs(0) - 1)
+    def _():
+        prod_ref[...] = total[...].astype(BF16)
+
+
+def close(d_first, own, x_plane):
+    owners, plane, offs, width = d_first.shape
+    height, here = owners * offs, 2
+    square = pl.BlockSpec((height, height), lambda g: (0, 0))
+    slab = pl.BlockSpec((here, height, width), lambda g: (g, 0, 0))
+    return pl.pallas_call(
+        close_kernel,
+        out_shape=(
+            jax.ShapeDtypeStruct((height, height), BF16),
+            jax.ShapeDtypeStruct((plane, height, width), BF16),
+        ),
+        grid=(plane // here,),
+        in_specs=[
+            pl.BlockSpec((owners, here, offs, width), lambda g: (0, g, 0, 0)),
+            square,
+            slab,
+        ],
+        out_specs=(square, slab),
+        scratch_shapes=[pltpu.VMEM((height, height), F32)],
+        name="close",
+    )(d_first, own, x_plane)
+
+
 def finish_kernel(part_ref, local_ref, out_ref):
     out_ref[...] = (part_ref[...].astype(F32) + local_ref[...]).astype(BF16)
 
@@ -165,7 +240,6 @@
     n_seq, n_hid = lax.axis_size(SEQ), lax.axis_size(HID)
     n_plane = lax.axis_size(PLANE)
     halves = n_hid // n_plane
-    zh = lax.axis_index("zh")
     rows, width = tokens.shape
     blocks, block = seq_first.shape[0], seq_first.shape[1]
     offs, nb = seq_second.shape[0], seq_second.shape[1]
@@ -183,15 +257,16 @@
 
     x_rows = x_blocks.transpose(1, 0, 2).reshape(wide)
     cot_rows = cotangent.reshape(blocks, block, width).transpose(1, 0, 2).reshape(wide)
-    small = feature_second_blocks.reshape(1, -1, count)
-    small = jnp.broadcast_to(small, (n_hid,) + small.shape[1:])
-    sent = jnp.concatenate([cot_rows.transpose(0, 2, 1), small], axis=1)
+    small = feature_second_blocks.reshape(-1, width)
+    sent = cot_rows.transpose(0, 2, 1)
     eye = jnp.eye(groups, dtype=BF16)
     panel = (feat_first[:, :, None, :] * eye[:, None, :, None]).reshape(width, width)
     got = swap(sent, HID)
     x_plane = swap(x_blocks, PLANE)
-    cot_moved = got[:, :width].reshape(by_panel)
-    second_all = got[:, width:].reshape(group, panels, panels)
+    cot_moved = got.reshape(by_panel)
+    for axis in ("c", "y", "zh"):
+        small = gather(small, axis)
+    second_all = small.reshape(group, panels, panels)
 
     strided = first.transpose(1, 0, 2, 3).reshape(offs, nb, width)
     mixed_j = dot("jab,jbc->jac", seq_second, strided).astype(BF16)
@@ -228,22 +303,17 @@
     d_first = move(d_first_j, SEQ + PLANE).reshape(n_seq, n_plane, offs, width)
 
     part = dot("jac,jbc->jab", d_mixed_j, strided).astype(BF16)
-    part = part.reshape(offs, halves, n_plane, nb // n_hid, nb)
-    part = swap(part.transpose(2, 1, 0, 3, 4), PLANE)
-    part = part.astype(F32).sum(0)
-    keep = lax.dynamic_index_in_dim(part, zh, 0, keepdims=False)
-    send = lax.dynamic_index_in_dim(part, 1 - zh, 0, keepdims=False)
-    second_grad = keep + lax.ppermute(send, "zh", [(0, 1), (1, 0)])
-
-    prod = dot("spjc,pkc->sjk", d_first, x_plane).astype(BF16)
+    part = part.reshape(offs, halves, n_plane, nb // n_hid, nb).transpose(2, 1, 0, 3, 4)
+    part = part.reshape((lax.axis_size("y"), lax.axis_size("c")) + part.shape[1:])
+    part = fold(part, "c", 1).astype(BF16)
+    part = fold(part, "y", 0)
+    second_grad = fold(part, "zh", 0)
+
+    own = lax.dynamic_index_in_dim(seq_first, lax.axis_index(PLANE), 0, keepdims=False)
+    prod, seq_part = close(d_first, own, x_plane)
+    seq_part = swap(seq_part, PLANE).reshape(rows, width)
     prod = move(prod.reshape(n_hid, offs, block), HID)
-    prod = prod.reshape(halves, n_plane, offs, block).astype(F32)
-    first_grad = prod[0] + prod[1]
-
-    own = lax.dynamic_index_in_dim(seq_first, lax.axis_index(PLANE), 0, keepdims=False)
-    own = own.reshape(n_seq, offs, block)
-    seq_part = dot("sjk,spjc->pkc", own, d_first).astype(BF16)
-    seq_part = swap(seq_part, PLANE).reshape(rows, width)
+    first_grad = prod.reshape(halves, n_plane, offs, block).astype(F32).sum(0)
 
     def whole(value):
         return value.reshape(block, blocks, width).transpose(1, 0, 2).reshape(rows, width)

time: 355 us -> 356 us (level)
  matrix products: 13.4 us -> 7.54 us
  starting transfers between devices: 73.4 us -> 78.6 us
  Pallas kernels: 18.5 us -> 23.6 us
  blocking collectives: 77.1 us -> 73.5 us
    ppermute x23 -> x28, starting transfers between devices: 34.6 us -> 45.4 us  [the longest x23 31.6 us: trade(): lax.ppermute(parts[r - 1], axis, [(s, s ^ r) for s in range(size)])]
    ppermute x23 -> x28, waiting for transfers between devices: 65 us -> 58.7 us  [the longest x23 54.7 us: trade(): lax.ppermute(parts[r - 1], axis, [(s, s ^ r) for s in range(size)])]
    dot_general x6 -> x4, matrix products: 13.4 us -> 7.54 us  [dot(): return jnp.einsum(spec, left, right, preferred_element_type=F32)]
    all_to_all x5, starting transfers between devices: 38.8 us -> 33.2 us  [move(): return lax.all_to_all(value, axes, split_axis=0, concat_axis=0, tiled=True)]
    pallas_call x0 -> x1, Pallas kernels: none -> 4.99 us  [close(): pl.pallas_call(close_kernel, out_shape=(jax.ShapeDtypeStruct((height, hei...]
    all_to_all x5, waiting for transfers between devices: 47.7 us -> 52.2 us  [move(): return lax.all_to_all(value, axes, split_axis=0, concat_axis=0, tiled=True)]
    all_to_all x2, blocking collectives: 77.1 us -> 73.5 us  [move(): return lax.all_to_all(value, axes, split_axis=0, concat_axis=0, tiled=True)]
    dynamic_update_slice x22 -> x19, local copies, waits for them, and re-layouts: 15.5 us -> 14.6 us  [turn(): value = lax.dynamic_update_slice_in_dim(value, got[r - 1], me ^ r, dim)]
  transfers between devices with their start and end apart: 28 -> 33, of which waited for: 14 -> 10; matrix products, arithmetic and copies ran while one was open for 16% -> 14% of each run, Pallas kernels for 2% -> 4%
where the time goes in v5:
time: 356 us; the launch traced here: 352 us
  waiting for transfers between devices  111 us (31%)
  starting transfers between devices  78.6 us (22%)
  blocking collectives  73.5 us (21%)
  local copies, waits for them, and re-layouts  52.3 us (15%)
  Pallas kernels  23.6 us (7%)
  matrix products  7.54 us (2%)
  other arithmetic  4.47 us (1%)
    all_to_all x2, blocking collectives, move(): return lax.all_to_all(value, axes, split_axis=0, concat_axis=0, tiled=True)  73.5 us
    ppermute x23, waiting for transfers between devices, trade(): lax.ppermute(parts[r - 1], axis, [(s, s ^ r) for s in range(size)])  54.7 us
    all_to_all x5, waiting for transfers between devices, move(): return lax.all_to_all(value, axes, split_axis=0, concat_axis=0, tiled=True)  52.2 us
    all_to_all x5, starting transfers between devices, move(): return lax.all_to_all(value, axes, split_axis=0, concat_axis=0, tiled=True)  33.2 us
    ppermute x23, starting transfers between devices, trade(): lax.ppermute(parts[r - 1], axis, [(s, s ^ r) for s in range(size)])  31.6 us
    dynamic_update_slice x19, local copies, waits for them, and re-layouts, turn(): value = lax.dynamic_update_slice_in_dim(value, got[r - 1], me ^ r, dim)  14.6 us
    ppermute x5, starting transfers between devices, gather(): other = lax.ppermute(value, axis, [(s, s ^ r) for s in range(size)])  13.8 us
    dynamic_slice x12, local copies, waits for them, and re-layouts, trade(): lax.dynamic_index_in_dim(value, me ^ r, dim, keepdims=True)  10.2 us
  transfers between devices with their start and end apart: 33, of which 10 were waited for; matrix products, arithmetic and copies ran while one was open for 14% of the time, Pallas kernels for 4%

profile of v5, /device:TPU:32, one launch (start us, length us, event | category | flops | bytes accessed | tf_op | source)
XLA Modules:
  0.0 351.9 jit_solution(13249416901269934509)
XLA Ops:
  2.0 4.7 %fusion.1 = bf16[512,8,128]{0,2,1:T(8,128)(2,1)} fusion(bf16[8,512,128]{2,1,0:T(8,128)(2,1)S(1)} %bitcast.118, bf16[8,512,512]{2,1,0:T(8,128)(2,1)} %param.10), kind=kOutput, calls=%fused_computation.6 | convolution fusion | flops 537395200 | bytes 6291456 | tf_op jit(solution)/shard_map/qkj,qjc->kqc/dot_general | solution.py:68
  8.4 34.3 %all_to_all.35 = bf16[16,32,8,128]{3,2,1,0:T(8,128)(2,1)S(1)} all-to-all(bf16[16,32,8,128]{3,2,1,0:T(8,128)(2,1)S(1)} %bitcast.136), channel_id=1, replica_groups=mesh['zl'=4,'x'=4,'zh'=2,'y'=4,'c'=2] {'zl','x'}, dimensions={0} | all-to-all | bytes 2097152 | tf_op jit(solution)/shard_map/all_to_all | solution.py:17
  44.4 5.1 %all-to-all-start.1 = ((bf16[16,32,8,128]{3,2,1,0:T(8,128)(2,1)}), bf16[16,32,8,128]{3,2,1,0:T(8,128)(2,1)}, u32[]{:S(2)}, u32[]{:S(2)}) async-start(bf16[16,32,8,128]{3,2,1,0:T(8,128)(2,1)} %bitcast.117), calls=%async_computation.1 | async-start | bytes 2097152 | tf_op jit(solution)/shard_map/all_to_all | solution.py:17
  52.3 4.5 %collective-permute-start = (bf16[1,4,2,128,256]{3,4,2,1,0:T(8,128)(2,1)}, bf16[1,4,2,128,256]{3,4,2,1,0:T(8,128)(2,1)}, u32[]{:S(2)}, u32[]{:S(2)}) collective-permute-start(bf16[1,4,2,128,256]{3,4,2,1,0:T(8,128)(2,1)} %constant_dynamic-slice_fusion.19), channel_id=1, source_target_pairs={{0,8},{8,0},{1,9},{9,1},{2,10},{10,2},{3,11},{11,3},{4,12},{12,4},... | collective-permute-start | bytes 1572872 | tf_op jit(solution)/shard_map/ppermute | solution.py:29
  65.3 31.7 %all-to-all-done.1 = bf16[16,32,8,128]{3,2,1,0:T(8,128)(2,1)} async-done(((bf16[16,32,8,128]{3,2,1,0:T(8,128)(2,1)}), bf16[16,32,8,128]{3,2,1,0:T(8,128)(2,1)}, u32[]{:S(2)}, u32[]{:S(2)}) %all-to-all-start.1) | async-done | bytes 1048608 | tf_op jit(solution)/shard_map/all_to_all | solution.py:17
  97.0 4.4 %shard_map.111 = (bf16[16,256,128]{2,1,0:T(8,128)(2,1)}, bf16[16,128,256]{2,1,0:T(8,128)(2,1)}) custom-call(bf16[16,256,128]{2,1,0:T(8,128)(2,1)} %bitcast.126, bf16[16,256,128]{2,1,0:T(8,128)(2,1)} %bitcast.10.mixed_ref, f32[1,128]{1,0:T(1,128)} %bitcast.145, f32[1,128]{1,0:T(1,128)} %bitcast.147, bf16[128,128]{1,0:T(8,128)(2,1)} %mul.23.panel_ref), custom_call_target="tpu_custom_call" | custom-call | tf_op jit(solution)/shard_map/pallas_call | solution.py:152
  101.4 8.6 %all-to-all-start.2 = ((bf16[16,128,256]{2,1,0:T(8,128)(2,1)}), bf16[16,128,256]{2,1,0:T(8,128)(2,1)}, u32[]{:S(2)}, u32[]{:S(2)}) async-start(bf16[16,128,256]{2,1,0:T(8,128)(2,1)} %get-tuple-element.28), calls=%async_computation.2 | async-start | bytes 2097152 | tf_op jit(solution)/shard_map/all_to_all | solution.py:17
  116.0 8.9 %collective-permute-done.1 = bf16[2,1,2,128,256]{3,4,2,1,0:T(8,128)(2,1)S(1)} collective-permute-done((bf16[2,1,2,128,256]{3,4,2,1,0:T(8,128)(2,1)S(1)}, bf16[2,1,2,128,256]{3,4,2,1,0:T(8,128)(2,1)S(1)}, u32[]{:S(2)}, u32[]{:S(2)}) %collective-permute-start.1) | collective-permute-done | bytes 262176 | tf_op jit(solution)/shard_map/ppermute | solution.py:29
  125.0 7.8 %collective-permute-done.2 = bf16[2,1,2,128,256]{3,4,2,1,0:T(8,128)(2,1)S(1)} collective-permute-done((bf16[2,1,2,128,256]{3,4,2,1,0:T(8,128)(2,1)S(1)}, bf16[2,1,2,128,256]{3,4,2,1,0:T(8,128)(2,1)S(1)}, u32[]{:S(2)}, u32[]{:S(2)}) %collective-permute-start.2) | collective-permute-done | bytes 262176 | tf_op jit(solution)/shard_map/ppermute | solution.py:29
  133.7 9.1 %collective-permute-start.9 = (bf16[4,2,32,128]{3,2,1,0:T(8,128)(2,1)S(1)}, bf16[4,2,32,128]{3,2,1,0:T(8,128)(2,1)S(1)}, u32[]{:S(2)}, u32[]{:S(2)}) collective-permute-start(bf16[4,2,32,128]{3,2,1,0:T(8,128)(2,1)S(1)} %bitcast_dynamic-update-slice_fusion.2), channel_id=1, source_target_pairs={{0,8},{8,0},{1,9},{9,1},{2,10},{10,2},{3,11},{11,3},{4,12},{12,4},... | collective-permute-start | bytes 196616 | tf_op jit(solution)/shard_map/ppermute | solution.py:46
  142.8 4.0 %collective-permute-done.9 = bf16[4,2,32,128]{3,2,1,0:T(8,128)(2,1)S(1)} collective-permute-done((bf16[4,2,32,128]{3,2,1,0:T(8,128)(2,1)S(1)}, bf16[4,2,32,128]{3,2,1,0:T(8,128)(2,1)S(1)}, u32[]{:S(2)}, u32[]{:S(2)}) %collective-permute-start.9) | collective-permute-done | bytes 65568 | tf_op jit(solution)/shard_map/ppermute | solution.py:46
  153.0 5.3 %mix_features.1 = (bf16[32,64,256]{2,1,0:T(8,128)(2,1)}, bf16[32,64,256]{2,1,0:T(8,128)(2,1)}) custom-call(bf16[32,64,256]{2,1,0:T(8,128)(2,1)} %bitcast.13.inner_ref, bf16[32,64,256]{2,1,0:T(8,128)(2,1)} %bitcast.135, bf16[32,64,32]{2,1,0:T(8,128)(2,1)} %bitcast.138), custom_call_target="tpu_custom_call" | custom-call | tf_op jit(solution)/shard_map/mix_features/pallas_call | solution.py:99
  158.3 39.2 %all_to_all.36.d_ref = bf16[16,128,256]{2,1,0:T(8,128)(2,1)} all-to-all(bf16[16,128,256]{2,1,0:T(8,128)(2,1)} %bitcast.143), channel_id=1, replica_groups=mesh['zl'=4,'x'=4,'zh'=2,'y'=4,'c'=2] {'zh','y','c'}, dimensions={0} | all-to-all | bytes 2097152 | tf_op jit(solution)/shard_map/all_to_all | solution.py:17
  197.5 5.1 %shard_map.112 = (bf16[16,256,128]{2,1,0:T(8,128)(2,1)}, f32[16,256,128]{2,1,0:T(8,128)}) custom-call(bf16[16,256,128]{2,1,0:T(8,128)(2,1)} %bitcast.127, bf16[16,256,128]{2,1,0:T(8,128)(2,1)} %bitcast.10.mixed_ref, f32[1,128]{1,0:T(1,128)} %bitcast.146, f32[1,128]{1,0:T(1,128)} %bitcast.148, bf16[128,128]{1,0:T(8,128)(2,1)} %mul.23.panel_ref, ...), custom_call_target="tpu_custom_call" | custom-call | tf_op jit(solution)/shard_map/pallas_call | solution.py:152
  202.6 5.5 %all-to-all-start.4 = ((bf16[16,32,8,128]{3,2,1,0:T(8,128)(2,1)}), bf16[16,32,8,128]{3,2,1,0:T(8,128)(2,1)S(1)}, u32[]{:S(2)}, u32[]{:S(2)}) async-start(bf16[16,32,8,128]{3,2,1,0:T(8,128)(2,1)} %bitcast.141), calls=%async_computation.4 | async-start | bytes 2097152 | tf_op jit(solution)/shard_map/all_to_all | solution.py:17
  215.4 4.5 %collective-permute-done.15 = bf16[1,2,512,128]{3,2,1,0:T(8,128)(2,1)S(1)} collective-permute-done((bf16[1,2,512,128]{3,2,1,0:T(8,128)(2,1)S(1)}, bf16[1,2,512,128]{3,2,1,0:T(8,128)(2,1)S(1)}, u32[]{:S(2)}, u32[]{:S(2)}) %collective-permute-start.15) | collective-permute-done | bytes 262176 | tf_op jit(solution)/shard_map/ppermute | solution.py:29
  219.9 15.9 %collective-permute-done.10 = bf16[1,4,2,128,256]{4,3,2,1,0:T(8,128)(2,1)S(1)} collective-permute-done((bf16[1,4,2,128,256]{4,3,2,1,0:T(8,128)(2,1)S(1)}, bf16[1,4,2,128,256]{4,3,2,1,0:T(8,128)(2,1)S(1)}, u32[]{:S(2)}, u32[]{:S(2)}) %collective-permute-start.10) | collective-permute-done | bytes 524320 | tf_op jit(solution)/shard_map/ppermute | solution.py:29
  237.1 19.4 %all-to-all-done.4 = bf16[16,32,8,128]{3,2,1,0:T(8,128)(2,1)S(1)} async-done(((bf16[16,32,8,128]{3,2,1,0:T(8,128)(2,1)}), bf16[16,32,8,128]{3,2,1,0:T(8,128)(2,1)S(1)}, u32[]{:S(2)}, u32[]{:S(2)}) %all-to-all-start.4) | async-done | bytes 1048608 | tf_op jit(solution)/shard_map/all_to_all | solution.py:17
  260.7 7.9 %all-to-all-start.5 = ((bf16[128,32,128]{2,1,0:T(8,128)(2,1)}), bf16[128,32,128]{2,1,0:T(8,128)(2,1)}, u32[]{:S(2)}, u32[]{:S(2)}) async-start(bf16[128,32,128]{2,1,0:T(8,128)(2,1)} %copy.54), calls=%async_computation.5 | async-start | bytes 2097152 | tf_op jit(solution)/shard_map/all_to_all | solution.py:17
  276.9 10.4 %collective-permute-done.12 = bf16[2,1,2,128,256]{4,3,2,1,0:T(8,128)(2,1)S(1)} collective-permute-done((bf16[2,1,2,128,256]{4,3,2,1,0:T(8,128)(2,1)}, bf16[2,1,2,128,256]{4,3,2,1,0:T(8,128)(2,1)S(1)}, u32[]{:S(2)}, u32[]{:S(2)}) %collective-permute-start.12) | collective-permute-done | bytes 262176 | tf_op jit(solution)/shard_map/ppermute | solution.py:29
  287.3 7.2 %collective-permute-done.13 = bf16[2,1,2,128,256]{4,3,2,1,0:T(8,128)(2,1)S(1)} collective-permute-done((bf16[2,1,2,128,256]{4,3,2,1,0:T(8,128)(2,1)}, bf16[2,1,2,128,256]{4,3,2,1,0:T(8,128)(2,1)S(1)}, u32[]{:S(2)}, u32[]{:S(2)}) %collective-permute-start.13) | collective-permute-done | bytes 262176 | tf_op jit(solution)/shard_map/ppermute | solution.py:29
  311.3 5.0 %close.1 = (bf16[512,512]{1,0:T(8,128)(2,1)}, bf16[8,512,128]{2,1,0:T(8,128)(2,1)}) custom-call(bf16[16,8,32,128]{3,2,1,0:T(8,128)(2,1)} %bitcast.43.d_ref, bf16[512,512]{1,0:T(8,128)(2,1)} %dynamic-slice_bitcast_fusion.own_ref, bf16[8,512,128]{2,1,0:T(8,128)(2,1)} %bitcast.122), custom_call_target="tpu_custom_call" | custom-call | tf_op jit(solution)/shard_map/close/pallas_call | solution.py:195
  326.5 6.1 %all-to-all-start.6 = ((bf16[16,32,512]{2,1,0:T(8,128)(2,1)}), bf16[16,32,512]{2,1,0:T(8,128)(2,1)}, u32[]{:S(2)}, u32[]{:S(2)}) async-start(bf16[16,32,512]{2,1,0:T(8,128)(2,1)} %bitcast.144), calls=%async_computation.6 | async-start | bytes 1048576 | tf_op jit(solution)/shard_map/all_to_all | solution.py:17
  345.1 3.8 %finish.1 = bf16[4096,128]{1,0:T(8,128)(2,1)} custom-call(bf16[4096,128]{1,0:T(8,128)(2,1)} %bitcast.133, f32[4096,128]{1,0:T(8,128)} %bitcast.128), custom_call_target="tpu_custom_call" | custom-call | tf_op jit(solution)/shard_map/finish/pallas_call | solution.py:220
  (156 shorter events, 92.6 us)
Async XLA Ops:
  44.4 52.6 %all-to-all-start.1 = ((bf16[16,32,8,128]{3,2,1,0:T(8,128)(2,1)}), bf16[16,32,8,128]{3,2,1,0:T(8,128)(2,1)}, u32[]{:S(2)}, u32[]{:S(2)}) async-start(bf16[16,32,8,128]{3,2,1,0:T(8,128)(2,1)} %bitcast.117), calls=%async_computation.1 | async-start | bytes 2097152 | tf_op jit(solution)/shard_map/all_to_all | solution.py:17
  52.3 57.6 %collective-permute-start = (bf16[1,4,2,128,256]{3,4,2,1,0:T(8,128)(2,1)}, bf16[1,4,2,128,256]{3,4,2,1,0:T(8,128)(2,1)}, u32[]{:S(2)}, u32[]{:S(2)}) collective-permute-start(bf16[1,4,2,128,256]{3,4,2,1,0:T(8,128)(2,1)} %constant_dynamic-slice_fusion.19), channel_id=1, source_target_pairs={{0,8},{8,0},{1,9},{9,1},{2,10},{10,2},{3,11},{11,3},{4,12},{12,4},... | collective-permute-start | bytes 1572872 | tf_op jit(solution)/shard_map/ppermute | solution.py:29
  60.6 52.5 %collective-permute-start.6 = (bf16[2,32,128]{2,1,0:T(8,128)(2,1)S(1)}, bf16[2,32,128]{2,1,0:T(8,128)(2,1)S(1)}, u32[]{:S(2)}, u32[]{:S(2)}) collective-permute-start(bf16[2,32,128]{2,1,0:T(8,128)(2,1)S(1)} %constant_dynamic-update-slice_fusion.13), channel_id=1, source_target_pairs={{0,2},{2,0},{4,6},{6,4},{1,3},{3,1},{5,7},{7,5},{8,10},{10,8},{12,... | collective-permute-start | bytes 49160 | tf_op jit(solution)/shard_map/ppermute | solution.py:46
  62.2 53.9 %collective-permute-start.7 = (bf16[2,32,128]{2,1,0:T(8,128)(2,1)S(1)}, bf16[2,32,128]{2,1,0:T(8,128)(2,1)S(1)}, u32[]{:S(2)}, u32[]{:S(2)}) collective-permute-start(bf16[2,32,128]{2,1,0:T(8,128)(2,1)S(1)} %constant_dynamic-update-slice_fusion.13), channel_id=1, source_target_pairs={{0,4},{2,6},{4,0},{6,2},{1,5},{3,7},{5,1},{7,3},{8,12},{10,14},{12... | collective-permute-start | bytes 49160 | tf_op jit(solution)/shard_map/ppermute | solution.py:46
  65.1 68.6 %collective-permute-start.8 = (bf16[2,32,128]{2,1,0:T(8,128)(2,1)S(1)}, bf16[2,32,128]{2,1,0:T(8,128)(2,1)S(1)}, u32[]{:S(2)}, u32[]{:S(2)}) collective-permute-start(bf16[2,32,128]{2,1,0:T(8,128)(2,1)S(1)} %constant_dynamic-update-slice_fusion.13), channel_id=1, source_target_pairs={{0,6},{2,4},{4,2},{6,0},{1,7},{3,5},{5,3},{7,1},{8,14},{10,12},{12... | collective-permute-start | bytes 49160 | tf_op jit(solution)/shard_map/ppermute | solution.py:46
  101.4 51.6 %all-to-all-start.2 = ((bf16[16,128,256]{2,1,0:T(8,128)(2,1)}), bf16[16,128,256]{2,1,0:T(8,128)(2,1)}, u32[]{:S(2)}, u32[]{:S(2)}) async-start(bf16[16,128,256]{2,1,0:T(8,128)(2,1)} %get-tuple-element.28), calls=%async_computation.2 | async-start | bytes 2097152 | tf_op jit(solution)/shard_map/all_to_all | solution.py:17
  113.1 19.6 %collective-permute-start.2 = (bf16[2,1,2,128,256]{3,4,2,1,0:T(8,128)(2,1)S(1)}, bf16[2,1,2,128,256]{3,4,2,1,0:T(8,128)(2,1)S(1)}, u32[]{:S(2)}, u32[]{:S(2)}) collective-permute-start(bf16[2,1,2,128,256]{3,4,2,1,0:T(8,128)(2,1)S(1)} %get-tuple-element.30), channel_id=1, source_target_pairs={{0,4},{2,6},{4,0},{6,2},{1,5},{3,7},{5,1},{7,3},{8,12},{10,14},{12... | collective-permute-start | bytes 786440 | tf_op jit(solution)/shard_map/ppermute | solution.py:29
  115.8 17.0 %collective-permute-start.3 = (bf16[2,1,2,128,256]{3,4,2,1,0:T(8,128)(2,1)S(1)}, bf16[2,1,2,128,256]{3,4,2,1,0:T(8,128)(2,1)S(1)}, u32[]{:S(2)}, u32[]{:S(2)}) collective-permute-start(bf16[2,1,2,128,256]{3,4,2,1,0:T(8,128)(2,1)S(1)} %get-tuple-element.31), channel_id=1, source_target_pairs={{0,6},{2,4},{4,2},{6,0},{1,7},{3,5},{5,3},{7,1},{8,14},{10,12},{12... | collective-permute-start | bytes 786440 | tf_op jit(solution)/shard_map/ppermute | solution.py:29
  133.7 16.8 %collective-permute-start.4 = (bf16[2,4,1,128,256]{3,4,2,1,0:T(8,128)(2,1)}, bf16[2,4,1,128,256]{3,4,2,1,0:T(8,128)(2,1)}, u32[]{:S(2)}, u32[]{:S(2)}) collective-permute-start(bf16[2,4,1,128,256]{3,4,2,1,0:T(8,128)(2,1)} %constant_dynamic-slice_fusion.15), channel_id=1, source_target_pairs={{0,1},{1,0},{2,3},{3,2},{4,5},{5,4},{6,7},{7,6},{8,9},{9,8},{10,11... | collective-permute-start | bytes 1572872 | tf_op jit(solution)/shard_map/ppermute | solution.py:29
  202.6 53.9 %all-to-all-start.4 = ((bf16[16,32,8,128]{3,2,1,0:T(8,128)(2,1)}), bf16[16,32,8,128]{3,2,1,0:T(8,128)(2,1)S(1)}, u32[]{:S(2)}, u32[]{:S(2)}) async-start(bf16[16,32,8,128]{3,2,1,0:T(8,128)(2,1)} %bitcast.141), calls=%async_computation.4 | async-start | bytes 2097152 | tf_op jit(solution)/shard_map/all_to_all | solution.py:17
  209.2 26.5 %collective-permute-start.10 = (bf16[1,4,2,128,256]{4,3,2,1,0:T(8,128)(2,1)S(1)}, bf16[1,4,2,128,256]{4,3,2,1,0:T(8,128)(2,1)S(1)}, u32[]{:S(2)}, u32[]{:S(2)}) collective-permute-start(bf16[1,4,2,128,256]{4,3,2,1,0:T(8,128)(2,1)S(1)} %constant_dynamic-slice_fusion.14), channel_id=1, source_target_pairs={{0,8},{8,0},{1,9},{9,1},{2,10},{10,2},{3,11},{11,3},{4,12},{12,4},... | collective-permute-start | bytes 1572872 | tf_op jit(solution)/shard_map/ppermute | solution.py:29
  210.7 58.0 %collective-permute-start.16 = (bf16[1,2,512,128]{3,2,1,0:T(8,128)(2,1)}, bf16[1,2,512,128]{3,2,1,0:T(8,128)(2,1)}, u32[]{:S(2)}, u32[]{:S(2)}) collective-permute-start(bf16[1,2,512,128]{3,2,1,0:T(8,128)(2,1)} %get-tuple-element.39), channel_id=1, source_target_pairs={{0,4},{2,6},{4,0},{6,2},{1,5},{3,7},{5,1},{7,3},{8,12},{10,14},{12... | collective-permute-start | bytes 786440 | tf_op jit(solution)/shard_map/ppermute | solution.py:29
  213.5 59.3 %collective-permute-start.17 = (bf16[1,2,512,128]{3,2,1,0:T(8,128)(2,1)S(1)}, bf16[1,2,512,128]{3,2,1,0:T(8,128)(2,1)}, u32[]{:S(2)}, u32[]{:S(2)}) collective-permute-start(bf16[1,2,512,128]{3,2,1,0:T(8,128)(2,1)S(1)} %get-tuple-element.40), channel_id=1, source_target_pairs={{0,6},{2,4},{4,2},{6,0},{1,7},{3,5},{5,3},{7,1},{8,14},{10,12},{12... | collective-permute-start | bytes 786440 | tf_op jit(solution)/shard_map/ppermute | solution.py:29
  237.1 38.8 %collective-permute-start.11 = (bf16[2,1,2,128,256]{4,3,2,1,0:T(8,128)(2,1)}, bf16[2,1,2,128,256]{4,3,2,1,0:T(8,128)(2,1)}, u32[]{:S(2)}, u32[]{:S(2)}) collective-permute-start(bf16[2,1,2,128,256]{4,3,2,1,0:T(8,128)(2,1)} %get-tuple-element.33), channel_id=1, source_target_pairs={{0,2},{2,0},{4,6},{6,4},{1,3},{3,1},{5,7},{7,5},{8,10},{10,8},{12,... | collective-permute-start | bytes 786440 | tf_op jit(solution)/shard_map/ppermute | solution.py:29
  260.7 50.6 %all-to-all-start.5 = ((bf16[128,32,128]{2,1,0:T(8,128)(2,1)}), bf16[128,32,128]{2,1,0:T(8,128)(2,1)}, u32[]{:S(2)}, u32[]{:S(2)}) async-start(bf16[128,32,128]{2,1,0:T(8,128)(2,1)} %copy.54), calls=%async_computation.5 | async-start | bytes 2097152 | tf_op jit(solution)/shard_map/all_to_all | solution.py:17
  269.7 17.5 %collective-permute-start.12 = (bf16[2,1,2,128,256]{4,3,2,1,0:T(8,128)(2,1)}, bf16[2,1,2,128,256]{4,3,2,1,0:T(8,128)(2,1)S(1)}, u32[]{:S(2)}, u32[]{:S(2)}) collective-permute-start(bf16[2,1,2,128,256]{4,3,2,1,0:T(8,128)(2,1)} %get-tuple-element.34), channel_id=1, source_target_pairs={{0,4},{2,6},{4,0},{6,2},{1,5},{3,7},{5,1},{7,3},{8,12},{10,14},{12... | collective-permute-start | bytes 786440 | tf_op jit(solution)/shard_map/ppermute | solution.py:29
  273.8 20.6 %collective-permute-start.13 = (bf16[2,1,2,128,256]{4,3,2,1,0:T(8,128)(2,1)}, bf16[2,1,2,128,256]{4,3,2,1,0:T(8,128)(2,1)S(1)}, u32[]{:S(2)}, u32[]{:S(2)}) collective-permute-start(bf16[2,1,2,128,256]{4,3,2,1,0:T(8,128)(2,1)} %get-tuple-element.35), channel_id=1, source_target_pairs={{0,6},{2,4},{4,2},{6,0},{1,7},{3,5},{5,3},{7,1},{8,14},{10,12},{12... | collective-permute-start | bytes 786440 | tf_op jit(solution)/shard_map/ppermute | solution.py:29
  275.9 25.6 %collective-permute-start.18 = (bf16[4,1,512,128]{3,2,1,0:T(8,128)(2,1)}, bf16[4,1,512,128]{3,2,1,0:T(8,128)(2,1)}, u32[]{:S(2)}, u32[]{:S(2)}) collective-permute-start(bf16[4,1,512,128]{3,2,1,0:T(8,128)(2,1)} %constant_dynamic-slice_fusion.6), channel_id=1, source_target_pairs={{0,1},{1,0},{2,3},{3,2},{4,5},{5,4},{6,7},{7,6},{8,9},{9,8},{10,11... | collective-permute-start | bytes 1572872 | tf_op jit(solution)/shard_map/ppermute | solution.py:29
  307.1 14.7 %collective-permute-start.26 = (bf16[1,2,32,8,128]{4,3,2,1,0:T(8,128)(2,1)S(1)}, bf16[1,2,32,8,128]{4,3,2,1,0:T(8,128)(2,1)S(1)}, u32[]{:S(2)}, u32[]{:S(2)}) collective-permute-start(bf16[1,2,32,8,128]{4,3,2,1,0:T(8,128)(2,1)S(1)} %get-tuple-element.49), channel_id=1, source_target_pairs={{0,6},{2,4},{4,2},{6,0},{1,7},{3,5},{5,3},{7,1},{8,14},{10,12},{12... | collective-permute-start | bytes 393224 | tf_op jit(solution)/shard_map/ppermute | solution.py:29
  318.3 14.4 %collective-permute-start.19 = (bf16[1,2,512,128]{3,2,1,0:T(8,128)(2,1)}, bf16[1,2,512,128]{3,2,1,0:T(8,128)(2,1)}, u32[]{:S(2)}, u32[]{:S(2)}) collective-permute-start(bf16[1,2,512,128]{3,2,1,0:T(8,128)(2,1)} %get-tuple-element.42), channel_id=1, source_target_pairs={{0,2},{2,0},{4,6},{6,4},{1,3},{3,1},{5,7},{7,5},{8,10},{10,8},{12,... | collective-permute-start | bytes 786440 | tf_op jit(solution)/shard_map/ppermute | solution.py:29
  319.3 15.2 %collective-permute-start.20 = (bf16[1,2,512,128]{3,2,1,0:T(8,128)(2,1)}, bf16[1,2,512,128]{3,2,1,0:T(8,128)(2,1)}, u32[]{:S(2)}, u32[]{:S(2)}) collective-permute-start(bf16[1,2,512,128]{3,2,1,0:T(8,128)(2,1)} %get-tuple-element.43), channel_id=1, source_target_pairs={{0,4},{2,6},{4,0},{6,2},{1,5},{3,7},{5,1},{7,3},{8,12},{10,14},{12... | collective-permute-start | bytes 786440 | tf_op jit(solution)/shard_map/ppermute | solution.py:29
  321.9 14.3 %collective-permute-start.21 = (bf16[1,2,512,128]{3,2,1,0:T(8,128)(2,1)}, bf16[1,2,512,128]{3,2,1,0:T(8,128)(2,1)}, u32[]{:S(2)}, u32[]{:S(2)}) collective-permute-start(bf16[1,2,512,128]{3,2,1,0:T(8,128)(2,1)} %get-tuple-element.44), channel_id=1, source_target_pairs={{0,6},{2,4},{4,2},{6,0},{1,7},{3,5},{5,3},{7,1},{8,14},{10,12},{12... | collective-permute-start | bytes 786440 | tf_op jit(solution)/shard_map/ppermute | solution.py:29
  323.9 19.5 %collective-permute-start.27 = (f32[1,32,8,128]{3,2,1,0:T(8,128)}, f32[1,32,8,128]{3,2,1,0:T(8,128)S(1)}, u32[]{:S(2)}, u32[]{:S(2)}) collective-permute-start(f32[1,32,8,128]{3,2,1,0:T(8,128)} %dynamic-slice_bitcast_fusion.1), channel_id=1, source_target_pairs={{0,8},{8,0},{1,9},{9,1},{2,10},{10,2},{3,11},{11,3},{4,12},{12,4},... | collective-permute-start | bytes 393224 | tf_op jit(solution)/shard_map/ppermute | solution.py:29
  326.5 23.4 %all-to-all-start.6 = ((bf16[16,32,512]{2,1,0:T(8,128)(2,1)}), bf16[16,32,512]{2,1,0:T(8,128)(2,1)}, u32[]{:S(2)}, u32[]{:S(2)}) async-start(bf16[16,32,512]{2,1,0:T(8,128)(2,1)} %bitcast.144), calls=%async_computation.6 | async-start | bytes 1048576 | tf_op jit(solution)/shard_map/all_to_all | solution.py:17
  (27 other events, 262.8 us)

commit v6 on v5

--- a/solution.py
+++ b/solution.py
@@ -109,7 +109,7 @@
 def gated(x_ref, mixed_ref, scale_ref, bias_ref):
     x = x_ref[...].astype(F32)
     mixed = mixed_ref[...].astype(F32)
-    return x, mixed, jax.nn.sigmoid(x * scale_ref[...] + bias_ref[...])
+    return x, mixed, 0.5 * jnp.tanh(0.5 * (x * scale_ref[...] + bias_ref[...])) + 0.5
 
 
 def enter_kernel(x_ref, mixed_ref, scale_ref, bias_ref, panel_ref, hidden_ref, inner_ref):
@@ -138,7 +138,7 @@
             preferred_element_type=F32,
         )
         d_mixed_ref[k] = (d_hidden * gate[k]).astype(BF16)
-        local_ref[k] = d_hidden * slope[k]
+        local_ref[k] = (d_hidden * slope[k]).astype(BF16)
 
 
 def by_rows(kernel, x, mixed, scale, bias, panel, more, outs):
@@ -160,7 +160,8 @@
     )(x, mixed, scale.reshape(1, width), bias.reshape(1, width), panel, *more)
 
 
-def close_kernel(d_ref, own_ref, x_ref, prod_ref, part_ref, total):
+def close_kernel(at_ref, d_ref, own_ref, x_ref, prod_ref, *more_refs):
+    *part_refs, total = more_refs
     step, (owners, here, offs, width) = pl.program_id(0), d_ref.shape
     height = owners * offs
     d_wide = jnp.concatenate([d_ref[:, k].reshape(height, width) for k in range(here)], axis=1)
@@ -171,8 +172,12 @@
     part = lax.dot_general(
         own_ref[...], d_wide, (((0,), (0,)), ((), ())), preferred_element_type=F32
     ).astype(BF16)
-    for k in range(here):
-        part_ref[k] = part[:, k * width : (k + 1) * width]
+    for r, part_ref in enumerate(part_refs):
+
+        @pl.when(step ^ at_ref[0] == r)
+        def _(part_ref=part_ref):
+            for k in range(here):
+                part_ref[k] = part[:, k * width : (k + 1) * width]
 
     @pl.when(step == 0)
     def _():
@@ -187,44 +192,63 @@
         prod_ref[...] = total[...].astype(BF16)
 
 
-def close(d_first, own, x_plane):
+def close(at, d_first, own, x_plane):
     owners, plane, offs, width = d_first.shape
-    height, here = owners * offs, 2
-    square = pl.BlockSpec((height, height), lambda g: (0, 0))
-    slab = pl.BlockSpec((here, height, width), lambda g: (g, 0, 0))
+    height, here = owners * offs, lax.axis_size("c")
+    steps_y = plane // here
+    square = pl.BlockSpec((height, height), lambda g, at: (0, 0))
+    part = jax.ShapeDtypeStruct((here, height, width), BF16)
     return pl.pallas_call(
         close_kernel,
-        out_shape=(
-            jax.ShapeDtypeStruct((height, height), BF16),
-            jax.ShapeDtypeStruct((plane, height, width), BF16),
+        out_shape=(jax.ShapeDtypeStruct((height, height), BF16),) + (part,) * steps_y,
+        grid_spec=pltpu.PrefetchScalarGridSpec(
+            num_scalar_prefetch=1,
+            grid=(steps_y,),
+            in_specs=[
+                pl.BlockSpec((owners, here, offs, width), lambda g, at: (0, g, 0, 0)),
+                square,
+                pl.BlockSpec((here, height, width), lambda g, at: (g, 0, 0)),
+            ],
+            out_specs=(square,)
+            + (pl.BlockSpec(part.shape, lambda g, at: (0, 0, 0)),) * steps_y,
+            scratch_shapes=[pltpu.VMEM((height, height), F32)],
         ),
-        grid=(plane // here,),
-        in_specs=[
-            pl.BlockSpec((owners, here, offs, width), lambda g: (0, g, 0, 0)),
-            square,
-            slab,
-        ],
-        out_specs=(square, slab),
-        scratch_shapes=[pltpu.VMEM((height, height), F32)],
         name="close",
-    )(d_first, own, x_plane)
-
-
-def finish_kernel(part_ref, local_ref, out_ref):
-    out_ref[...] = (part_ref[...].astype(F32) + local_ref[...]).astype(BF16)
-
-
-def finish(part, local):
-    rows, width = part.shape
-    block = pl.BlockSpec((rows // 4, width), lambda g: (g, 0))
+    )(at, d_first, own, x_plane)
+
+
+def finish_kernel(at_ref, crossed_ref, local_ref, *refs):
+    *part_refs, out_ref = refs
+    here = pl.program_id(0) ^ at_ref[0]
+    crossed = crossed_ref[0, 0].astype(F32)
+    for r, part_ref in enumerate(part_refs):
+
+        @pl.when(here == r)
+        def _(part_ref=part_ref):
+            kept = part_ref[0].astype(F32)
+            for c in range(local_ref.shape[1]):
+                value = jnp.where(at_ref[1] == c, kept, crossed)
+                out_ref[0, c] = (value + local_ref[0, c].astype(F32)).astype(BF16)
+
+
+def finish(at, parts, crossed, local):
+    here, height, width = parts[0].shape
+    whole = pl.BlockSpec((1, here, height, width), lambda g, at: (g, 0, 0, 0))
     return pl.pallas_call(
         finish_kernel,
-        out_shape=jax.ShapeDtypeStruct(part.shape, BF16),
-        grid=(4,),
-        in_specs=[block, block],
-        out_specs=block,
+        out_shape=jax.ShapeDtypeStruct(local.shape, BF16),
+        grid_spec=pltpu.PrefetchScalarGridSpec(
+            num_scalar_prefetch=1,
+            grid=(len(parts),),
+            in_specs=[
+                pl.BlockSpec((1, 1, height, width), lambda g, at: (g ^ at[0], 0, 0, 0)),
+                whole,
+            ]
+            + [pl.BlockSpec((1, height, width), lambda g, at: (at[1], 0, 0))] * len(parts),
+            out_specs=whole,
+        ),
         name="finish",
-    )(part, local)
+    )(at, crossed, local, *parts)
 
 
 def steps(
@@ -294,7 +318,7 @@
         gate_bias,
         panel,
         (cot_rows, d_back),
-        (jax.ShapeDtypeStruct(wide, BF16), jax.ShapeDtypeStruct(wide, F32)),
+        (jax.ShapeDtypeStruct(wide, BF16), jax.ShapeDtypeStruct(wide, BF16)),
     )
     d_mixed = move(d_mixed.reshape(flat), SEQ)
     d_mixed_j = d_mixed.transpose(1, 0, 2, 3).reshape(offs, nb, width)
@@ -310,8 +334,13 @@
     second_grad = fold(part, "zh", 0)
 
     own = lax.dynamic_index_in_dim(seq_first, lax.axis_index(PLANE), 0, keepdims=False)
-    prod, seq_part = close(d_first, own, x_plane)
-    seq_part = swap(seq_part, PLANE).reshape(rows, width)
+    at = jnp.stack([lax.axis_index("y"), lax.axis_index("c")]).astype(jnp.int32)
+    prod, *parts = close(at, d_first, own, x_plane)
+    near = lax.axis_size("y")
+    for r in range(1, near):
+        parts[r] = lax.ppermute(parts[r], "y", [(k, k ^ r) for k in range(near)])
+    crossed = jnp.stack([lax.dynamic_index_in_dim(p, 1 - at[1], 0, keepdims=True) for p in parts])
+    crossed = lax.ppermute(crossed, "c", [(0, 1), (1, 0)])
     prod = move(prod.reshape(n_hid, offs, block), HID)
     first_grad = prod.reshape(halves, n_plane, offs, block).astype(F32).sum(0)
 
@@ -320,7 +349,8 @@
 
     result = whole((hidden.astype(F32) + outer.astype(F32)).astype(BF16))
     local = whole(local)
-    token_grad = finish(seq_part, local)
+    local = local.reshape(near, len(at), block, width)
+    token_grad = finish(at, parts, crossed, local).reshape(rows, width)
     return result, token_grad, first_grad, second_grad
 
 

time: 356 us -> 354 us (level)
  local copies, waits for them, and re-layouts: 52.3 us -> 48.1 us
    all_to_all x5, waiting for transfers between devices: 52.2 us -> 69.2 us  [move(): return lax.all_to_all(value, axes, split_axis=0, concat_axis=0, tiled=True)]
    ppermute x23 -> x19, waiting for transfers between devices: 54.7 us -> 40.4 us  [trade(): lax.ppermute(parts[r - 1], axis, [(s, s ^ r) for s in range(size)])]
    ppermute x23 -> x19, starting transfers between devices: 31.6 us -> 24.2 us  [trade(): lax.ppermute(parts[r - 1], axis, [(s, s ^ r) for s in range(size)])]
    ppermute x0 -> x4, starting transfers between devices: none -> 4.46 us  [the longest x3 4.01 us: steps(): parts[r] = lax.ppermute(parts[r], 'y', [(k, k ^ r) for k in range(near)])]
    another operation x0 -> x4, local copies, waits for them, and re-layouts: none -> 3.77 us  [steps(): jnp.stack([lax.dynamic_index_in_dim(p, 1 - at[1], 0, keepdims=True) for p...]
    dynamic_update_slice x19 -> x15, local copies, waits for them, and re-layouts: 14.6 us -> 11.2 us  [turn(): value = lax.dynamic_update_slice_in_dim(value, got[r - 1], me ^ r, dim)]
    dynamic_slice x12 -> x10, local copies, waits for them, and re-layouts: 10.2 us -> 7.77 us  [trade(): lax.dynamic_index_in_dim(value, me ^ r, dim, keepdims=True)]
  transfers between devices with their start and end apart: 33 -> 33, of which waited for: 10 -> 11; matrix products, arithmetic and copies ran while one was open for 14% -> 14% of each run, Pallas kernels for 4% -> 4%
where the time goes in v6:
time: 354 us; the launch traced here: 352 us
  waiting for transfers between devices  114 us (32%)
  starting transfers between devices  76.9 us (22%)
  blocking collectives  73.5 us (21%)
  local copies, waits for them, and re-layouts  48.1 us (14%)
  Pallas kernels  25.3 us (7%)
  matrix products  7.5 us (2%)
  other arithmetic  6.3 us (2%)
    all_to_all x2, blocking collectives, move(): return lax.all_to_all(value, axes, split_axis=0, concat_axis=0, tiled=True)  73.5 us
    all_to_all x5, waiting for transfers between devices, move(): return lax.all_to_all(value, axes, split_axis=0, concat_axis=0, tiled=True)  69.2 us
    ppermute x19, waiting for transfers between devices, trade(): lax.ppermute(parts[r - 1], axis, [(s, s ^ r) for s in range(size)])  40.4 us
    all_to_all x5, starting transfers between devices, move(): return lax.all_to_all(value, axes, split_axis=0, concat_axis=0, tiled=True)  34.4 us
    ppermute x19, starting transfers between devices, trade(): lax.ppermute(parts[r - 1], axis, [(s, s ^ r) for s in range(size)])  24.2 us
    ppermute x5, starting transfers between devices, gather(): other = lax.ppermute(value, axis, [(s, s ^ r) for s in range(size)])  13.8 us
    dynamic_update_slice x15, local copies, waits for them, and re-layouts, turn(): value = lax.dynamic_update_slice_in_dim(value, got[r - 1], me ^ r, dim)  11.2 us
    pallas_call x2, Pallas kernels, by_rows(): pl.pallas_call(kernel, out_shape=outs, grid=(owners // here,), in_specs=[...  9.38 us
  transfers between devices with their start and end apart: 33, of which 11 were waited for; matrix products, arithmetic and copies ran while one was open for 14% of the time, Pallas kernels for 4%

profile of v6, /device:TPU:32, one launch (start us, length us, event | category | flops | bytes accessed | tf_op | source)
XLA Modules:
  0.0 352.3 jit_solution(1224347669667886460)
XLA Ops:
  2.0 4.7 %fusion.1 = bf16[512,8,128]{0,2,1:T(8,128)(2,1)} fusion(bf16[8,512,128]{2,1,0:T(8,128)(2,1)S(1)} %bitcast.127, bf16[8,512,512]{2,1,0:T(8,128)(2,1)} %param.10), kind=kOutput, calls=%fused_computation.6 | convolution fusion | flops 537395200 | bytes 6291456 | tf_op jit(solution)/shard_map/qkj,qjc->kqc/dot_general | solution.py:68
  8.4 34.3 %all_to_all.35 = bf16[16,32,8,128]{3,2,1,0:T(8,128)(2,1)S(1)} all-to-all(bf16[16,32,8,128]{3,2,1,0:T(8,128)(2,1)S(1)} %bitcast.141), channel_id=1, replica_groups=mesh['zl'=4,'x'=4,'zh'=2,'y'=4,'c'=2] {'zl','x'}, dimensions={0} | all-to-all | bytes 2097152 | tf_op jit(solution)/shard_map/all_to_all | solution.py:17
  44.4 5.1 %all-to-all-start.1 = ((bf16[16,32,8,128]{3,2,1,0:T(8,128)(2,1)}), bf16[16,32,8,128]{3,2,1,0:T(8,128)(2,1)}, u32[]{:S(2)}, u32[]{:S(2)}) async-start(bf16[16,32,8,128]{3,2,1,0:T(8,128)(2,1)} %bitcast.126), calls=%async_computation.1 | async-start | bytes 2097152 | tf_op jit(solution)/shard_map/all_to_all | solution.py:17
  52.3 4.5 %collective-permute-start = (bf16[1,4,2,128,256]{3,4,2,1,0:T(8,128)(2,1)}, bf16[1,4,2,128,256]{3,4,2,1,0:T(8,128)(2,1)}, u32[]{:S(2)}, u32[]{:S(2)}) collective-permute-start(bf16[1,4,2,128,256]{3,4,2,1,0:T(8,128)(2,1)} %constant_dynamic-slice_fusion.15), channel_id=1, source_target_pairs={{0,8},{8,0},{1,9},{9,1},{2,10},{10,2},{3,11},{11,3},{4,12},{12,4},... | collective-permute-start | bytes 1572872 | tf_op jit(solution)/shard_map/ppermute | solution.py:29
  65.3 31.7 %all-to-all-done.1 = bf16[16,32,8,128]{3,2,1,0:T(8,128)(2,1)} async-done(((bf16[16,32,8,128]{3,2,1,0:T(8,128)(2,1)}), bf16[16,32,8,128]{3,2,1,0:T(8,128)(2,1)}, u32[]{:S(2)}, u32[]{:S(2)}) %all-to-all-start.1) | async-done | bytes 1048608 | tf_op jit(solution)/shard_map/all_to_all | solution.py:17
  97.0 4.4 %shard_map.111 = (bf16[16,256,128]{2,1,0:T(8,128)(2,1)}, bf16[16,128,256]{2,1,0:T(8,128)(2,1)}) custom-call(bf16[16,256,128]{2,1,0:T(8,128)(2,1)} %bitcast.135, bf16[16,256,128]{2,1,0:T(8,128)(2,1)} %bitcast.10.mixed_ref, f32[1,128]{1,0:T(1,128)} %bitcast.152, f32[1,128]{1,0:T(1,128)} %bitcast.154, bf16[128,128]{1,0:T(8,128)(2,1)} %mul.23.panel_ref), custom_call_target="tpu_custom_call" | custom-call | tf_op jit(solution)/shard_map/pallas_call | solution.py:152
  101.4 8.6 %all-to-all-start.2 = ((bf16[16,128,256]{2,1,0:T(8,128)(2,1)}), bf16[16,128,256]{2,1,0:T(8,128)(2,1)}, u32[]{:S(2)}, u32[]{:S(2)}) async-start(bf16[16,128,256]{2,1,0:T(8,128)(2,1)} %get-tuple-element.28), calls=%async_computation.2 | async-start | bytes 2097152 | tf_op jit(solution)/shard_map/all_to_all | solution.py:17
  116.1 8.9 %collective-permute-done.1 = bf16[2,1,2,128,256]{3,4,2,1,0:T(8,128)(2,1)S(1)} collective-permute-done((bf16[2,1,2,128,256]{3,4,2,1,0:T(8,128)(2,1)S(1)}, bf16[2,1,2,128,256]{3,4,2,1,0:T(8,128)(2,1)S(1)}, u32[]{:S(2)}, u32[]{:S(2)}) %collective-permute-start.1) | collective-permute-done | bytes 262176 | tf_op jit(solution)/shard_map/ppermute | solution.py:29
  125.0 7.8 %collective-permute-done.2 = bf16[2,1,2,128,256]{3,4,2,1,0:T(8,128)(2,1)S(1)} collective-permute-done((bf16[2,1,2,128,256]{3,4,2,1,0:T(8,128)(2,1)S(1)}, bf16[2,1,2,128,256]{3,4,2,1,0:T(8,128)(2,1)S(1)}, u32[]{:S(2)}, u32[]{:S(2)}) %collective-permute-start.2) | collective-permute-done | bytes 262176 | tf_op jit(solution)/shard_map/ppermute | solution.py:29
  133.7 9.1 %collective-permute-start.9 = (bf16[4,2,32,128]{3,2,1,0:T(8,128)(2,1)S(1)}, bf16[4,2,32,128]{3,2,1,0:T(8,128)(2,1)S(1)}, u32[]{:S(2)}, u32[]{:S(2)}) collective-permute-start(bf16[4,2,32,128]{3,2,1,0:T(8,128)(2,1)S(1)} %bitcast_dynamic-update-slice_fusion.2), channel_id=1, source_target_pairs={{0,8},{8,0},{1,9},{9,1},{2,10},{10,2},{3,11},{11,3},{4,12},{12,4},... | collective-permute-start | bytes 196616 | tf_op jit(solution)/shard_map/ppermute | solution.py:46
  142.9 4.0 %collective-permute-done.9 = bf16[4,2,32,128]{3,2,1,0:T(8,128)(2,1)S(1)} collective-permute-done((bf16[4,2,32,128]{3,2,1,0:T(8,128)(2,1)S(1)}, bf16[4,2,32,128]{3,2,1,0:T(8,128)(2,1)S(1)}, u32[]{:S(2)}, u32[]{:S(2)}) %collective-permute-start.9) | collective-permute-done | bytes 65568 | tf_op jit(solution)/shard_map/ppermute | solution.py:46
  153.0 5.3 %mix_features.1 = (bf16[32,64,256]{2,1,0:T(8,128)(2,1)}, bf16[32,64,256]{2,1,0:T(8,128)(2,1)}) custom-call(bf16[32,64,256]{2,1,0:T(8,128)(2,1)} %bitcast.13.inner_ref, bf16[32,64,256]{2,1,0:T(8,128)(2,1)} %bitcast.140, bf16[32,64,32]{2,1,0:T(8,128)(2,1)} %bitcast.144), custom_call_target="tpu_custom_call" | custom-call | tf_op jit(solution)/shard_map/mix_features/pallas_call | solution.py:99
  158.3 39.2 %all_to_all.36.d_ref = bf16[16,128,256]{2,1,0:T(8,128)(2,1)} all-to-all(bf16[16,128,256]{2,1,0:T(8,128)(2,1)} %bitcast.149), channel_id=1, replica_groups=mesh['zl'=4,'x'=4,'zh'=2,'y'=4,'c'=2] {'zh','y','c'}, dimensions={0} | all-to-all | bytes 2097152 | tf_op jit(solution)/shard_map/all_to_all | solution.py:17
  197.5 4.9 %shard_map.112 = (bf16[16,256,128]{2,1,0:T(8,128)(2,1)}, bf16[16,256,128]{2,1,0:T(8,128)(2,1)}) custom-call(bf16[16,256,128]{2,1,0:T(8,128)(2,1)} %bitcast.136, bf16[16,256,128]{2,1,0:T(8,128)(2,1)} %bitcast.10.mixed_ref, f32[1,128]{1,0:T(1,128)} %bitcast.153, f32[1,128]{1,0:T(1,128)} %bitcast.155, bf16[128,128]{1,0:T(8,128)(2,1)} %mul.23.panel_ref, ...), custom_call_target="tpu_custom_call" | custom-call | tf_op jit(solution)/shard_map/pallas_call | solution.py:152
  202.4 5.5 %all-to-all-start.4 = ((bf16[16,32,8,128]{3,2,1,0:T(8,128)(2,1)}), bf16[16,32,8,128]{3,2,1,0:T(8,128)(2,1)S(1)}, u32[]{:S(2)}, u32[]{:S(2)}) async-start(bf16[16,32,8,128]{3,2,1,0:T(8,128)(2,1)} %bitcast.147), calls=%async_computation.4 | async-start | bytes 2097152 | tf_op jit(solution)/shard_map/all_to_all | solution.py:17
  219.2 4.2 %collective-permute-done.16 = bf16[1,2,512,128]{3,2,1,0:T(8,128)(2,1)} collective-permute-done((bf16[1,2,512,128]{3,2,1,0:T(8,128)(2,1)}, bf16[1,2,512,128]{3,2,1,0:T(8,128)(2,1)}, u32[]{:S(2)}, u32[]{:S(2)}) %collective-permute-start.16) | collective-permute-done | bytes 262176 | tf_op jit(solution)/shard_map/ppermute | solution.py:29
  225.8 30.6 %all-to-all-done.4 = bf16[16,32,8,128]{3,2,1,0:T(8,128)(2,1)S(1)} async-done(((bf16[16,32,8,128]{3,2,1,0:T(8,128)(2,1)}), bf16[16,32,8,128]{3,2,1,0:T(8,128)(2,1)S(1)}, u32[]{:S(2)}, u32[]{:S(2)}) %all-to-all-start.4) | async-done | bytes 1048608 | tf_op jit(solution)/shard_map/all_to_all | solution.py:17
  260.6 7.9 %all-to-all-start.5 = ((bf16[128,32,128]{2,1,0:T(8,128)(2,1)}), bf16[128,32,128]{2,1,0:T(8,128)(2,1)}, u32[]{:S(2)}, u32[]{:S(2)}) async-start(bf16[128,32,128]{2,1,0:T(8,128)(2,1)} %copy.54), calls=%async_computation.5 | async-start | bytes 2097152 | tf_op jit(solution)/shard_map/all_to_all | solution.py:17
  281.2 5.6 %collective-permute-done.11 = bf16[2,1,2,128,256]{4,3,2,1,0:T(8,128)(2,1)S(1)} collective-permute-done((bf16[2,1,2,128,256]{4,3,2,1,0:T(8,128)(2,1)S(1)}, bf16[2,1,2,128,256]{4,3,2,1,0:T(8,128)(2,1)S(1)}, u32[]{:S(2)}, u32[]{:S(2)}) %collective-permute-start.11) | collective-permute-done | bytes 262176 | tf_op jit(solution)/shard_map/ppermute | solution.py:29
  286.9 9.7 %collective-permute-done.12 = bf16[2,1,2,128,256]{4,3,2,1,0:T(8,128)(2,1)S(1)} collective-permute-done((bf16[2,1,2,128,256]{4,3,2,1,0:T(8,128)(2,1)S(1)}, bf16[2,1,2,128,256]{4,3,2,1,0:T(8,128)(2,1)S(1)}, u32[]{:S(2)}, u32[]{:S(2)}) %collective-permute-start.12) | collective-permute-done | bytes 262176 | tf_op jit(solution)/shard_map/ppermute | solution.py:29
  310.5 6.0 %close.1 = (bf16[512,512]{1,0:T(8,128)(2,1)}, bf16[2,512,128]{2,1,0:T(8,128)(2,1)}, bf16[2,512,128]{2,1,0:T(8,128)(2,1)}, bf16[2,512,128]{2,1,0:T(8,128)(2,1)}, bf16[2,512,128]{2,1,0:T(8,128)(2,1)}) custom-call(s32[2]{0:T(128)} %pad_add_fusion.at_ref, bf16[16,8,32,128]{3,2,1,0:T(8,128)(2,1)} %bitcast.45.d_ref, ...), custom_call_target="tpu_custom_call" | custom-call | tf_op jit(solution)/shard_map/close/pallas_call | solution.py:201
  322.5 7.4 %all-to-all-start.6 = ((bf16[16,32,512]{2,1,0:T(8,128)(2,1)}), bf16[16,32,512]{2,1,0:T(8,128)(2,1)}, u32[]{:S(2)}, u32[]{:S(2)}) async-start(bf16[16,32,512]{2,1,0:T(8,128)(2,1)} %bitcast.151), calls=%async_computation.6 | async-start | bytes 1048576 | tf_op jit(solution)/shard_map/all_to_all | solution.py:17
  338.8 4.6 %finish.1 = bf16[4,2,512,128]{3,2,1,0:T(8,128)(2,1)} custom-call(s32[2]{0:T(128)} %pad_add_fusion.at_ref, bf16[4,1,512,128]{3,2,1,0:T(8,128)(2,1)} %copy-done.12, bf16[4,2,512,128]{3,2,1,0:T(8,128)(2,1)} %bitcast.142, bf16[2,512,128]{2,1,0:T(8,128)(2,1)} %get-tuple-element.41.refs_0_, bf16[2,512,128]{2,1,0:T(8,128)(2,1)} %collective-permute-done.19.refs_1_, ...), custom_call_target="tpu_custom_call" | custom-call | tf_op jit(solution)/shard_map/finish/pallas_call | solution.py:237
  343.3 7.0 %all-to-all-done.6 = bf16[16,32,512]{2,1,0:T(8,128)(2,1)} async-done(((bf16[16,32,512]{2,1,0:T(8,128)(2,1)}), bf16[16,32,512]{2,1,0:T(8,128)(2,1)}, u32[]{:S(2)}, u32[]{:S(2)}) %all-to-all-start.6) | async-done | bytes 524320 | tf_op jit(solution)/shard_map/all_to_all | solution.py:17
  (150 shorter events, 90.3 us)
Async XLA Ops:
  44.4 52.6 %all-to-all-start.1 = ((bf16[16,32,8,128]{3,2,1,0:T(8,128)(2,1)}), bf16[16,32,8,128]{3,2,1,0:T(8,128)(2,1)}, u32[]{:S(2)}, u32[]{:S(2)}) async-start(bf16[16,32,8,128]{3,2,1,0:T(8,128)(2,1)} %bitcast.126), calls=%async_computation.1 | async-start | bytes 2097152 | tf_op jit(solution)/shard_map/all_to_all | solution.py:17
  52.3 57.7 %collective-permute-start = (bf16[1,4,2,128,256]{3,4,2,1,0:T(8,128)(2,1)}, bf16[1,4,2,128,256]{3,4,2,1,0:T(8,128)(2,1)}, u32[]{:S(2)}, u32[]{:S(2)}) collective-permute-start(bf16[1,4,2,128,256]{3,4,2,1,0:T(8,128)(2,1)} %constant_dynamic-slice_fusion.15), channel_id=1, source_target_pairs={{0,8},{8,0},{1,9},{9,1},{2,10},{10,2},{3,11},{11,3},{4,12},{12,4},... | collective-permute-start | bytes 1572872 | tf_op jit(solution)/shard_map/ppermute | solution.py:29
  60.6 52.6 %collective-permute-start.6 = (bf16[2,32,128]{2,1,0:T(8,128)(2,1)S(1)}, bf16[2,32,128]{2,1,0:T(8,128)(2,1)S(1)}, u32[]{:S(2)}, u32[]{:S(2)}) collective-permute-start(bf16[2,32,128]{2,1,0:T(8,128)(2,1)S(1)} %constant_dynamic-update-slice_fusion.9), channel_id=1, source_target_pairs={{0,2},{2,0},{4,6},{6,4},{1,3},{3,1},{5,7},{7,5},{8,10},{10,8},{12,... | collective-permute-start | bytes 49160 | tf_op jit(solution)/shard_map/ppermute | solution.py:46
  62.2 53.9 %collective-permute-start.7 = (bf16[2,32,128]{2,1,0:T(8,128)(2,1)S(1)}, bf16[2,32,128]{2,1,0:T(8,128)(2,1)S(1)}, u32[]{:S(2)}, u32[]{:S(2)}) collective-permute-start(bf16[2,32,128]{2,1,0:T(8,128)(2,1)S(1)} %constant_dynamic-update-slice_fusion.9), channel_id=1, source_target_pairs={{0,4},{2,6},{4,0},{6,2},{1,5},{3,7},{5,1},{7,3},{8,12},{10,14},{12... | collective-permute-start | bytes 49160 | tf_op jit(solution)/shard_map/ppermute | solution.py:46
  65.1 68.7 %collective-permute-start.8 = (bf16[2,32,128]{2,1,0:T(8,128)(2,1)S(1)}, bf16[2,32,128]{2,1,0:T(8,128)(2,1)S(1)}, u32[]{:S(2)}, u32[]{:S(2)}) collective-permute-start(bf16[2,32,128]{2,1,0:T(8,128)(2,1)S(1)} %constant_dynamic-update-slice_fusion.9), channel_id=1, source_target_pairs={{0,6},{2,4},{4,2},{6,0},{1,7},{3,5},{5,3},{7,1},{8,14},{10,12},{12... | collective-permute-start | bytes 49160 | tf_op jit(solution)/shard_map/ppermute | solution.py:46
  101.4 51.6 %all-to-all-start.2 = ((bf16[16,128,256]{2,1,0:T(8,128)(2,1)}), bf16[16,128,256]{2,1,0:T(8,128)(2,1)}, u32[]{:S(2)}, u32[]{:S(2)}) async-start(bf16[16,128,256]{2,1,0:T(8,128)(2,1)} %get-tuple-element.28), calls=%async_computation.2 | async-start | bytes 2097152 | tf_op jit(solution)/shard_map/all_to_all | solution.py:17
  113.2 19.6 %collective-permute-start.2 = (bf16[2,1,2,128,256]{3,4,2,1,0:T(8,128)(2,1)S(1)}, bf16[2,1,2,128,256]{3,4,2,1,0:T(8,128)(2,1)S(1)}, u32[]{:S(2)}, u32[]{:S(2)}) collective-permute-start(bf16[2,1,2,128,256]{3,4,2,1,0:T(8,128)(2,1)S(1)} %get-tuple-element.30), channel_id=1, source_target_pairs={{0,4},{2,6},{4,0},{6,2},{1,5},{3,7},{5,1},{7,3},{8,12},{10,14},{12... | collective-permute-start | bytes 786440 | tf_op jit(solution)/shard_map/ppermute | solution.py:29
  115.9 17.0 %collective-permute-start.3 = (bf16[2,1,2,128,256]{3,4,2,1,0:T(8,128)(2,1)S(1)}, bf16[2,1,2,128,256]{3,4,2,1,0:T(8,128)(2,1)S(1)}, u32[]{:S(2)}, u32[]{:S(2)}) collective-permute-start(bf16[2,1,2,128,256]{3,4,2,1,0:T(8,128)(2,1)S(1)} %get-tuple-element.31), channel_id=1, source_target_pairs={{0,6},{2,4},{4,2},{6,0},{1,7},{3,5},{5,3},{7,1},{8,14},{10,12},{12... | collective-permute-start | bytes 786440 | tf_op jit(solution)/shard_map/ppermute | solution.py:29
  133.7 16.8 %collective-permute-start.4 = (bf16[2,4,1,128,256]{3,4,2,1,0:T(8,128)(2,1)}, bf16[2,4,1,128,256]{3,4,2,1,0:T(8,128)(2,1)}, u32[]{:S(2)}, u32[]{:S(2)}) collective-permute-start(bf16[2,4,1,128,256]{3,4,2,1,0:T(8,128)(2,1)} %constant_dynamic-slice_fusion.11), channel_id=1, source_target_pairs={{0,1},{1,0},{2,3},{3,2},{4,5},{5,4},{6,7},{7,6},{8,9},{9,8},{10,11... | collective-permute-start | bytes 1572872 | tf_op jit(solution)/shard_map/ppermute | solution.py:29
  202.4 53.9 %all-to-all-start.4 = ((bf16[16,32,8,128]{3,2,1,0:T(8,128)(2,1)}), bf16[16,32,8,128]{3,2,1,0:T(8,128)(2,1)S(1)}, u32[]{:S(2)}, u32[]{:S(2)}) async-start(bf16[16,32,8,128]{3,2,1,0:T(8,128)(2,1)} %bitcast.147), calls=%async_computation.4 | async-start | bytes 2097152 | tf_op jit(solution)/shard_map/all_to_all | solution.py:17
  208.8 14.6 %collective-permute-start.16 = (bf16[1,2,512,128]{3,2,1,0:T(8,128)(2,1)}, bf16[1,2,512,128]{3,2,1,0:T(8,128)(2,1)}, u32[]{:S(2)}, u32[]{:S(2)}) collective-permute-start(bf16[1,2,512,128]{3,2,1,0:T(8,128)(2,1)} %get-tuple-element.39), channel_id=1, source_target_pairs={{0,4},{2,6},{4,0},{6,2},{1,5},{3,7},{5,1},{7,3},{8,12},{10,14},{12... | collective-permute-start | bytes 786440 | tf_op jit(solution)/shard_map/ppermute | solution.py:29
  211.6 56.9 %collective-permute-start.17 = (bf16[1,2,512,128]{3,2,1,0:T(8,128)(2,1)S(1)}, bf16[1,2,512,128]{3,2,1,0:T(8,128)(2,1)}, u32[]{:S(2)}, u32[]{:S(2)}) collective-permute-start(bf16[1,2,512,128]{3,2,1,0:T(8,128)(2,1)S(1)} %get-tuple-element.40), channel_id=1, source_target_pairs={{0,6},{2,4},{4,2},{6,0},{1,7},{3,5},{5,3},{7,1},{8,14},{10,12},{12... | collective-permute-start | bytes 786440 | tf_op jit(solution)/shard_map/ppermute | solution.py:29
  225.2 45.3 %collective-permute-start.10 = (bf16[1,4,2,128,256]{4,3,2,1,0:T(8,128)(2,1)}, bf16[1,4,2,128,256]{4,3,2,1,0:T(8,128)(2,1)}, u32[]{:S(2)}, u32[]{:S(2)}) collective-permute-start(bf16[1,4,2,128,256]{4,3,2,1,0:T(8,128)(2,1)} %constant_dynamic-slice_fusion.10), channel_id=1, source_target_pairs={{0,8},{8,0},{1,9},{9,1},{2,10},{10,2},{3,11},{11,3},{4,12},{12,4},... | collective-permute-start | bytes 1572872 | tf_op jit(solution)/shard_map/ppermute | solution.py:29
  260.6 50.0 %all-to-all-start.5 = ((bf16[128,32,128]{2,1,0:T(8,128)(2,1)}), bf16[128,32,128]{2,1,0:T(8,128)(2,1)}, u32[]{:S(2)}, u32[]{:S(2)}) async-start(bf16[128,32,128]{2,1,0:T(8,128)(2,1)} %copy.54), calls=%async_computation.5 | async-start | bytes 2097152 | tf_op jit(solution)/shard_map/all_to_all | solution.py:17
  270.4 35.8 %collective-permute-start.18 = (bf16[4,1,512,128]{3,2,1,0:T(8,128)(2,1)}, bf16[4,1,512,128]{3,2,1,0:T(8,128)(2,1)}, u32[]{:S(2)}, u32[]{:S(2)}) collective-permute-start(bf16[4,1,512,128]{3,2,1,0:T(8,128)(2,1)} %constant_dynamic-slice_fusion.2), channel_id=1, source_target_pairs={{0,1},{1,0},{2,3},{3,2},{4,5},{5,4},{6,7},{7,6},{8,9},{9,8},{10,11... | collective-permute-start | bytes 1572872 | tf_op jit(solution)/shard_map/ppermute | solution.py:29
  275.2 21.5 %collective-permute-start.12 = (bf16[2,1,2,128,256]{4,3,2,1,0:T(8,128)(2,1)S(1)}, bf16[2,1,2,128,256]{4,3,2,1,0:T(8,128)(2,1)S(1)}, u32[]{:S(2)}, u32[]{:S(2)}) collective-permute-start(bf16[2,1,2,128,256]{4,3,2,1,0:T(8,128)(2,1)S(1)} %get-tuple-element.34), channel_id=1, source_target_pairs={{0,4},{2,6},{4,0},{6,2},{1,5},{3,7},{5,1},{7,3},{8,12},{10,14},{12... | collective-permute-start | bytes 786440 | tf_op jit(solution)/shard_map/ppermute | solution.py:29
  277.9 20.1 %collective-permute-start.13 = (bf16[2,1,2,128,256]{4,3,2,1,0:T(8,128)(2,1)S(1)}, bf16[2,1,2,128,256]{4,3,2,1,0:T(8,128)(2,1)S(1)}, u32[]{:S(2)}, u32[]{:S(2)}) collective-permute-start(bf16[2,1,2,128,256]{4,3,2,1,0:T(8,128)(2,1)S(1)} %get-tuple-element.35), channel_id=1, source_target_pairs={{0,6},{2,4},{4,2},{6,0},{1,7},{3,5},{5,3},{7,1},{8,14},{10,12},{12... | collective-permute-start | bytes 786440 | tf_op jit(solution)/shard_map/ppermute | solution.py:29
  281.2 18.2 %collective-permute-start.23 = (bf16[4,1,2,32,8,128]{5,4,3,2,1,0:T(8,128)(2,1)}, bf16[4,1,2,32,8,128]{5,4,3,2,1,0:T(8,128)(2,1)}, u32[]{:S(2)}, u32[]{:S(2)}) collective-permute-start(bf16[4,1,2,32,8,128]{5,4,3,2,1,0:T(8,128)(2,1)} %copy.61), channel_id=1, source_target_pairs={{0,1},{1,0},{2,3},{3,2},{4,5},{5,4},{6,7},{7,6},{8,9},{9,8},{10,11... | collective-permute-start | bytes 1572872 | tf_op jit(solution)/shard_map/ppermute | solution.py:29
  301.6 15.0 %collective-permute-start.24 = (bf16[1,2,32,8,128]{4,3,2,1,0:T(8,128)(2,1)}, bf16[1,2,32,8,128]{4,3,2,1,0:T(8,128)(2,1)S(1)}, u32[]{:S(2)}, u32[]{:S(2)}) collective-permute-start(bf16[1,2,32,8,128]{4,3,2,1,0:T(8,128)(2,1)} %get-tuple-element.47), channel_id=1, source_target_pairs={{0,2},{2,0},{4,6},{6,4},{1,3},{3,1},{5,7},{7,5},{8,10},{10,8},{12,... | collective-permute-start | bytes 393224 | tf_op jit(solution)/shard_map/ppermute | solution.py:29
  301.6 15.0 %collective-permute-start.25 = (bf16[1,2,32,8,128]{4,3,2,1,0:T(8,128)(2,1)S(1)}, bf16[1,2,32,8,128]{4,3,2,1,0:T(8,128)(2,1)}, u32[]{:S(2)}, u32[]{:S(2)}) collective-permute-start(bf16[1,2,32,8,128]{4,3,2,1,0:T(8,128)(2,1)S(1)} %get-tuple-element.48), channel_id=1, source_target_pairs={{0,4},{2,6},{4,0},{6,2},{1,5},{3,7},{5,1},{7,3},{8,12},{10,14},{12... | collective-permute-start | bytes 393224 | tf_op jit(solution)/shard_map/ppermute | solution.py:29
  316.6 14.4 %collective-permute-start.20 = (bf16[2,512,128]{2,1,0:T(8,128)(2,1)}, bf16[2,512,128]{2,1,0:T(8,128)(2,1)}, u32[]{:S(2)}, u32[]{:S(2)}) collective-permute-start(bf16[2,512,128]{2,1,0:T(8,128)(2,1)} %get-tuple-element.43), channel_id=1, source_target_pairs={{0,4},{2,6},{4,0},{6,2},{1,5},{3,7},{5,1},{7,3},{8,12},{10,14},{12... | collective-permute-start | bytes 786440 | tf_op jit(solution)/shard_map/ppermute | solution.py:341
  317.9 14.0 %collective-permute-start.19 = (bf16[2,512,128]{2,1,0:T(8,128)(2,1)}, bf16[2,512,128]{2,1,0:T(8,128)(2,1)}, u32[]{:S(2)}, u32[]{:S(2)}) collective-permute-start(bf16[2,512,128]{2,1,0:T(8,128)(2,1)} %get-tuple-element.42), channel_id=1, source_target_pairs={{0,2},{2,0},{4,6},{6,4},{1,3},{3,1},{5,7},{7,5},{8,10},{10,8},{12,... | collective-permute-start | bytes 786440 | tf_op jit(solution)/shard_map/ppermute | solution.py:341
  319.7 17.6 %collective-permute-start.27 = (f32[1,32,8,128]{3,2,1,0:T(8,128)}, f32[1,32,8,128]{3,2,1,0:T(8,128)S(1)}, u32[]{:S(2)}, u32[]{:S(2)}) collective-permute-start(f32[1,32,8,128]{3,2,1,0:T(8,128)} %dynamic-slice_bitcast_fusion.1), channel_id=1, source_target_pairs={{0,8},{8,0},{1,9},{9,1},{2,10},{10,2},{3,11},{11,3},{4,12},{12,4},... | collective-permute-start | bytes 393224 | tf_op jit(solution)/shard_map/ppermute | solution.py:29
  322.5 27.8 %all-to-all-start.6 = ((bf16[16,32,512]{2,1,0:T(8,128)(2,1)}), bf16[16,32,512]{2,1,0:T(8,128)(2,1)}, u32[]{:S(2)}, u32[]{:S(2)}) async-start(bf16[16,32,512]{2,1,0:T(8,128)(2,1)} %bitcast.151), calls=%async_computation.6 | async-start | bytes 1048576 | tf_op jit(solution)/shard_map/all_to_all | solution.py:17
  (24 other events, 234.9 us)

commit v7 on v6

--- a/solution.py
+++ b/solution.py
@@ -69,31 +69,36 @@
 
 
 def mix_kernel(inner_ref, cot_ref, rows_ref, outer_ref, d_inner_ref):
-    panels, offs, count = inner_ref.shape
+    panels, here, count = inner_ref.shape
+    offs = 16
     width = panels * offs
     col = lax.broadcasted_iota(jnp.int32, (panels, width), 1)
     row = lax.broadcasted_iota(jnp.int32, (panels, width), 0)
     pick = (col // offs == row).astype(F32).astype(BF16)
-    full = jnp.dot(rows_ref[...].reshape(width, panels), pick, preferred_element_type=F32)
     at = lax.broadcasted_iota(jnp.int32, (width, width), 0) % offs
     to = lax.broadcasted_iota(jnp.int32, (width, width), 1) % offs
-    spread = jnp.where(at == to, full, 0.0).astype(BF16)
-    d_act = jnp.dot(spread, cot_ref[...].reshape(width, count), preferred_element_type=F32)
-    inner = inner_ref[...].reshape(width, count).astype(F32)
-    cdf = 0.5 * (1.0 + lax.erf(inner * 0.7071067811865476))
-    density = jnp.exp(-0.5 * inner * inner) * 0.3989422804014327
-    d_inner = (d_act * (cdf + inner * density)).astype(BF16)
-    d_inner_ref[...] = d_inner.reshape(panels, offs, count)
-    act = (inner * cdf).astype(BF16)
-    outer = lax.dot_general(
-        spread, act, (((0,), (0,)), ((), ())), preferred_element_type=F32
-    ).astype(BF16)
-    outer_ref[...] = outer.reshape(panels, offs, count)
+    for k in range(0, here, offs):
+        part = pl.ds(k, offs)
+        rows = rows_ref[:, part].reshape(width, panels)
+        full = jnp.dot(rows, pick, preferred_element_type=F32)
+        spread = jnp.where(at == to, full, 0.0).astype(BF16)
+        cot = cot_ref[:, part].reshape(width, count)
+        d_act = jnp.dot(spread, cot, preferred_element_type=F32)
+        inner = inner_ref[:, part].reshape(width, count).astype(F32)
+        cdf = 0.5 * (1.0 + lax.erf(inner * 0.7071067811865476))
+        density = jnp.exp(-0.5 * inner * inner) * 0.3989422804014327
+        d_inner = (d_act * (cdf + inner * density)).astype(BF16)
+        d_inner_ref[:, part] = d_inner.reshape(panels, offs, count)
+        act = (inner * cdf).astype(BF16)
+        outer = lax.dot_general(
+            spread, act, (((0,), (0,)), ((), ())), preferred_element_type=F32
+        ).astype(BF16)
+        outer_ref[:, part] = outer.reshape(panels, offs, count)
 
 
 def mix_features(inner, cot, blocks):
     panels, group, count = inner.shape
-    offs = 16
+    offs = 32
     rows = blocks.transpose(2, 0, 1)
     data = pl.BlockSpec((panels, offs, count), lambda g: (0, g, 0))
     return pl.pallas_call(
@@ -143,7 +148,7 @@
 
 def by_rows(kernel, x, mixed, scale, bias, panel, more, outs):
     owners, _, width = x.shape
-    here = 4
+    here = 8
 
     def spec(shape):
         return pl.BlockSpec((here,) + shape[1:], lambda g: (g, 0, 0))
@@ -172,12 +177,16 @@
     part = lax.dot_general(
         own_ref[...], d_wide, (((0,), (0,)), ((), ())), preferred_element_type=F32
     ).astype(BF16)
-    for r, part_ref in enumerate(part_refs):
-
-        @pl.when(step ^ at_ref[0] == r)
-        def _(part_ref=part_ref):
-            for k in range(here):
-                part_ref[k] = part[:, k * width : (k + 1) * width]
+    cores = part_refs[0].shape[0]
+    near = here // cores
+    for i in range(near):
+        for r, part_ref in enumerate(part_refs):
+
+            @pl.when((step * near + i) ^ at_ref[0] == r)
+            def _(i=i, part_ref=part_ref):
+                for k in range(cores):
+                    lane = (i * cores + k) * width
+                    part_ref[k] = part[:, lane : lane + width]
 
     @pl.when(step == 0)
     def _():
@@ -194,23 +203,23 @@
 
 def close(at, d_first, own, x_plane):
     owners, plane, offs, width = d_first.shape
-    height, here = owners * offs, lax.axis_size("c")
-    steps_y = plane // here
+    height, here, cores = owners * offs, plane // 2, lax.axis_size("c")
+    near = plane // cores
     square = pl.BlockSpec((height, height), lambda g, at: (0, 0))
-    part = jax.ShapeDtypeStruct((here, height, width), BF16)
+    part = jax.ShapeDtypeStruct((cores, height, width), BF16)
     return pl.pallas_call(
         close_kernel,
-        out_shape=(jax.ShapeDtypeStruct((height, height), BF16),) + (part,) * steps_y,
+        out_shape=(jax.ShapeDtypeStruct((height, height), BF16),) + (part,) * near,
         grid_spec=pltpu.PrefetchScalarGridSpec(
             num_scalar_prefetch=1,
-            grid=(steps_y,),
+            grid=(plane // here,),
             in_specs=[
                 pl.BlockSpec((owners, here, offs, width), lambda g, at: (0, g, 0, 0)),
                 square,
                 pl.BlockSpec((here, height, width), lambda g, at: (g, 0, 0)),
             ],
             out_specs=(square,)
-            + (pl.BlockSpec(part.shape, lambda g, at: (0, 0, 0)),) * steps_y,
+            + (pl.BlockSpec(part.shape, lambda g, at: (0, 0, 0)),) * near,
             scratch_shapes=[pltpu.VMEM((height, height), F32)],
         ),
         name="close",
@@ -219,29 +228,33 @@
 
 def finish_kernel(at_ref, crossed_ref, local_ref, *refs):
     *part_refs, out_ref = refs
-    here = pl.program_id(0) ^ at_ref[0]
-    crossed = crossed_ref[0, 0].astype(F32)
-    for r, part_ref in enumerate(part_refs):
-
-        @pl.when(here == r)
-        def _(part_ref=part_ref):
-            kept = part_ref[0].astype(F32)
-            for c in range(local_ref.shape[1]):
-                value = jnp.where(at_ref[1] == c, kept, crossed)
-                out_ref[0, c] = (value + local_ref[0, c].astype(F32)).astype(BF16)
+    step, here = pl.program_id(0), local_ref.shape[0]
+    for i in range(here):
+        for r, part_ref in enumerate(part_refs):
+
+            @pl.when((step * here + i) ^ at_ref[0] == r)
+            def _(i=i, r=r, part_ref=part_ref):
+                kept = part_ref[0].astype(F32)
+                crossed = crossed_ref[r % here, 0].astype(F32)
+                for c in range(local_ref.shape[1]):
+                    value = jnp.where(at_ref[1] == c, kept, crossed)
+                    out_ref[i, c] = (value + local_ref[i, c].astype(F32)).astype(BF16)
 
 
 def finish(at, parts, crossed, local):
-    here, height, width = parts[0].shape
-    whole = pl.BlockSpec((1, here, height, width), lambda g, at: (g, 0, 0, 0))
+    cores, height, width = parts[0].shape
+    here = 2
+    whole = pl.BlockSpec((here, cores, height, width), lambda g, at: (g, 0, 0, 0))
     return pl.pallas_call(
         finish_kernel,
         out_shape=jax.ShapeDtypeStruct(local.shape, BF16),
         grid_spec=pltpu.PrefetchScalarGridSpec(
             num_scalar_prefetch=1,
-            grid=(len(parts),),
+            grid=(len(parts) // here,),
             in_specs=[
-                pl.BlockSpec((1, 1, height, width), lambda g, at: (g ^ at[0], 0, 0, 0)),
+                pl.BlockSpec(
+                    (here, 1, height, width), lambda g, at: (g ^ (at[0] // here), 0, 0, 0)
+                ),
                 whole,
             ]
             + [pl.BlockSpec((1, height, width), lambda g, at: (at[1], 0, 0))] * len(parts),

time: 354 us -> 351 us (level)
  Pallas kernels: 25.3 us -> 20.8 us
  transfers between devices with their start and end apart: 33 -> 33, of which waited for: 11 -> 11; matrix products, arithmetic and copies ran while one was open for 14% -> 14% of each run, Pallas kernels for 4% -> 3%
where the time goes in v7:
time: 351 us; the launch traced here: 349 us
  waiting for transfers between devices  115 us (33%)
  starting transfers between devices  76.9 us (22%)
  blocking collectives  73.5 us (21%)
  local copies, waits for them, and re-layouts  48.1 us (14%)
  Pallas kernels  20.8 us (6%)
  matrix products  7.5 us (2%)
  other arithmetic  6.3 us (2%)
    all_to_all x2, blocking collectives, move(): return lax.all_to_all(value, axes, split_axis=0, concat_axis=0, tiled=True)  73.5 us
    all_to_all x5, waiting for transfers between devices, move(): return lax.all_to_all(value, axes, split_axis=0, concat_axis=0, tiled=True)  70.5 us
    ppermute x19, waiting for transfers between devices, trade(): lax.ppermute(parts[r - 1], axis, [(s, s ^ r) for s in range(size)])  40.4 us
    all_to_all x5, starting transfers between devices, move(): return lax.all_to_all(value, axes, split_axis=0, concat_axis=0, tiled=True)  34.4 us
    ppermute x19, starting transfers between devices, trade(): lax.ppermute(parts[r - 1], axis, [(s, s ^ r) for s in range(size)])  24.2 us
    ppermute x5, starting transfers between devices, gather(): other = lax.ppermute(value, axis, [(s, s ^ r) for s in range(size)])  13.8 us
    dynamic_update_slice x15, local copies, waits for them, and re-layouts, turn(): value = lax.dynamic_update_slice_in_dim(value, got[r - 1], me ^ r, dim)  11.2 us
    dynamic_slice x10, local copies, waits for them, and re-layouts, trade(): lax.dynamic_index_in_dim(value, me ^ r, dim, keepdims=True)  7.77 us
  transfers between devices with their start and end apart: 33, of which 11 were waited for; matrix products, arithmetic and copies ran while one was open for 14% of the time, Pallas kernels for 3%

profile of v7, /device:TPU:32, one launch (start us, length us, event | category | flops | bytes accessed | tf_op | source)
XLA Modules:
  0.0 349.1 jit_solution(2361291142045628733)
XLA Ops:
  2.0 4.7 %fusion.1 = bf16[512,8,128]{0,2,1:T(8,128)(2,1)} fusion(bf16[8,512,128]{2,1,0:T(8,128)(2,1)S(1)} %bitcast.127, bf16[8,512,512]{2,1,0:T(8,128)(2,1)} %param.10), kind=kOutput, calls=%fused_computation.6 | convolution fusion | flops 537395200 | bytes 6291456 | tf_op jit(solution)/shard_map/qkj,qjc->kqc/dot_general | solution.py:68
  8.4 34.3 %all_to_all.35 = bf16[16,32,8,128]{3,2,1,0:T(8,128)(2,1)S(1)} all-to-all(bf16[16,32,8,128]{3,2,1,0:T(8,128)(2,1)S(1)} %bitcast.141), channel_id=1, replica_groups=mesh['zl'=4,'x'=4,'zh'=2,'y'=4,'c'=2] {'zl','x'}, dimensions={0} | all-to-all | bytes 2097152 | tf_op jit(solution)/shard_map/all_to_all | solution.py:17
  44.4 5.1 %all-to-all-start.1 = ((bf16[16,32,8,128]{3,2,1,0:T(8,128)(2,1)}), bf16[16,32,8,128]{3,2,1,0:T(8,128)(2,1)}, u32[]{:S(2)}, u32[]{:S(2)}) async-start(bf16[16,32,8,128]{3,2,1,0:T(8,128)(2,1)} %bitcast.126), calls=%async_computation.1 | async-start | bytes 2097152 | tf_op jit(solution)/shard_map/all_to_all | solution.py:17
  52.3 4.5 %collective-permute-start = (bf16[1,4,2,128,256]{3,4,2,1,0:T(8,128)(2,1)}, bf16[1,4,2,128,256]{3,4,2,1,0:T(8,128)(2,1)}, u32[]{:S(2)}, u32[]{:S(2)}) collective-permute-start(bf16[1,4,2,128,256]{3,4,2,1,0:T(8,128)(2,1)} %constant_dynamic-slice_fusion.15), channel_id=1, source_target_pairs={{0,8},{8,0},{1,9},{9,1},{2,10},{10,2},{3,11},{11,3},{4,12},{12,4},... | collective-permute-start | bytes 1572872 | tf_op jit(solution)/shard_map/ppermute | solution.py:29
  65.3 31.7 %all-to-all-done.1 = bf16[16,32,8,128]{3,2,1,0:T(8,128)(2,1)} async-done(((bf16[16,32,8,128]{3,2,1,0:T(8,128)(2,1)}), bf16[16,32,8,128]{3,2,1,0:T(8,128)(2,1)}, u32[]{:S(2)}, u32[]{:S(2)}) %all-to-all-start.1) | async-done | bytes 1048608 | tf_op jit(solution)/shard_map/all_to_all | solution.py:17
  97.0 3.5 %shard_map.111 = (bf16[16,256,128]{2,1,0:T(8,128)(2,1)}, bf16[16,128,256]{2,1,0:T(8,128)(2,1)}) custom-call(bf16[16,256,128]{2,1,0:T(8,128)(2,1)} %bitcast.135, bf16[16,256,128]{2,1,0:T(8,128)(2,1)} %bitcast.10.mixed_ref, f32[1,128]{1,0:T(1,128)} %bitcast.152, f32[1,128]{1,0:T(1,128)} %bitcast.154, bf16[128,128]{1,0:T(8,128)(2,1)} %mul.23.panel_ref), custom_call_target="tpu_custom_call" | custom-call | tf_op jit(solution)/shard_map/pallas_call | solution.py:157
  100.5 8.6 %all-to-all-start.2 = ((bf16[16,128,256]{2,1,0:T(8,128)(2,1)}), bf16[16,128,256]{2,1,0:T(8,128)(2,1)}, u32[]{:S(2)}, u32[]{:S(2)}) async-start(bf16[16,128,256]{2,1,0:T(8,128)(2,1)} %get-tuple-element.28), calls=%async_computation.2 | async-start | bytes 2097152 | tf_op jit(solution)/shard_map/all_to_all | solution.py:17
  115.1 8.9 %collective-permute-done.1 = bf16[2,1,2,128,256]{3,4,2,1,0:T(8,128)(2,1)S(1)} collective-permute-done((bf16[2,1,2,128,256]{3,4,2,1,0:T(8,128)(2,1)S(1)}, bf16[2,1,2,128,256]{3,4,2,1,0:T(8,128)(2,1)S(1)}, u32[]{:S(2)}, u32[]{:S(2)}) %collective-permute-start.1) | collective-permute-done | bytes 262176 | tf_op jit(solution)/shard_map/ppermute | solution.py:29
  124.1 7.8 %collective-permute-done.2 = bf16[2,1,2,128,256]{3,4,2,1,0:T(8,128)(2,1)S(1)} collective-permute-done((bf16[2,1,2,128,256]{3,4,2,1,0:T(8,128)(2,1)S(1)}, bf16[2,1,2,128,256]{3,4,2,1,0:T(8,128)(2,1)S(1)}, u32[]{:S(2)}, u32[]{:S(2)}) %collective-permute-start.2) | collective-permute-done | bytes 262176 | tf_op jit(solution)/shard_map/ppermute | solution.py:29
  132.8 9.1 %collective-permute-start.9 = (bf16[4,2,32,128]{3,2,1,0:T(8,128)(2,1)S(1)}, bf16[4,2,32,128]{3,2,1,0:T(8,128)(2,1)S(1)}, u32[]{:S(2)}, u32[]{:S(2)}) collective-permute-start(bf16[4,2,32,128]{3,2,1,0:T(8,128)(2,1)S(1)} %bitcast_dynamic-update-slice_fusion.2), channel_id=1, source_target_pairs={{0,8},{8,0},{1,9},{9,1},{2,10},{10,2},{3,11},{11,3},{4,12},{12,4},... | collective-permute-start | bytes 196616 | tf_op jit(solution)/shard_map/ppermute | solution.py:46
  141.9 4.0 %collective-permute-done.9 = bf16[4,2,32,128]{3,2,1,0:T(8,128)(2,1)S(1)} collective-permute-done((bf16[4,2,32,128]{3,2,1,0:T(8,128)(2,1)S(1)}, bf16[4,2,32,128]{3,2,1,0:T(8,128)(2,1)S(1)}, u32[]{:S(2)}, u32[]{:S(2)}) %collective-permute-start.9) | collective-permute-done | bytes 65568 | tf_op jit(solution)/shard_map/ppermute | solution.py:46
  152.1 4.6 %mix_features.1 = (bf16[32,64,256]{2,1,0:T(8,128)(2,1)}, bf16[32,64,256]{2,1,0:T(8,128)(2,1)}) custom-call(bf16[32,64,256]{2,1,0:T(8,128)(2,1)} %bitcast.13.inner_ref, bf16[32,64,256]{2,1,0:T(8,128)(2,1)} %bitcast.140, bf16[32,64,32]{2,1,0:T(8,128)(2,1)} %bitcast.144), custom_call_target="tpu_custom_call" | custom-call | tf_op jit(solution)/shard_map/mix_features/pallas_call | solution.py:104
  156.7 39.2 %all_to_all.36.d_ref = bf16[16,128,256]{2,1,0:T(8,128)(2,1)} all-to-all(bf16[16,128,256]{2,1,0:T(8,128)(2,1)} %bitcast.149), channel_id=1, replica_groups=mesh['zl'=4,'x'=4,'zh'=2,'y'=4,'c'=2] {'zh','y','c'}, dimensions={0} | all-to-all | bytes 2097152 | tf_op jit(solution)/shard_map/all_to_all | solution.py:17
  195.9 4.2 %shard_map.112 = (bf16[16,256,128]{2,1,0:T(8,128)(2,1)}, bf16[16,256,128]{2,1,0:T(8,128)(2,1)}) custom-call(bf16[16,256,128]{2,1,0:T(8,128)(2,1)} %bitcast.136, bf16[16,256,128]{2,1,0:T(8,128)(2,1)} %bitcast.10.mixed_ref, f32[1,128]{1,0:T(1,128)} %bitcast.153, f32[1,128]{1,0:T(1,128)} %bitcast.155, bf16[128,128]{1,0:T(8,128)(2,1)} %mul.23.panel_ref, ...), custom_call_target="tpu_custom_call" | custom-call | tf_op jit(solution)/shard_map/pallas_call | solution.py:157
  200.2 5.5 %all-to-all-start.4 = ((bf16[16,32,8,128]{3,2,1,0:T(8,128)(2,1)}), bf16[16,32,8,128]{3,2,1,0:T(8,128)(2,1)S(1)}, u32[]{:S(2)}, u32[]{:S(2)}) async-start(bf16[16,32,8,128]{3,2,1,0:T(8,128)(2,1)} %bitcast.147), calls=%async_computation.4 | async-start | bytes 2097152 | tf_op jit(solution)/shard_map/all_to_all | solution.py:17
  217.0 4.2 %collective-permute-done.16 = bf16[1,2,512,128]{3,2,1,0:T(8,128)(2,1)} collective-permute-done((bf16[1,2,512,128]{3,2,1,0:T(8,128)(2,1)}, bf16[1,2,512,128]{3,2,1,0:T(8,128)(2,1)}, u32[]{:S(2)}, u32[]{:S(2)}) %collective-permute-start.16) | collective-permute-done | bytes 262176 | tf_op jit(solution)/shard_map/ppermute | solution.py:29
  223.5 30.6 %all-to-all-done.4 = bf16[16,32,8,128]{3,2,1,0:T(8,128)(2,1)S(1)} async-done(((bf16[16,32,8,128]{3,2,1,0:T(8,128)(2,1)}), bf16[16,32,8,128]{3,2,1,0:T(8,128)(2,1)S(1)}, u32[]{:S(2)}, u32[]{:S(2)}) %all-to-all-start.4) | async-done | bytes 1048608 | tf_op jit(solution)/shard_map/all_to_all | solution.py:17
  258.3 7.9 %all-to-all-start.5 = ((bf16[128,32,128]{2,1,0:T(8,128)(2,1)}), bf16[128,32,128]{2,1,0:T(8,128)(2,1)}, u32[]{:S(2)}, u32[]{:S(2)}) async-start(bf16[128,32,128]{2,1,0:T(8,128)(2,1)} %copy.54), calls=%async_computation.5 | async-start | bytes 2097152 | tf_op jit(solution)/shard_map/all_to_all | solution.py:17
  278.9 5.6 %collective-permute-done.11 = bf16[2,1,2,128,256]{4,3,2,1,0:T(8,128)(2,1)S(1)} collective-permute-done((bf16[2,1,2,128,256]{4,3,2,1,0:T(8,128)(2,1)S(1)}, bf16[2,1,2,128,256]{4,3,2,1,0:T(8,128)(2,1)S(1)}, u32[]{:S(2)}, u32[]{:S(2)}) %collective-permute-start.11) | collective-permute-done | bytes 262176 | tf_op jit(solution)/shard_map/ppermute | solution.py:29
  284.6 9.7 %collective-permute-done.12 = bf16[2,1,2,128,256]{4,3,2,1,0:T(8,128)(2,1)S(1)} collective-permute-done((bf16[2,1,2,128,256]{4,3,2,1,0:T(8,128)(2,1)S(1)}, bf16[2,1,2,128,256]{4,3,2,1,0:T(8,128)(2,1)S(1)}, u32[]{:S(2)}, u32[]{:S(2)}) %collective-permute-start.12) | collective-permute-done | bytes 262176 | tf_op jit(solution)/shard_map/ppermute | solution.py:29
  308.2 5.1 %close.1 = (bf16[512,512]{1,0:T(8,128)(2,1)}, bf16[2,512,128]{2,1,0:T(8,128)(2,1)}, bf16[2,512,128]{2,1,0:T(8,128)(2,1)}, bf16[2,512,128]{2,1,0:T(8,128)(2,1)}, bf16[2,512,128]{2,1,0:T(8,128)(2,1)}) custom-call(s32[2]{0:T(128)} %pad_add_fusion.at_ref, bf16[16,8,32,128]{3,2,1,0:T(8,128)(2,1)} %bitcast.45.d_ref, ...), custom_call_target="tpu_custom_call" | custom-call | tf_op jit(solution)/shard_map/close/pallas_call | solution.py:210
  319.3 7.4 %all-to-all-start.6 = ((bf16[16,32,512]{2,1,0:T(8,128)(2,1)}), bf16[16,32,512]{2,1,0:T(8,128)(2,1)}, u32[]{:S(2)}, u32[]{:S(2)}) async-start(bf16[16,32,512]{2,1,0:T(8,128)(2,1)} %bitcast.151), calls=%async_computation.6 | async-start | bytes 1048576 | tf_op jit(solution)/shard_map/all_to_all | solution.py:17
  335.6 3.3 finish.1
  338.9 8.2 %all-to-all-done.6 = bf16[16,32,512]{2,1,0:T(8,128)(2,1)} async-done(((bf16[16,32,512]{2,1,0:T(8,128)(2,1)}), bf16[16,32,512]{2,1,0:T(8,128)(2,1)}, u32[]{:S(2)}, u32[]{:S(2)}) %all-to-all-start.6) | async-done | bytes 524320 | tf_op jit(solution)/shard_map/all_to_all | solution.py:17
  (150 shorter events, 90.3 us)
Async XLA Ops:
  44.4 52.6 %all-to-all-start.1 = ((bf16[16,32,8,128]{3,2,1,0:T(8,128)(2,1)}), bf16[16,32,8,128]{3,2,1,0:T(8,128)(2,1)}, u32[]{:S(2)}, u32[]{:S(2)}) async-start(bf16[16,32,8,128]{3,2,1,0:T(8,128)(2,1)} %bitcast.126), calls=%async_computation.1 | async-start | bytes 2097152 | tf_op jit(solution)/shard_map/all_to_all | solution.py:17
  52.3 56.7 %collective-permute-start = (bf16[1,4,2,128,256]{3,4,2,1,0:T(8,128)(2,1)}, bf16[1,4,2,128,256]{3,4,2,1,0:T(8,128)(2,1)}, u32[]{:S(2)}, u32[]{:S(2)}) collective-permute-start(bf16[1,4,2,128,256]{3,4,2,1,0:T(8,128)(2,1)} %constant_dynamic-slice_fusion.15), channel_id=1, source_target_pairs={{0,8},{8,0},{1,9},{9,1},{2,10},{10,2},{3,11},{11,3},{4,12},{12,4},... | collective-permute-start | bytes 1572872 | tf_op jit(solution)/shard_map/ppermute | solution.py:29
  60.6 51.7 %collective-permute-start.6 = (bf16[2,32,128]{2,1,0:T(8,128)(2,1)S(1)}, bf16[2,32,128]{2,1,0:T(8,128)(2,1)S(1)}, u32[]{:S(2)}, u32[]{:S(2)}) collective-permute-start(bf16[2,32,128]{2,1,0:T(8,128)(2,1)S(1)} %constant_dynamic-update-slice_fusion.9), channel_id=1, source_target_pairs={{0,2},{2,0},{4,6},{6,4},{1,3},{3,1},{5,7},{7,5},{8,10},{10,8},{12,... | collective-permute-start | bytes 49160 | tf_op jit(solution)/shard_map/ppermute | solution.py:46
  62.2 53.0 %collective-permute-start.7 = (bf16[2,32,128]{2,1,0:T(8,128)(2,1)S(1)}, bf16[2,32,128]{2,1,0:T(8,128)(2,1)S(1)}, u32[]{:S(2)}, u32[]{:S(2)}) collective-permute-start(bf16[2,32,128]{2,1,0:T(8,128)(2,1)S(1)} %constant_dynamic-update-slice_fusion.9), channel_id=1, source_target_pairs={{0,4},{2,6},{4,0},{6,2},{1,5},{3,7},{5,1},{7,3},{8,12},{10,14},{12... | collective-permute-start | bytes 49160 | tf_op jit(solution)/shard_map/ppermute | solution.py:46
  65.1 67.7 %collective-permute-start.8 = (bf16[2,32,128]{2,1,0:T(8,128)(2,1)S(1)}, bf16[2,32,128]{2,1,0:T(8,128)(2,1)S(1)}, u32[]{:S(2)}, u32[]{:S(2)}) collective-permute-start(bf16[2,32,128]{2,1,0:T(8,128)(2,1)S(1)} %constant_dynamic-update-slice_fusion.9), channel_id=1, source_target_pairs={{0,6},{2,4},{4,2},{6,0},{1,7},{3,5},{5,3},{7,1},{8,14},{10,12},{12... | collective-permute-start | bytes 49160 | tf_op jit(solution)/shard_map/ppermute | solution.py:46
  100.5 51.6 %all-to-all-start.2 = ((bf16[16,128,256]{2,1,0:T(8,128)(2,1)}), bf16[16,128,256]{2,1,0:T(8,128)(2,1)}, u32[]{:S(2)}, u32[]{:S(2)}) async-start(bf16[16,128,256]{2,1,0:T(8,128)(2,1)} %get-tuple-element.28), calls=%async_computation.2 | async-start | bytes 2097152 | tf_op jit(solution)/shard_map/all_to_all | solution.py:17
  112.3 19.6 %collective-permute-start.2 = (bf16[2,1,2,128,256]{3,4,2,1,0:T(8,128)(2,1)S(1)}, bf16[2,1,2,128,256]{3,4,2,1,0:T(8,128)(2,1)S(1)}, u32[]{:S(2)}, u32[]{:S(2)}) collective-permute-start(bf16[2,1,2,128,256]{3,4,2,1,0:T(8,128)(2,1)S(1)} %get-tuple-element.30), channel_id=1, source_target_pairs={{0,4},{2,6},{4,0},{6,2},{1,5},{3,7},{5,1},{7,3},{8,12},{10,14},{12... | collective-permute-start | bytes 786440 | tf_op jit(solution)/shard_map/ppermute | solution.py:29
  114.9 17.0 %collective-permute-start.3 = (bf16[2,1,2,128,256]{3,4,2,1,0:T(8,128)(2,1)S(1)}, bf16[2,1,2,128,256]{3,4,2,1,0:T(8,128)(2,1)S(1)}, u32[]{:S(2)}, u32[]{:S(2)}) collective-permute-start(bf16[2,1,2,128,256]{3,4,2,1,0:T(8,128)(2,1)S(1)} %get-tuple-element.31), channel_id=1, source_target_pairs={{0,6},{2,4},{4,2},{6,0},{1,7},{3,5},{5,3},{7,1},{8,14},{10,12},{12... | collective-permute-start | bytes 786440 | tf_op jit(solution)/shard_map/ppermute | solution.py:29
  132.8 16.9 %collective-permute-start.4 = (bf16[2,4,1,128,256]{3,4,2,1,0:T(8,128)(2,1)}, bf16[2,4,1,128,256]{3,4,2,1,0:T(8,128)(2,1)}, u32[]{:S(2)}, u32[]{:S(2)}) collective-permute-start(bf16[2,4,1,128,256]{3,4,2,1,0:T(8,128)(2,1)} %constant_dynamic-slice_fusion.11), channel_id=1, source_target_pairs={{0,1},{1,0},{2,3},{3,2},{4,5},{5,4},{6,7},{7,6},{8,9},{9,8},{10,11... | collective-permute-start | bytes 1572872 | tf_op jit(solution)/shard_map/ppermute | solution.py:29
  200.2 53.9 %all-to-all-start.4 = ((bf16[16,32,8,128]{3,2,1,0:T(8,128)(2,1)}), bf16[16,32,8,128]{3,2,1,0:T(8,128)(2,1)S(1)}, u32[]{:S(2)}, u32[]{:S(2)}) async-start(bf16[16,32,8,128]{3,2,1,0:T(8,128)(2,1)} %bitcast.147), calls=%async_computation.4 | async-start | bytes 2097152 | tf_op jit(solution)/shard_map/all_to_all | solution.py:17
  206.5 14.6 %collective-permute-start.16 = (bf16[1,2,512,128]{3,2,1,0:T(8,128)(2,1)}, bf16[1,2,512,128]{3,2,1,0:T(8,128)(2,1)}, u32[]{:S(2)}, u32[]{:S(2)}) collective-permute-start(bf16[1,2,512,128]{3,2,1,0:T(8,128)(2,1)} %get-tuple-element.39), channel_id=1, source_target_pairs={{0,4},{2,6},{4,0},{6,2},{1,5},{3,7},{5,1},{7,3},{8,12},{10,14},{12... | collective-permute-start | bytes 786440 | tf_op jit(solution)/shard_map/ppermute | solution.py:29
  209.3 56.9 %collective-permute-start.17 = (bf16[1,2,512,128]{3,2,1,0:T(8,128)(2,1)S(1)}, bf16[1,2,512,128]{3,2,1,0:T(8,128)(2,1)}, u32[]{:S(2)}, u32[]{:S(2)}) collective-permute-start(bf16[1,2,512,128]{3,2,1,0:T(8,128)(2,1)S(1)} %get-tuple-element.40), channel_id=1, source_target_pairs={{0,6},{2,4},{4,2},{6,0},{1,7},{3,5},{5,3},{7,1},{8,14},{10,12},{12... | collective-permute-start | bytes 786440 | tf_op jit(solution)/shard_map/ppermute | solution.py:29
  223.0 45.3 %collective-permute-start.10 = (bf16[1,4,2,128,256]{4,3,2,1,0:T(8,128)(2,1)}, bf16[1,4,2,128,256]{4,3,2,1,0:T(8,128)(2,1)}, u32[]{:S(2)}, u32[]{:S(2)}) collective-permute-start(bf16[1,4,2,128,256]{4,3,2,1,0:T(8,128)(2,1)} %constant_dynamic-slice_fusion.10), channel_id=1, source_target_pairs={{0,8},{8,0},{1,9},{9,1},{2,10},{10,2},{3,11},{11,3},{4,12},{12,4},... | collective-permute-start | bytes 1572872 | tf_op jit(solution)/shard_map/ppermute | solution.py:29
  258.3 50.0 %all-to-all-start.5 = ((bf16[128,32,128]{2,1,0:T(8,128)(2,1)}), bf16[128,32,128]{2,1,0:T(8,128)(2,1)}, u32[]{:S(2)}, u32[]{:S(2)}) async-start(bf16[128,32,128]{2,1,0:T(8,128)(2,1)} %copy.54), calls=%async_computation.5 | async-start | bytes 2097152 | tf_op jit(solution)/shard_map/all_to_all | solution.py:17
  268.1 35.8 %collective-permute-start.18 = (bf16[4,1,512,128]{3,2,1,0:T(8,128)(2,1)}, bf16[4,1,512,128]{3,2,1,0:T(8,128)(2,1)}, u32[]{:S(2)}, u32[]{:S(2)}) collective-permute-start(bf16[4,1,512,128]{3,2,1,0:T(8,128)(2,1)} %constant_dynamic-slice_fusion.2), channel_id=1, source_target_pairs={{0,1},{1,0},{2,3},{3,2},{4,5},{5,4},{6,7},{7,6},{8,9},{9,8},{10,11... | collective-permute-start | bytes 1572872 | tf_op jit(solution)/shard_map/ppermute | solution.py:29
  272.9 21.5 %collective-permute-start.12 = (bf16[2,1,2,128,256]{4,3,2,1,0:T(8,128)(2,1)S(1)}, bf16[2,1,2,128,256]{4,3,2,1,0:T(8,128)(2,1)S(1)}, u32[]{:S(2)}, u32[]{:S(2)}) collective-permute-start(bf16[2,1,2,128,256]{4,3,2,1,0:T(8,128)(2,1)S(1)} %get-tuple-element.34), channel_id=1, source_target_pairs={{0,4},{2,6},{4,0},{6,2},{1,5},{3,7},{5,1},{7,3},{8,12},{10,14},{12... | collective-permute-start | bytes 786440 | tf_op jit(solution)/shard_map/ppermute | solution.py:29
  275.6 20.1 %collective-permute-start.13 = (bf16[2,1,2,128,256]{4,3,2,1,0:T(8,128)(2,1)S(1)}, bf16[2,1,2,128,256]{4,3,2,1,0:T(8,128)(2,1)S(1)}, u32[]{:S(2)}, u32[]{:S(2)}) collective-permute-start(bf16[2,1,2,128,256]{4,3,2,1,0:T(8,128)(2,1)S(1)} %get-tuple-element.35), channel_id=1, source_target_pairs={{0,6},{2,4},{4,2},{6,0},{1,7},{3,5},{5,3},{7,1},{8,14},{10,12},{12... | collective-permute-start | bytes 786440 | tf_op jit(solution)/shard_map/ppermute | solution.py:29
  278.9 18.2 %collective-permute-start.23 = (bf16[4,1,2,32,8,128]{5,4,3,2,1,0:T(8,128)(2,1)}, bf16[4,1,2,32,8,128]{5,4,3,2,1,0:T(8,128)(2,1)}, u32[]{:S(2)}, u32[]{:S(2)}) collective-permute-start(bf16[4,1,2,32,8,128]{5,4,3,2,1,0:T(8,128)(2,1)} %copy.61), channel_id=1, source_target_pairs={{0,1},{1,0},{2,3},{3,2},{4,5},{5,4},{6,7},{7,6},{8,9},{9,8},{10,11... | collective-permute-start | bytes 1572872 | tf_op jit(solution)/shard_map/ppermute | solution.py:29
  299.3 14.1 %collective-permute-start.24 = (bf16[1,2,32,8,128]{4,3,2,1,0:T(8,128)(2,1)}, bf16[1,2,32,8,128]{4,3,2,1,0:T(8,128)(2,1)S(1)}, u32[]{:S(2)}, u32[]{:S(2)}) collective-permute-start(bf16[1,2,32,8,128]{4,3,2,1,0:T(8,128)(2,1)} %get-tuple-element.47), channel_id=1, source_target_pairs={{0,2},{2,0},{4,6},{6,4},{1,3},{3,1},{5,7},{7,5},{8,10},{10,8},{12,... | collective-permute-start | bytes 393224 | tf_op jit(solution)/shard_map/ppermute | solution.py:29
  299.3 14.1 %collective-permute-start.25 = (bf16[1,2,32,8,128]{4,3,2,1,0:T(8,128)(2,1)S(1)}, bf16[1,2,32,8,128]{4,3,2,1,0:T(8,128)(2,1)}, u32[]{:S(2)}, u32[]{:S(2)}) collective-permute-start(bf16[1,2,32,8,128]{4,3,2,1,0:T(8,128)(2,1)S(1)} %get-tuple-element.48), channel_id=1, source_target_pairs={{0,4},{2,6},{4,0},{6,2},{1,5},{3,7},{5,1},{7,3},{8,12},{10,14},{12... | collective-permute-start | bytes 393224 | tf_op jit(solution)/shard_map/ppermute | solution.py:29
  313.4 14.4 %collective-permute-start.20 = (bf16[2,512,128]{2,1,0:T(8,128)(2,1)}, bf16[2,512,128]{2,1,0:T(8,128)(2,1)}, u32[]{:S(2)}, u32[]{:S(2)}) collective-permute-start(bf16[2,512,128]{2,1,0:T(8,128)(2,1)} %get-tuple-element.43), channel_id=1, source_target_pairs={{0,4},{2,6},{4,0},{6,2},{1,5},{3,7},{5,1},{7,3},{8,12},{10,14},{12... | collective-permute-start | bytes 786440 | tf_op jit(solution)/shard_map/ppermute | solution.py:354
  314.7 14.0 %collective-permute-start.19 = (bf16[2,512,128]{2,1,0:T(8,128)(2,1)}, bf16[2,512,128]{2,1,0:T(8,128)(2,1)}, u32[]{:S(2)}, u32[]{:S(2)}) collective-permute-start(bf16[2,512,128]{2,1,0:T(8,128)(2,1)} %get-tuple-element.42), channel_id=1, source_target_pairs={{0,2},{2,0},{4,6},{6,4},{1,3},{3,1},{5,7},{7,5},{8,10},{10,8},{12,... | collective-permute-start | bytes 786440 | tf_op jit(solution)/shard_map/ppermute | solution.py:354
  316.5 17.6 %collective-permute-start.27 = (f32[1,32,8,128]{3,2,1,0:T(8,128)}, f32[1,32,8,128]{3,2,1,0:T(8,128)S(1)}, u32[]{:S(2)}, u32[]{:S(2)}) collective-permute-start(f32[1,32,8,128]{3,2,1,0:T(8,128)} %dynamic-slice_bitcast_fusion.1), channel_id=1, source_target_pairs={{0,8},{8,0},{1,9},{9,1},{2,10},{10,2},{3,11},{11,3},{4,12},{12,4},... | collective-permute-start | bytes 393224 | tf_op jit(solution)/shard_map/ppermute | solution.py:29
  319.3 27.8 %all-to-all-start.6 = ((bf16[16,32,512]{2,1,0:T(8,128)(2,1)}), bf16[16,32,512]{2,1,0:T(8,128)(2,1)}, u32[]{:S(2)}, u32[]{:S(2)}) async-start(bf16[16,32,512]{2,1,0:T(8,128)(2,1)} %bitcast.151), calls=%async_computation.6 | async-start | bytes 1048576 | tf_op jit(solution)/shard_map/all_to_all | solution.py:17
  (24 other events, 233.1 us)

commit v8 on v7

--- a/solution.py
+++ b/solution.py
@@ -277,6 +277,7 @@
     n_seq, n_hid = lax.axis_size(SEQ), lax.axis_size(HID)
     n_plane = lax.axis_size(PLANE)
     halves = n_hid // n_plane
+    zh = lax.axis_index("zh")
     rows, width = tokens.shape
     blocks, block = seq_first.shape[0], seq_first.shape[1]
     offs, nb = seq_second.shape[0], seq_second.shape[1]
@@ -344,7 +345,9 @@
     part = part.reshape((lax.axis_size("y"), lax.axis_size("c")) + part.shape[1:])
     part = fold(part, "c", 1).astype(BF16)
     part = fold(part, "y", 0)
-    second_grad = fold(part, "zh", 0)
+    keep = lax.dynamic_index_in_dim(part, zh, 0, keepdims=False)
+    send = lax.dynamic_index_in_dim(part, 1 - zh, 0, keepdims=False).astype(BF16)
+    second_grad = keep + lax.ppermute(send, "zh", [(0, 1), (1, 0)]).astype(F32)
 
     own = lax.dynamic_index_in_dim(seq_first, lax.axis_index(PLANE), 0, keepdims=False)
     at = jnp.stack([lax.axis_index("y"), lax.axis_index("c")]).astype(jnp.int32)

time: 351 us -> 350 us (level)
    ppermute x19 -> x18, waiting for transfers between devices: 40.4 us -> 41.2 us  [trade(): lax.ppermute(parts[r - 1], axis, [(s, s ^ r) for s in range(size)])]
    ppermute x19 -> x18, starting transfers between devices: 24.2 us -> 24.2 us  [trade(): lax.ppermute(parts[r - 1], axis, [(s, s ^ r) for s in range(size)])]
where the time goes in v8:
time: 350 us; the launch traced here: 349 us
  waiting for transfers between devices  116 us (33%)
  starting transfers between devices  77 us (22%)
  blocking collectives  73.5 us (21%)
  local copies, waits for them, and re-layouts  46.6 us (13%)
  Pallas kernels  20.9 us (6%)
  matrix products  7.5 us (2%)
  other arithmetic  6.36 us (2%)
    all_to_all x2, blocking collectives, move(): return lax.all_to_all(value, axes, split_axis=0, concat_axis=0, tiled=True)  73.5 us
    all_to_all x5, waiting for transfers between devices, move(): return lax.all_to_all(value, axes, split_axis=0, concat_axis=0, tiled=True)  70.5 us
    ppermute x18, waiting for transfers between devices, trade(): lax.ppermute(parts[r - 1], axis, [(s, s ^ r) for s in range(size)])  41.2 us
    all_to_all x5, starting transfers between devices, move(): return lax.all_to_all(value, axes, split_axis=0, concat_axis=0, tiled=True)  34.3 us
    ppermute x18, starting transfers between devices, trade(): lax.ppermute(parts[r - 1], axis, [(s, s ^ r) for s in range(size)])  24.2 us
    ppermute x5, starting transfers between devices, gather(): other = lax.ppermute(value, axis, [(s, s ^ r) for s in range(size)])  13.8 us
    dynamic_update_slice x15, local copies, waits for them, and re-layouts, turn(): value = lax.dynamic_update_slice_in_dim(value, got[r - 1], me ^ r, dim)  11.2 us
    dynamic_slice x10, local copies, waits for them, and re-layouts, trade(): lax.dynamic_index_in_dim(value, me ^ r, dim, keepdims=True)  7.97 us
  transfers between devices with their start and end apart: 33, of which 11 were waited for; matrix products, arithmetic and copies ran while one was open for 14% of the time, Pallas kernels for 3%

profile of v8, /device:TPU:32, one launch (start us, length us, event | category | flops | bytes accessed | tf_op | source)
XLA Modules:
  0.0 348.6 jit_solution(1898734969056854489)
XLA Ops:
  2.0 4.7 %fusion.1 = bf16[512,8,128]{0,2,1:T(8,128)(2,1)} fusion(bf16[8,512,128]{2,1,0:T(8,128)(2,1)S(1)} %bitcast.122, bf16[8,512,512]{2,1,0:T(8,128)(2,1)} %param.10), kind=kOutput, calls=%fused_computation.6 | convolution fusion | flops 537395200 | bytes 6291456 | tf_op jit(solution)/shard_map/qkj,qjc->kqc/dot_general | solution.py:68
  8.4 34.3 %all_to_all.35 = bf16[16,32,8,128]{3,2,1,0:T(8,128)(2,1)S(1)} all-to-all(bf16[16,32,8,128]{3,2,1,0:T(8,128)(2,1)S(1)} %bitcast.138), channel_id=1, replica_groups=mesh['zl'=4,'x'=4,'zh'=2,'y'=4,'c'=2] {'zl','x'}, dimensions={0} | all-to-all | bytes 2097152 | tf_op jit(solution)/shard_map/all_to_all | solution.py:17
  44.4 5.1 %all-to-all-start.1 = ((bf16[16,32,8,128]{3,2,1,0:T(8,128)(2,1)}), bf16[16,32,8,128]{3,2,1,0:T(8,128)(2,1)}, u32[]{:S(2)}, u32[]{:S(2)}) async-start(bf16[16,32,8,128]{3,2,1,0:T(8,128)(2,1)} %bitcast.121), calls=%async_computation.1 | async-start | bytes 2097152 | tf_op jit(solution)/shard_map/all_to_all | solution.py:17
  52.3 4.5 %collective-permute-start = (bf16[1,4,2,128,256]{3,4,2,1,0:T(8,128)(2,1)}, bf16[1,4,2,128,256]{3,4,2,1,0:T(8,128)(2,1)}, u32[]{:S(2)}, u32[]{:S(2)}) collective-permute-start(bf16[1,4,2,128,256]{3,4,2,1,0:T(8,128)(2,1)} %constant_dynamic-slice_fusion.14), channel_id=1, source_target_pairs={{0,8},{8,0},{1,9},{9,1},{2,10},{10,2},{3,11},{11,3},{4,12},{12,4},... | collective-permute-start | bytes 1572872 | tf_op jit(solution)/shard_map/ppermute | solution.py:29
  65.3 31.7 %all-to-all-done.1 = bf16[16,32,8,128]{3,2,1,0:T(8,128)(2,1)} async-done(((bf16[16,32,8,128]{3,2,1,0:T(8,128)(2,1)}), bf16[16,32,8,128]{3,2,1,0:T(8,128)(2,1)}, u32[]{:S(2)}, u32[]{:S(2)}) %all-to-all-start.1) | async-done | bytes 1048608 | tf_op jit(solution)/shard_map/all_to_all | solution.py:17
  97.0 3.5 %shard_map.111 = (bf16[16,256,128]{2,1,0:T(8,128)(2,1)}, bf16[16,128,256]{2,1,0:T(8,128)(2,1)}) custom-call(bf16[16,256,128]{2,1,0:T(8,128)(2,1)} %bitcast.130, bf16[16,256,128]{2,1,0:T(8,128)(2,1)} %bitcast.10.mixed_ref, f32[1,128]{1,0:T(1,128)} %bitcast.149, f32[1,128]{1,0:T(1,128)} %bitcast.151, bf16[128,128]{1,0:T(8,128)(2,1)} %mul.23.panel_ref), custom_call_target="tpu_custom_call" | custom-call | tf_op jit(solution)/shard_map/pallas_call | solution.py:157
  100.5 8.6 %all-to-all-start.2 = ((bf16[16,128,256]{2,1,0:T(8,128)(2,1)}), bf16[16,128,256]{2,1,0:T(8,128)(2,1)}, u32[]{:S(2)}, u32[]{:S(2)}) async-start(bf16[16,128,256]{2,1,0:T(8,128)(2,1)} %get-tuple-element.28), calls=%async_computation.2 | async-start | bytes 2097152 | tf_op jit(solution)/shard_map/all_to_all | solution.py:17
  115.1 8.9 %collective-permute-done.1 = bf16[2,1,2,128,256]{3,4,2,1,0:T(8,128)(2,1)S(1)} collective-permute-done((bf16[2,1,2,128,256]{3,4,2,1,0:T(8,128)(2,1)S(1)}, bf16[2,1,2,128,256]{3,4,2,1,0:T(8,128)(2,1)S(1)}, u32[]{:S(2)}, u32[]{:S(2)}) %collective-permute-start.1) | collective-permute-done | bytes 262176 | tf_op jit(solution)/shard_map/ppermute | solution.py:29
  124.1 7.8 %collective-permute-done.2 = bf16[2,1,2,128,256]{3,4,2,1,0:T(8,128)(2,1)S(1)} collective-permute-done((bf16[2,1,2,128,256]{3,4,2,1,0:T(8,128)(2,1)S(1)}, bf16[2,1,2,128,256]{3,4,2,1,0:T(8,128)(2,1)S(1)}, u32[]{:S(2)}, u32[]{:S(2)}) %collective-permute-start.2) | collective-permute-done | bytes 262176 | tf_op jit(solution)/shard_map/ppermute | solution.py:29
  132.8 9.1 %collective-permute-start.9 = (bf16[4,2,32,128]{3,2,1,0:T(8,128)(2,1)S(1)}, bf16[4,2,32,128]{3,2,1,0:T(8,128)(2,1)S(1)}, u32[]{:S(2)}, u32[]{:S(2)}) collective-permute-start(bf16[4,2,32,128]{3,2,1,0:T(8,128)(2,1)S(1)} %bitcast_dynamic-update-slice_fusion.2), channel_id=1, source_target_pairs={{0,8},{8,0},{1,9},{9,1},{2,10},{10,2},{3,11},{11,3},{4,12},{12,4},... | collective-permute-start | bytes 196616 | tf_op jit(solution)/shard_map/ppermute | solution.py:46
  141.9 4.0 %collective-permute-done.9 = bf16[4,2,32,128]{3,2,1,0:T(8,128)(2,1)S(1)} collective-permute-done((bf16[4,2,32,128]{3,2,1,0:T(8,128)(2,1)S(1)}, bf16[4,2,32,128]{3,2,1,0:T(8,128)(2,1)S(1)}, u32[]{:S(2)}, u32[]{:S(2)}) %collective-permute-start.9) | collective-permute-done | bytes 65568 | tf_op jit(solution)/shard_map/ppermute | solution.py:46
  152.1 4.6 %mix_features.1 = (bf16[32,64,256]{2,1,0:T(8,128)(2,1)}, bf16[32,64,256]{2,1,0:T(8,128)(2,1)}) custom-call(bf16[32,64,256]{2,1,0:T(8,128)(2,1)} %bitcast.13.inner_ref, bf16[32,64,256]{2,1,0:T(8,128)(2,1)} %bitcast.137, bf16[32,64,32]{2,1,0:T(8,128)(2,1)} %bitcast.141), custom_call_target="tpu_custom_call" | custom-call | tf_op jit(solution)/shard_map/mix_features/pallas_call | solution.py:104
  156.7 39.2 %all_to_all.36.d_ref = bf16[16,128,256]{2,1,0:T(8,128)(2,1)} all-to-all(bf16[16,128,256]{2,1,0:T(8,128)(2,1)} %bitcast.146), channel_id=1, replica_groups=mesh['zl'=4,'x'=4,'zh'=2,'y'=4,'c'=2] {'zh','y','c'}, dimensions={0} | all-to-all | bytes 2097152 | tf_op jit(solution)/shard_map/all_to_all | solution.py:17
  195.9 4.3 %shard_map.112 = (bf16[16,256,128]{2,1,0:T(8,128)(2,1)}, bf16[16,256,128]{2,1,0:T(8,128)(2,1)}) custom-call(bf16[16,256,128]{2,1,0:T(8,128)(2,1)} %bitcast.131, bf16[16,256,128]{2,1,0:T(8,128)(2,1)} %bitcast.10.mixed_ref, f32[1,128]{1,0:T(1,128)} %bitcast.150, f32[1,128]{1,0:T(1,128)} %bitcast.152, bf16[128,128]{1,0:T(8,128)(2,1)} %mul.23.panel_ref, ...), custom_call_target="tpu_custom_call" | custom-call | tf_op jit(solution)/shard_map/pallas_call | solution.py:157
  200.2 5.5 %all-to-all-start.4 = ((bf16[16,32,8,128]{3,2,1,0:T(8,128)(2,1)}), bf16[16,32,8,128]{3,2,1,0:T(8,128)(2,1)S(1)}, u32[]{:S(2)}, u32[]{:S(2)}) async-start(bf16[16,32,8,128]{3,2,1,0:T(8,128)(2,1)} %bitcast.144), calls=%async_computation.4 | async-start | bytes 2097152 | tf_op jit(solution)/shard_map/all_to_all | solution.py:17
  217.0 4.2 %collective-permute-done.16 = bf16[1,2,512,128]{3,2,1,0:T(8,128)(2,1)} collective-permute-done((bf16[1,2,512,128]{3,2,1,0:T(8,128)(2,1)}, bf16[1,2,512,128]{3,2,1,0:T(8,128)(2,1)}, u32[]{:S(2)}, u32[]{:S(2)}) %collective-permute-start.16) | collective-permute-done | bytes 262176 | tf_op jit(solution)/shard_map/ppermute | solution.py:29
  223.6 30.6 %all-to-all-done.4 = bf16[16,32,8,128]{3,2,1,0:T(8,128)(2,1)S(1)} async-done(((bf16[16,32,8,128]{3,2,1,0:T(8,128)(2,1)}), bf16[16,32,8,128]{3,2,1,0:T(8,128)(2,1)S(1)}, u32[]{:S(2)}, u32[]{:S(2)}) %all-to-all-start.4) | async-done | bytes 1048608 | tf_op jit(solution)/shard_map/all_to_all | solution.py:17
  258.3 7.9 %all-to-all-start.5 = ((bf16[128,32,128]{2,1,0:T(8,128)(2,1)}), bf16[128,32,128]{2,1,0:T(8,128)(2,1)}, u32[]{:S(2)}, u32[]{:S(2)}) async-start(bf16[128,32,128]{2,1,0:T(8,128)(2,1)} %copy.52), calls=%async_computation.5 | async-start | bytes 2097152 | tf_op jit(solution)/shard_map/all_to_all | solution.py:17
  278.2 6.4 %collective-permute-done.11 = bf16[2,1,2,128,256]{4,3,2,1,0:T(8,128)(2,1)S(1)} collective-permute-done((bf16[2,1,2,128,256]{4,3,2,1,0:T(8,128)(2,1)S(1)}, bf16[2,1,2,128,256]{4,3,2,1,0:T(8,128)(2,1)S(1)}, u32[]{:S(2)}, u32[]{:S(2)}) %collective-permute-start.11) | collective-permute-done | bytes 262176 | tf_op jit(solution)/shard_map/ppermute | solution.py:29
  284.6 9.8 %collective-permute-done.12 = bf16[2,1,2,128,256]{4,3,2,1,0:T(8,128)(2,1)S(1)} collective-permute-done((bf16[2,1,2,128,256]{4,3,2,1,0:T(8,128)(2,1)S(1)}, bf16[2,1,2,128,256]{4,3,2,1,0:T(8,128)(2,1)S(1)}, u32[]{:S(2)}, u32[]{:S(2)}) %collective-permute-start.12) | collective-permute-done | bytes 262176 | tf_op jit(solution)/shard_map/ppermute | solution.py:29
  308.3 5.1 %close.1 = (bf16[512,512]{1,0:T(8,128)(2,1)}, bf16[2,512,128]{2,1,0:T(8,128)(2,1)}, bf16[2,512,128]{2,1,0:T(8,128)(2,1)}, bf16[2,512,128]{2,1,0:T(8,128)(2,1)}, bf16[2,512,128]{2,1,0:T(8,128)(2,1)}) custom-call(s32[2]{0:T(128)} %pad_add_fusion.at_ref, bf16[16,8,32,128]{3,2,1,0:T(8,128)(2,1)} %bitcast.45.d_ref, ...), custom_call_target="tpu_custom_call" | custom-call | tf_op jit(solution)/shard_map/close/pallas_call | solution.py:210
  319.0 7.3 %all-to-all-start.6 = ((bf16[16,32,512]{2,1,0:T(8,128)(2,1)}), bf16[16,32,512]{2,1,0:T(8,128)(2,1)}, u32[]{:S(2)}, u32[]{:S(2)}) async-start(bf16[16,32,512]{2,1,0:T(8,128)(2,1)} %bitcast.148), calls=%async_computation.6 | async-start | bytes 1048576 | tf_op jit(solution)/shard_map/all_to_all | solution.py:17
  335.1 3.3 finish.1
  338.4 8.2 %all-to-all-done.6 = bf16[16,32,512]{2,1,0:T(8,128)(2,1)} async-done(((bf16[16,32,512]{2,1,0:T(8,128)(2,1)}), bf16[16,32,512]{2,1,0:T(8,128)(2,1)}, u32[]{:S(2)}, u32[]{:S(2)}) %all-to-all-start.6) | async-done | bytes 524320 | tf_op jit(solution)/shard_map/all_to_all | solution.py:17
  (152 shorter events, 89.1 us)
Async XLA Ops:
  44.4 52.6 %all-to-all-start.1 = ((bf16[16,32,8,128]{3,2,1,0:T(8,128)(2,1)}), bf16[16,32,8,128]{3,2,1,0:T(8,128)(2,1)}, u32[]{:S(2)}, u32[]{:S(2)}) async-start(bf16[16,32,8,128]{3,2,1,0:T(8,128)(2,1)} %bitcast.121), calls=%async_computation.1 | async-start | bytes 2097152 | tf_op jit(solution)/shard_map/all_to_all | solution.py:17
  52.3 56.7 %collective-permute-start = (bf16[1,4,2,128,256]{3,4,2,1,0:T(8,128)(2,1)}, bf16[1,4,2,128,256]{3,4,2,1,0:T(8,128)(2,1)}, u32[]{:S(2)}, u32[]{:S(2)}) collective-permute-start(bf16[1,4,2,128,256]{3,4,2,1,0:T(8,128)(2,1)} %constant_dynamic-slice_fusion.14), channel_id=1, source_target_pairs={{0,8},{8,0},{1,9},{9,1},{2,10},{10,2},{3,11},{11,3},{4,12},{12,4},... | collective-permute-start | bytes 1572872 | tf_op jit(solution)/shard_map/ppermute | solution.py:29
  60.6 51.7 %collective-permute-start.6 = (bf16[2,32,128]{2,1,0:T(8,128)(2,1)S(1)}, bf16[2,32,128]{2,1,0:T(8,128)(2,1)S(1)}, u32[]{:S(2)}, u32[]{:S(2)}) collective-permute-start(bf16[2,32,128]{2,1,0:T(8,128)(2,1)S(1)} %constant_dynamic-update-slice_fusion.9), channel_id=1, source_target_pairs={{0,2},{2,0},{4,6},{6,4},{1,3},{3,1},{5,7},{7,5},{8,10},{10,8},{12,... | collective-permute-start | bytes 49160 | tf_op jit(solution)/shard_map/ppermute | solution.py:46
  62.2 53.0 %collective-permute-start.7 = (bf16[2,32,128]{2,1,0:T(8,128)(2,1)S(1)}, bf16[2,32,128]{2,1,0:T(8,128)(2,1)S(1)}, u32[]{:S(2)}, u32[]{:S(2)}) collective-permute-start(bf16[2,32,128]{2,1,0:T(8,128)(2,1)S(1)} %constant_dynamic-update-slice_fusion.9), channel_id=1, source_target_pairs={{0,4},{2,6},{4,0},{6,2},{1,5},{3,7},{5,1},{7,3},{8,12},{10,14},{12... | collective-permute-start | bytes 49160 | tf_op jit(solution)/shard_map/ppermute | solution.py:46
  65.1 67.7 %collective-permute-start.8 = (bf16[2,32,128]{2,1,0:T(8,128)(2,1)S(1)}, bf16[2,32,128]{2,1,0:T(8,128)(2,1)S(1)}, u32[]{:S(2)}, u32[]{:S(2)}) collective-permute-start(bf16[2,32,128]{2,1,0:T(8,128)(2,1)S(1)} %constant_dynamic-update-slice_fusion.9), channel_id=1, source_target_pairs={{0,6},{2,4},{4,2},{6,0},{1,7},{3,5},{5,3},{7,1},{8,14},{10,12},{12... | collective-permute-start | bytes 49160 | tf_op jit(solution)/shard_map/ppermute | solution.py:46
  100.5 51.6 %all-to-all-start.2 = ((bf16[16,128,256]{2,1,0:T(8,128)(2,1)}), bf16[16,128,256]{2,1,0:T(8,128)(2,1)}, u32[]{:S(2)}, u32[]{:S(2)}) async-start(bf16[16,128,256]{2,1,0:T(8,128)(2,1)} %get-tuple-element.28), calls=%async_computation.2 | async-start | bytes 2097152 | tf_op jit(solution)/shard_map/all_to_all | solution.py:17
  110.3 13.8 %collective-permute-start.1 = (bf16[2,1,2,128,256]{3,4,2,1,0:T(8,128)(2,1)S(1)}, bf16[2,1,2,128,256]{3,4,2,1,0:T(8,128)(2,1)S(1)}, u32[]{:S(2)}, u32[]{:S(2)}) collective-permute-start(bf16[2,1,2,128,256]{3,4,2,1,0:T(8,128)(2,1)S(1)} %get-tuple-element.29), channel_id=1, source_target_pairs={{0,2},{2,0},{4,6},{6,4},{1,3},{3,1},{5,7},{7,5},{8,10},{10,8},{12,... | collective-permute-start | bytes 786440 | tf_op jit(solution)/shard_map/ppermute | solution.py:29
  112.3 19.6 %collective-permute-start.2 = (bf16[2,1,2,128,256]{3,4,2,1,0:T(8,128)(2,1)S(1)}, bf16[2,1,2,128,256]{3,4,2,1,0:T(8,128)(2,1)S(1)}, u32[]{:S(2)}, u32[]{:S(2)}) collective-permute-start(bf16[2,1,2,128,256]{3,4,2,1,0:T(8,128)(2,1)S(1)} %get-tuple-element.30), channel_id=1, source_target_pairs={{0,4},{2,6},{4,0},{6,2},{1,5},{3,7},{5,1},{7,3},{8,12},{10,14},{12... | collective-permute-start | bytes 786440 | tf_op jit(solution)/shard_map/ppermute | solution.py:29
  114.9 17.0 %collective-permute-start.3 = (bf16[2,1,2,128,256]{3,4,2,1,0:T(8,128)(2,1)S(1)}, bf16[2,1,2,128,256]{3,4,2,1,0:T(8,128)(2,1)S(1)}, u32[]{:S(2)}, u32[]{:S(2)}) collective-permute-start(bf16[2,1,2,128,256]{3,4,2,1,0:T(8,128)(2,1)S(1)} %get-tuple-element.31), channel_id=1, source_target_pairs={{0,6},{2,4},{4,2},{6,0},{1,7},{3,5},{5,3},{7,1},{8,14},{10,12},{12... | collective-permute-start | bytes 786440 | tf_op jit(solution)/shard_map/ppermute | solution.py:29
  132.8 16.9 %collective-permute-start.4 = (bf16[2,4,1,128,256]{3,4,2,1,0:T(8,128)(2,1)}, bf16[2,4,1,128,256]{3,4,2,1,0:T(8,128)(2,1)}, u32[]{:S(2)}, u32[]{:S(2)}) collective-permute-start(bf16[2,4,1,128,256]{3,4,2,1,0:T(8,128)(2,1)} %constant_dynamic-slice_fusion.10), channel_id=1, source_target_pairs={{0,1},{1,0},{2,3},{3,2},{4,5},{5,4},{6,7},{7,6},{8,9},{9,8},{10,11... | collective-permute-start | bytes 1572872 | tf_op jit(solution)/shard_map/ppermute | solution.py:29
  200.2 53.9 %all-to-all-start.4 = ((bf16[16,32,8,128]{3,2,1,0:T(8,128)(2,1)}), bf16[16,32,8,128]{3,2,1,0:T(8,128)(2,1)S(1)}, u32[]{:S(2)}, u32[]{:S(2)}) async-start(bf16[16,32,8,128]{3,2,1,0:T(8,128)(2,1)} %bitcast.144), calls=%async_computation.4 | async-start | bytes 2097152 | tf_op jit(solution)/shard_map/all_to_all | solution.py:17
  206.5 14.6 %collective-permute-start.16 = (bf16[1,2,512,128]{3,2,1,0:T(8,128)(2,1)}, bf16[1,2,512,128]{3,2,1,0:T(8,128)(2,1)}, u32[]{:S(2)}, u32[]{:S(2)}) collective-permute-start(bf16[1,2,512,128]{3,2,1,0:T(8,128)(2,1)} %get-tuple-element.39), channel_id=1, source_target_pairs={{0,4},{2,6},{4,0},{6,2},{1,5},{3,7},{5,1},{7,3},{8,12},{10,14},{12... | collective-permute-start | bytes 786440 | tf_op jit(solution)/shard_map/ppermute | solution.py:29
  209.4 56.8 %collective-permute-start.17 = (bf16[1,2,512,128]{3,2,1,0:T(8,128)(2,1)S(1)}, bf16[1,2,512,128]{3,2,1,0:T(8,128)(2,1)}, u32[]{:S(2)}, u32[]{:S(2)}) collective-permute-start(bf16[1,2,512,128]{3,2,1,0:T(8,128)(2,1)S(1)} %get-tuple-element.40), channel_id=1, source_target_pairs={{0,6},{2,4},{4,2},{6,0},{1,7},{3,5},{5,3},{7,1},{8,14},{10,12},{12... | collective-permute-start | bytes 786440 | tf_op jit(solution)/shard_map/ppermute | solution.py:29
  223.0 45.3 %collective-permute-start.10 = (bf16[1,4,2,128,256]{4,3,2,1,0:T(8,128)(2,1)}, bf16[1,4,2,128,256]{4,3,2,1,0:T(8,128)(2,1)}, u32[]{:S(2)}, u32[]{:S(2)}) collective-permute-start(bf16[1,4,2,128,256]{4,3,2,1,0:T(8,128)(2,1)} %constant_dynamic-slice_fusion.9), channel_id=1, source_target_pairs={{0,8},{8,0},{1,9},{9,1},{2,10},{10,2},{3,11},{11,3},{4,12},{12,4},... | collective-permute-start | bytes 1572872 | tf_op jit(solution)/shard_map/ppermute | solution.py:29
  258.3 50.0 %all-to-all-start.5 = ((bf16[128,32,128]{2,1,0:T(8,128)(2,1)}), bf16[128,32,128]{2,1,0:T(8,128)(2,1)}, u32[]{:S(2)}, u32[]{:S(2)}) async-start(bf16[128,32,128]{2,1,0:T(8,128)(2,1)} %copy.52), calls=%async_computation.5 | async-start | bytes 2097152 | tf_op jit(solution)/shard_map/all_to_all | solution.py:17
  268.2 35.9 %collective-permute-start.18 = (bf16[4,1,512,128]{3,2,1,0:T(8,128)(2,1)}, bf16[4,1,512,128]{3,2,1,0:T(8,128)(2,1)}, u32[]{:S(2)}, u32[]{:S(2)}) collective-permute-start(bf16[4,1,512,128]{3,2,1,0:T(8,128)(2,1)} %constant_dynamic-slice_fusion.1), channel_id=1, source_target_pairs={{0,1},{1,0},{2,3},{3,2},{4,5},{5,4},{6,7},{7,6},{8,9},{9,8},{10,11... | collective-permute-start | bytes 1572872 | tf_op jit(solution)/shard_map/ppermute | solution.py:29
  272.9 21.5 %collective-permute-start.12 = (bf16[2,1,2,128,256]{4,3,2,1,0:T(8,128)(2,1)S(1)}, bf16[2,1,2,128,256]{4,3,2,1,0:T(8,128)(2,1)S(1)}, u32[]{:S(2)}, u32[]{:S(2)}) collective-permute-start(bf16[2,1,2,128,256]{4,3,2,1,0:T(8,128)(2,1)S(1)} %get-tuple-element.34), channel_id=1, source_target_pairs={{0,4},{2,6},{4,0},{6,2},{1,5},{3,7},{5,1},{7,3},{8,12},{10,14},{12... | collective-permute-start | bytes 786440 | tf_op jit(solution)/shard_map/ppermute | solution.py:29
  275.6 20.1 %collective-permute-start.13 = (bf16[2,1,2,128,256]{4,3,2,1,0:T(8,128)(2,1)S(1)}, bf16[2,1,2,128,256]{4,3,2,1,0:T(8,128)(2,1)S(1)}, u32[]{:S(2)}, u32[]{:S(2)}) collective-permute-start(bf16[2,1,2,128,256]{4,3,2,1,0:T(8,128)(2,1)S(1)} %get-tuple-element.35), channel_id=1, source_target_pairs={{0,6},{2,4},{4,2},{6,0},{1,7},{3,5},{5,3},{7,1},{8,14},{10,12},{12... | collective-permute-start | bytes 786440 | tf_op jit(solution)/shard_map/ppermute | solution.py:29
  278.2 19.1 %collective-permute-start.23 = (bf16[4,1,2,32,8,128]{5,4,3,2,1,0:T(8,128)(2,1)}, bf16[4,1,2,32,8,128]{5,4,3,2,1,0:T(8,128)(2,1)}, u32[]{:S(2)}, u32[]{:S(2)}) collective-permute-start(bf16[4,1,2,32,8,128]{5,4,3,2,1,0:T(8,128)(2,1)} %constant_dynamic-slice_fusion), channel_id=1, source_target_pairs={{0,1},{1,0},{2,3},{3,2},{4,5},{5,4},{6,7},{7,6},{8,9},{9,8},{10,11... | collective-permute-start | bytes 1572872 | tf_op jit(solution)/shard_map/ppermute | solution.py:29
  299.4 14.1 %collective-permute-start.24 = (bf16[1,2,32,8,128]{4,3,2,1,0:T(8,128)(2,1)}, bf16[1,2,32,8,128]{4,3,2,1,0:T(8,128)(2,1)S(1)}, u32[]{:S(2)}, u32[]{:S(2)}) collective-permute-start(bf16[1,2,32,8,128]{4,3,2,1,0:T(8,128)(2,1)} %get-tuple-element.47), channel_id=1, source_target_pairs={{0,2},{2,0},{4,6},{6,4},{1,3},{3,1},{5,7},{7,5},{8,10},{10,8},{12,... | collective-permute-start | bytes 393224 | tf_op jit(solution)/shard_map/ppermute | solution.py:29
  299.4 14.1 %collective-permute-start.25 = (bf16[1,2,32,8,128]{4,3,2,1,0:T(8,128)(2,1)S(1)}, bf16[1,2,32,8,128]{4,3,2,1,0:T(8,128)(2,1)}, u32[]{:S(2)}, u32[]{:S(2)}) collective-permute-start(bf16[1,2,32,8,128]{4,3,2,1,0:T(8,128)(2,1)S(1)} %get-tuple-element.48), channel_id=1, source_target_pairs={{0,4},{2,6},{4,0},{6,2},{1,5},{3,7},{5,1},{7,3},{8,12},{10,14},{12... | collective-permute-start | bytes 393224 | tf_op jit(solution)/shard_map/ppermute | solution.py:29
  313.5 13.8 %collective-permute-start.20 = (bf16[2,512,128]{2,1,0:T(8,128)(2,1)}, bf16[2,512,128]{2,1,0:T(8,128)(2,1)}, u32[]{:S(2)}, u32[]{:S(2)}) collective-permute-start(bf16[2,512,128]{2,1,0:T(8,128)(2,1)} %get-tuple-element.43), channel_id=1, source_target_pairs={{0,4},{2,6},{4,0},{6,2},{1,5},{3,7},{5,1},{7,3},{8,12},{10,14},{12... | collective-permute-start | bytes 786440 | tf_op jit(solution)/shard_map/ppermute | solution.py:357
  315.9 17.7 %collective-permute-start.27 = (bf16[32,8,128]{2,1,0:T(8,128)(2,1)S(1)}, bf16[32,8,128]{2,1,0:T(8,128)(2,1)S(1)}, u32[]{:S(2)}, u32[]{:S(2)}) collective-permute-start(bf16[32,8,128]{2,1,0:T(8,128)(2,1)S(1)} %fusion.14), channel_id=1, source_target_pairs={{0,8},{8,0},{1,9},{9,1},{2,10},{10,2},{3,11},{11,3},{4,12},{12,4},... | collective-permute-start | bytes 196616 | tf_op jit(solution)/shard_map/ppermute | solution.py:350
  319.0 27.7 %all-to-all-start.6 = ((bf16[16,32,512]{2,1,0:T(8,128)(2,1)}), bf16[16,32,512]{2,1,0:T(8,128)(2,1)}, u32[]{:S(2)}, u32[]{:S(2)}) async-start(bf16[16,32,512]{2,1,0:T(8,128)(2,1)} %bitcast.148), calls=%async_computation.6 | async-start | bytes 1048576 | tf_op jit(solution)/shard_map/all_to_all | solution.py:17
  (25 other events, 250.7 us)
